TPU v7x, 256 devices: a whole 4x4x8 slice. The times are simulated.
256 devices in a mesh: seq: 32 (over y_lo, z, core), fsdp: 8 (over x, y_hi).
Axes of the slice: x: 4, y: 4 (y_hi: 2, y_lo: 2; y = y_hi * 2 + y_lo), z: 8, core: 2. Of those that a mesh axis runs over, the one named last changes fastest.
Arguments:
- tokens: float32 [1, 12288, 3072], P(None, 'seq', 'fsdp'), may hold values from -6 to 6
- block_mask: int32 [16, 6, 6], replicated, may hold values from 0 to 1, as said below
- space_qkv: bfloat16 [3072, 3, 2048], P(None, None, 'fsdp'), may hold values from -0.109375 to 0.109375
- space_out: bfloat16 [2048, 3072], P('fsdp'), may hold values from -0.1875 to 0.1875
- space_mod: float32 [3, 3072], replicated, may hold values from -2 to 3
- time_qkv: bfloat16 [3072, 3, 2048], P(None, None, 'fsdp'), may hold values from -0.109375 to 0.109375
- time_out: bfloat16 [2048, 3072], P('fsdp'), may hold values from -0.1875 to 0.1875
- time_mod: float32 [3, 3072], replicated, may hold values from -2 to 3
Outputs:
- result: float32 [1, 12288, 3072], P(None, 'seq', 'fsdp')
Inputs may be any that keep to these rules, and one draw needn't show every extreme that they name: block_mask[f, i, i] = 1 for every frame f and block i.
All inputs are finite; a program needn't handle non-finite values.
Results may differ from a plain program's by a relative error of at most 0.015.
Values may be sent and summed in bfloat16 or wider, within the bound.
No kernel may reach another device: no remote copies, remote signals or barrier semaphores. Data moves between devices by JAX's collectives and lax.ppermute only.
A program may use at most 128 MiB of HBM per device.

v0:
```python
import math

import jax
import jax.numpy as jnp
from jax import lax
from jax.sharding import PartitionSpec as P

HD = 128
BLOCK = 128


EPS = 1e-06


def from_partner(shard, axis, distance):
    return lax.ppermute(shard, axis, [(i, i ^ 1 << distance) for i in range(lax.axis_size(axis))])


def modulate(stream, modulation):
    centre = jnp.mean(stream, axis=-1, keepdims=True)
    centred = stream - centre
    variance = jnp.mean(centred * centred, axis=-1, keepdims=True)
    normed = centred * lax.rsqrt(variance + EPS)
    return (normed * (1.0 + modulation[1]) + modulation[0]).astype(jnp.bfloat16)


def softmax_rounded(scores, reduce_axis):
    row_max = jnp.max(scores, axis=reduce_axis, keepdims=True)
    lifted = jnp.exp(scores - row_max)
    return (lifted / jnp.sum(lifted, axis=reduce_axis, keepdims=True)).astype(jnp.bfloat16)


def widen(shard):
    return lax.all_gather(shard, "fsdp", axis=2, tiled=True)


def head_total(partial_value):
    return lax.psum_scatter(
        partial_value.astype(jnp.bfloat16), "fsdp", scatter_dimension=2, tiled=True
    ).astype(jnp.float32)


def project_inputs(normed, qkv_weight):
    model_width = qkv_weight.shape[0]
    flat_rows = normed.reshape(-1, model_width)
    return jnp.dot(
        flat_rows, qkv_weight.reshape(model_width, -1), preferred_element_type=jnp.float32
    ).astype(jnp.bfloat16)


def on_device(tokens, block_mask, space_qkv, space_out, space_mod, time_qkv, time_out, time_mod):
    videos, row_count, part_width = tokens.shape
    model_width = space_qkv.shape[0]
    heads_width = space_qkv.shape[2]
    local_heads = heads_width // HD
    seq_count = lax.axis_size("seq")
    piece_rows = row_count // seq_count
    frame_count = seq_count // 2
    seq_index = lax.axis_index("seq")
    half_index = seq_index % 2
    frame_index = seq_index // 2
    feature_start = lax.axis_index("fsdp") * part_width
    score_scale = 1.0 / math.sqrt(HD)
    query_blocks = row_count // BLOCK
    key_blocks = 2 * query_blocks
    full_tokens = widen(tokens)
    packed = project_inputs(modulate(full_tokens, space_mod), space_qkv)
    packed = packed.reshape(videos, row_count, 3, local_heads, HD)
    queries = packed[:, :, 0]
    keys_values = packed[:, :, 1:]
    partner = from_partner(keys_values, "seq", 0)
    all_keys = jnp.where(
        half_index == 0,
        jnp.concatenate([keys_values, partner], axis=1),
        jnp.concatenate([partner, keys_values], axis=1),
    )
    zero_index = jnp.zeros((), jnp.int32)
    mask_rows = lax.dynamic_slice(
        block_mask,
        (frame_index, half_index * query_blocks, zero_index),
        (1, query_blocks, key_blocks),
    )[0]
    scores = (
        jnp.einsum(
            "bqhd,bkhd->bhqk", queries, all_keys[:, :, 0], preferred_element_type=jnp.float32
        )
        * score_scale
    )
    scores = scores.reshape(videos, local_heads, query_blocks, BLOCK, key_blocks, BLOCK)
    allowed = (mask_rows == 1)[None, None, :, None, :, None]
    scores = jnp.where(allowed, scores, -jnp.inf).reshape(
        videos, local_heads, row_count, 2 * row_count
    )
    weights_bf = softmax_rounded(scores, 3)
    attended = jnp.einsum(
        "bhqk,bkhd->bqhd", weights_bf, all_keys[:, :, 1], preferred_element_type=jnp.float32
    ).astype(jnp.bfloat16)
    partial_value = jnp.dot(
        attended.reshape(-1, heads_width), space_out, preferred_element_type=jnp.float32
    ).reshape(videos, row_count, model_width)
    summed = head_total(partial_value)
    space_gate = lax.dynamic_slice_in_dim(space_mod[2], feature_start, part_width, 0)
    stream = tokens + space_gate * summed
    wide_stream = widen(stream)
    packed_time = project_inputs(modulate(wide_stream, time_mod), time_qkv)
    arrived = lax.all_to_all(
        packed_time.reshape(videos, seq_count, piece_rows, 3 * heads_width),
        "seq",
        split_axis=1,
        concat_axis=1,
        tiled=True,
    )
    packed_time = arrived.reshape(videos, frame_count, 2 * piece_rows, 3, local_heads, HD)
    scores_time = (
        jnp.einsum(
            "bfphd,bgphd->bphfg",
            packed_time[:, :, :, 0],
            packed_time[:, :, :, 1],
            preferred_element_type=jnp.float32,
        )
        * score_scale
    )
    weights_time = softmax_rounded(scores_time, 4)
    attended_time = jnp.einsum(
        "bphfg,bgphd->bfphd",
        weights_time,
        packed_time[:, :, :, 2],
        preferred_element_type=jnp.float32,
    ).astype(jnp.bfloat16)
    returned = lax.all_to_all(
        attended_time.reshape(videos, seq_count, piece_rows, heads_width),
        "seq",
        split_axis=1,
        concat_axis=1,
        tiled=True,
    )
    partial_time = jnp.dot(
        returned.reshape(-1, heads_width), time_out, preferred_element_type=jnp.float32
    ).reshape(videos, row_count, model_width)
    summed_time = head_total(partial_time)
    time_gate = lax.dynamic_slice_in_dim(time_mod[2], feature_start, part_width, 0)
    return stream + time_gate * summed_time


def solution(mesh):
    placed = (
        P(None, "seq", "fsdp"),
        P(),
        P(None, None, "fsdp"),
        P("fsdp", None),
        P(),
        P(None, None, "fsdp"),
        P("fsdp", None),
        P(),
    )
    return jax.shard_map(
        on_device, mesh=mesh, in_specs=placed, out_specs=P(None, "seq", "fsdp"), check_vma=False
    )
```

profile of v0, /device:TPU:32, one launch (start us, length us, event | category | flops | bytes accessed | tf_op | source)
XLA Modules:
  0.0 463.8 jit_solution(11474330209221537298)
XLA Ops:
  7.3 6.7 %copy.23 = bf16[3072,3,256]{0,2,1:T(8,128)(2,1)} copy(bf16[3072,3,256]{2,0,1:T(8,128)(2,1)} %param.10) | data formatting | bytes 9437184 | tf_op args[2]
  14.1 79.5 %all-gather.3.cloned.1.call-done = f32[1,384,3072]{2,1,0:T(8,128)} async-done(((f32[1,384,384]{2,1,0:T(8,128)}), f32[1,384,3072]{2,1,0:T(8,128)}) %all-gather.3.cloned.1.call-update) | async-done | bytes 4718608 | tf_op jit(solution)/shard_map/all_gather | solution.py:34
  93.6 2.6 reduce_sum.54
  96.2 3.1 multiply_reduce_fusion.1
  100.0 4.7 %fusion.22 = bf16[384,768]{1,0:T(8,128)(2,1)S(1)} fusion(bf16[3072,768]{0,1:T(8,128)(2,1)} %bitcast.115, f32[1,384,3072]{2,1,0:T(8,128)S(1)} %copy-done.2, f32[3072]{0:T(1024)S(1)} %bitcast.124, f32[3072]{0:T(1024)S(1)} %bitcast.125, f32[384]{0:T(512)S(1)} %add_rsqrt_fusion.1, f32[384]{0:T(512)S(1)} %broadcast_multiply_fusion.1), kind=kOutput, calls=%fused_computation.29 | convolution fusion | flops 1818132480 | bytes 10054656 | tf_op jit(solution)/shard_map/dot_general | solution.py:46
  107.1 1.3 maximum_select_fusion
  108.4 2.0 fusion.47
  110.5 2.9 fusion.31
  113.4 2.3 fusion.2
  115.6 10.8 %copy.37 = bf16[1,384,3072]{1,0,2:T(2,128)(2,1)} copy(bf16[1,384,3072]{2,1,0:T(8,128)(2,1)} %fusion.2) | data formatting | bytes 4718592
  126.4 4.2 copy.83
  130.7 80.2 %reduce-scatter.7.cloned.1.call-done = bf16[384,384]{1,0:T(8,128)(2,1)} async-done(((bf16[3072,384]{1,0:T(8,128)(2,1)}), bf16[384,384]{1,0:T(8,128)(2,1)}) %reduce-scatter.7.cloned.1.call-update) | async-done | bytes 294928
  214.2 6.7 %copy.27 = bf16[3072,3,256]{0,2,1:T(8,128)(2,1)} copy(bf16[3072,3,256]{2,0,1:T(8,128)(2,1)} %param.13) | data formatting | bytes 9437184 | tf_op args[5]
  220.9 73.0 %all-gather.5.cloned.1.call-done = f32[1,384,3072]{2,1,0:T(8,128)} async-done(((f32[1,384,384]{2,1,0:T(8,128)}), f32[1,384,3072]{2,1,0:T(8,128)}) %all-gather.5.cloned.1.call-update) | async-done | bytes 4718608 | tf_op jit(solution)/shard_map/all_gather | solution.py:34
  294.0 2.6 reduce_sum.57
  296.6 3.1 multiply_reduce_fusion
  300.4 4.7 %fusion.19 = bf16[384,768]{1,0:T(8,128)(2,1)S(1)} fusion(bf16[3072,768]{0,1:T(8,128)(2,1)} %bitcast.114, f32[1,384,3072]{2,1,0:T(8,128)S(1)} %copy-done.1, f32[3072]{0:T(1024)S(1)} %bitcast.122, f32[3072]{0:T(1024)S(1)} %bitcast.123, f32[384]{0:T(512)S(1)} %add_rsqrt_fusion, f32[384]{0:T(512)S(1)} %broadcast_multiply_fusion), kind=kOutput, calls=%fused_computation.28 | convolution fusion | flops 1818132480 | bytes 10054656 | tf_op jit(solution)/shard_map/dot_general | solution.py:46
  305.2 30.8 %all_to_all.10 = bf16[1,32,12,768]{3,2,0,1:T(8,128)(2,1)S(1)} all-to-all(bf16[1,32,12,768]{3,2,0,1:T(8,128)(2,1)S(1)} %bitcast.116), channel_id=1, replica_groups=mesh['seq'=32,'fsdp'=8] {'seq'}, dimensions={1} | all-to-all | bytes 1179648 | tf_op jit(solution)/shard_map/all_to_all | solution.py:106
  337.4 2.7 fusion.48
  343.2 15.7 %all_to_all.11 = bf16[1,32,12,256]{3,2,0,1:T(8,128)(2,1)} all-to-all(bf16[1,32,12,256]{3,2,0,1:T(8,128)(2,1)S(1)} %bitcast.118), channel_id=1, replica_groups=mesh['seq'=32,'fsdp'=8] {'seq'}, dimensions={1} | all-to-all | bytes 393216 | tf_op jit(solution)/shard_map/all_to_all | solution.py:130
  360.0 2.2 fusion.3
  362.2 10.8 %copy.39 = bf16[1,384,3072]{1,0,2:T(2,128)(2,1)} copy(bf16[1,384,3072]{2,1,0:T(8,128)(2,1)} %fusion.3) | data formatting | bytes 4718592
  373.0 4.2 copy.82
  377.2 77.0 %reduce-scatter.9.cloned.1.call-done = bf16[384,384]{1,0:T(8,128)(2,1)} async-done(((bf16[3072,384]{1,0:T(8,128)(2,1)}), bf16[384,384]{1,0:T(8,128)(2,1)}) %reduce-scatter.9.cloned.1.call-update) | async-done | bytes 294928
  (56 shorter events, 16.5 us)
Async XLA Ops:
  6.5 106.8 %copy-start = (bf16[256,3072]{1,0:T(8,128)(2,1)S(1)}, bf16[256,3072]{1,0:T(8,128)(2,1)}, u32[]{:S(2)}) copy-start(bf16[256,3072]{1,0:T(8,128)(2,1)} %param.11) | copy-start | bytes 4718596
  6.5 87.1 %all-gather.3.cloned.1.call-start = ((), (), s32[]{:S(2)}) async-start(), calls=%async_computation.4 | async-start | bytes 5308416 | tf_op jit(solution)/shard_map/all_gather | solution.py:34
  7.3 6.8 %copy-start.6 = (f32[3,3072]{1,0:T(4,128)S(1)}, f32[3,3072]{1,0:T(4,128)}, u32[]{:S(2)}) copy-start(f32[3,3072]{1,0:T(4,128)} %param.12) | copy-start | bytes 110596
  7.3 203.6 %reduce-scatter.7.cloned.1.call-start = ((), (), s32[]{:S(2)}) async-start(), calls=%async_computation.6 | async-start | bytes 2654208
  96.2 3.8 copy-start.2
  104.7 0.7 copy-start.8
  105.2 1.9 collective-permute-start
  130.6 82.4 %copy-start.4 = (f32[1,384,384]{2,1,0:T(8,128)S(1)}, f32[1,384,384]{2,1,0:T(8,128)}, u32[]{:S(2)}) copy-start(f32[1,384,384]{2,1,0:T(8,128)} %param.8) | copy-start | bytes 1769476
  130.6 163.3 %all-gather.5.cloned.1.call-start = ((), (), s32[]{:S(2)}) async-start(), calls=%async_computation.5 | async-start | bytes 5308416 | tf_op jit(solution)/shard_map/all_gather | solution.py:34
  213.9 7.0 %copy-start.7 = (f32[3,3072]{1,0:T(4,128)S(1)}, f32[3,3072]{1,0:T(4,128)}, u32[]{:S(2)}) copy-start(f32[3,3072]{1,0:T(4,128)} %param.15) | copy-start | bytes 110596
  213.9 240.3 %reduce-scatter.9.cloned.1.call-start = ((), (), s32[]{:S(2)}) async-start(), calls=%async_computation.7 | async-start | bytes 2654208
  296.6 3.8 copy-start.1
  337.4 22.6 %copy-start.5 = (bf16[256,3072]{1,0:T(8,128)(2,1)S(1)}, bf16[256,3072]{1,0:T(8,128)(2,1)}, u32[]{:S(2)}) copy-start(bf16[256,3072]{1,0:T(8,128)(2,1)} %param.14) | copy-start | bytes 4718596
  377.2 79.1 %copy-start.3 = (f32[1,384,384]{2,1,0:T(8,128)S(1)}, f32[1,384,384]{2,1,0:T(8,128)}, u32[]{:S(2)}) copy-start(f32[1,384,384]{2,1,0:T(8,128)} %multiply_add_fusion.1) | copy-start | bytes 1769476
Sparse Core Ops, SparseCore 0:
  10.0 83.5 all-gather.2
  130.8 80.0 reduce-scatter.6
  214.1 79.8 all-gather.4
  377.3 76.8 reduce-scatter.8
where the time goes:
time: 465 us; the launch traced here: 464 us
  waiting for transfers between devices  311 us (67%)
  local copies, waits for them, and re-layouts  55.1 us (12%)
  blocking collectives  46.6 us (10%)
  matrix products  22.7 us (5%)
  other arithmetic  14.8 us (3%)
  between operations  13.4 us (3%)
    unnamed x6, waiting for transfers between devices  158 us
    all_gather x2, waiting for transfers between devices, widen(): return lax.all_gather(shard, 'fsdp', axis=2, tiled=True)  153 us
    unnamed x30, local copies, waits for them, and re-layouts  50 us
    all_to_all x1, blocking collectives, on_device(): lax.all_to_all(packed_time.reshape(videos, seq_count, piece_rows, 3 * hea...  30.8 us
    all_to_all x1, blocking collectives, on_device(): lax.all_to_all(attended_time.reshape(videos, seq_count, piece_rows, heads...  15.7 us
    dot_general x2, matrix products, project_inputs(): jnp.dot(flat_rows, qkv_weight.reshape(model_width, -1), preferred_element...  9.34 us
  transfers between devices with their start and end apart: 5, of which 5 were waited for; matrix products, arithmetic and copies ran while one was open for 3% of the time, Pallas kernels for 0%

commit v1 on v0

v1 whole, which is shorter than its diff:
```python
import functools
import math

import jax
import jax.numpy as jnp
from jax import lax
from jax.experimental import pallas as pl
from jax.experimental.pallas import tpu as pltpu
from jax.sharding import PartitionSpec as P

HD = 128
BLOCK = 128
EPS = 1e-06
SCALE = 1.0 / math.sqrt(HD)
VMEM_LIMIT = 48 * 1024 * 1024
F32 = jnp.float32
BF16 = jnp.bfloat16


def whole(shape):
    return pl.BlockSpec(shape, lambda *_: (0,) * len(shape))


def params():
    return pltpu.CompilerParams(vmem_limit_bytes=VMEM_LIMIT)


def row_stats(parts_ref, mean_ref, rstd_ref):
    parts, rows, width = parts_ref.shape
    total = jnp.zeros((rows, 1), F32)
    for part in range(parts):
        total += jnp.sum(parts_ref[part].astype(F32), axis=1, keepdims=True)
    mean = total / (parts * width)
    spread = jnp.zeros((rows, 1), F32)
    for part in range(parts):
        centred = parts_ref[part].astype(F32) - mean
        spread += jnp.sum(centred * centred, axis=1, keepdims=True)
    mean_ref[...] = mean
    rstd_ref[...] = lax.rsqrt(spread / (parts * width) + EPS)


def modulated(parts_ref, mod_ref, mean_ref, rstd_ref, step, pair):
    mean, rstd = mean_ref[...], rstd_ref[...]
    width = parts_ref.shape[2]
    pieces = []
    for offset in range(pair):
        values = parts_ref[step * pair + offset].astype(F32)
        shift = mod_ref[0:1, offset * width : (offset + 1) * width]
        gain = 1.0 + mod_ref[1:2, offset * width : (offset + 1) * width]
        pieces.append((((values - mean) * rstd) * gain + shift).astype(BF16))
    return jnp.concatenate(pieces, axis=1)


def accumulate_qkv(parts_ref, mod_ref, weight_ref, acc_ref, mean_ref, rstd_ref, pair):
    step = pl.program_id(0)

    @pl.when(step == 0)
    def _():
        row_stats(parts_ref, mean_ref, rstd_ref)

    normed = modulated(parts_ref, mod_ref, mean_ref, rstd_ref, step, pair)
    width = weight_ref.shape[2]
    for part in range(3):
        product = jnp.dot(normed, weight_ref[part], preferred_element_type=F32)
        columns = slice(part * width, (part + 1) * width)

        @pl.when(step == 0)
        def _():
            acc_ref[:, columns] = product

        @pl.when(step > 0)
        def _():
            acc_ref[:, columns] += product


def space_in_kernel(pair, parts_ref, mod_ref, weight_ref, q_ref, kv_ref, acc_ref, mean_ref, rstd_ref):
    accumulate_qkv(parts_ref, mod_ref, weight_ref, acc_ref, mean_ref, rstd_ref, pair)

    @pl.when(pl.program_id(0) == pl.num_programs(0) - 1)
    def _():
        width = q_ref.shape[1]
        q_ref[...] = acc_ref[:, :width].astype(BF16)
        kv_ref[...] = acc_ref[:, width:].astype(BF16)


def space_in(parts, mod, weight):
    count, rows, width = parts.shape
    pair = 2 if count % 2 == 0 else 1
    heads_width = weight.shape[2]
    return pl.pallas_call(
        functools.partial(space_in_kernel, pair),
        grid=(count // pair,),
        in_specs=[
            whole((count, rows, width)),
            pl.BlockSpec((3, pair * width), lambda k: (0, k)),
            pl.BlockSpec((3, pair * width, heads_width), lambda k: (0, k, 0)),
        ],
        out_specs=[whole((rows, heads_width)), whole((rows, 2 * heads_width))],
        out_shape=[
            jax.ShapeDtypeStruct((rows, heads_width), BF16),
            jax.ShapeDtypeStruct((rows, 2 * heads_width), BF16),
        ],
        scratch_shapes=[
            pltpu.VMEM((rows, 3 * heads_width), F32),
            pltpu.VMEM((rows, 1), F32),
            pltpu.VMEM((rows, 1), F32),
        ],
        compiler_params=params(),
        cost_estimate=pl.CostEstimate(
            flops=2 * rows * count * width * 3 * heads_width,
            bytes_accessed=2 * count * width * (rows + 3 * heads_width),
            transcendentals=0,
        ),
        name="space_in",
    )(parts, mod, weight)


def project_out(attended, weight_ref, out_ref):
    blocks, _, width = out_ref.shape
    for block in range(blocks):
        out_ref[block] = jnp.dot(
            attended, weight_ref[:, block * width : (block + 1) * width], preferred_element_type=F32
        ).astype(BF16)


def space_attend_kernel(where_ref, mask_ref, q_ref, own_ref, other_ref, weight_ref, out_ref):
    rows, heads_width = q_ref.shape
    query_blocks = rows // BLOCK
    key_blocks = 2 * query_blocks
    frame, half = where_ref[0], where_ref[1]
    mask_base = (frame * key_blocks + half * query_blocks) * key_blocks
    heads = []
    for head in range(heads_width // HD):
        key_cols = slice(head * HD, (head + 1) * HD)
        value_cols = slice(heads_width + head * HD, heads_width + (head + 1) * HD)
        keys = [own_ref[:, key_cols], other_ref[:, key_cols]]
        values = [own_ref[:, value_cols], other_ref[:, value_cols]]
        pieces = []
        for block in range(query_blocks):
            query = q_ref[block * BLOCK : (block + 1) * BLOCK, key_cols]
            scored = []
            for side in range(2):
                scores = lax.dot_general(
                    query, keys[side], (((1,), (1,)), ((), ())), preferred_element_type=F32
                )
                side_half = half if side == 0 else 1 - half
                for key_block in range(query_blocks):
                    kept = mask_ref[
                        mask_base + block * key_blocks + side_half * query_blocks + key_block
                    ]
                    bias = jnp.where(kept == 1, 0.0, -jnp.inf).astype(F32)
                    scored.append(
                        scores[:, key_block * BLOCK : (key_block + 1) * BLOCK] * SCALE + bias
                    )
            scored = jnp.concatenate(scored, axis=1)
            row_max = jnp.max(scored, axis=1, keepdims=True)
            lifted = jnp.exp(scored - row_max)
            norm = jnp.sum(lifted, axis=1, keepdims=True)
            lifted = lifted.astype(BF16)
            mixed = jnp.dot(lifted[:, :rows], values[0], preferred_element_type=F32)
            mixed += jnp.dot(lifted[:, rows:], values[1], preferred_element_type=F32)
            pieces.append((mixed / norm).astype(BF16))
        heads.append(jnp.concatenate(pieces, axis=0))
    project_out(jnp.concatenate(heads, axis=1), weight_ref, out_ref)


def space_attend(where, mask, queries, own, other, weight, blocks):
    rows, heads_width = queries.shape
    width = weight.shape[1] // blocks
    return pl.pallas_call(
        space_attend_kernel,
        grid_spec=pltpu.PrefetchScalarGridSpec(
            num_scalar_prefetch=2,
            grid=(1,),
            in_specs=[
                whole(queries.shape),
                whole(own.shape),
                whole(other.shape),
                whole(weight.shape),
            ],
            out_specs=whole((blocks, rows, width)),
        ),
        out_shape=jax.ShapeDtypeStruct((blocks, rows, width), BF16),
        compiler_params=params(),
        cost_estimate=pl.CostEstimate(
            flops=2 * rows * heads_width * (4 * rows + weight.shape[1]),
            bytes_accessed=2 * (weight.size + rows * weight.shape[1] + 5 * rows * heads_width),
            transcendentals=2 * rows * rows * heads_width // HD,
        ),
        name="space_attend",
    )(where, mask, queries, own, other, weight)


def join_kernel(where_ref, parts_ref, tokens_ref, mod_ref, stream_ref, sent_ref):
    total = parts_ref[0].astype(F32)
    for part in range(1, parts_ref.shape[0]):
        total += parts_ref[part].astype(F32)
    stream = tokens_ref[...] + mod_ref[2:3, :] * total
    stream_ref[...] = stream
    sent_ref[...] = stream.astype(BF16)


def join(where, parts, tokens, mod):
    count, rows, width = parts.shape
    tile = BLOCK
    return pl.pallas_call(
        join_kernel,
        grid_spec=pltpu.PrefetchScalarGridSpec(
            num_scalar_prefetch=1,
            grid=(rows // tile,),
            in_specs=[
                pl.BlockSpec((count, tile, width), lambda i, w: (0, i, 0)),
                pl.BlockSpec((tile, width), lambda i, w: (i, 0)),
                pl.BlockSpec((3, width), lambda i, w: (0, w[2])),
            ],
            out_specs=[
                pl.BlockSpec((tile, width), lambda i, w: (i, 0)),
                pl.BlockSpec((tile, width), lambda i, w: (i, 0)),
            ],
        ),
        out_shape=[
            jax.ShapeDtypeStruct((rows, width), F32),
            jax.ShapeDtypeStruct((rows, width), BF16),
        ],
        compiler_params=params(),
        name="join",
    )(where, parts, tokens, mod)


def total_kernel(parts_ref, out_ref):
    total = parts_ref[0].astype(F32)
    for part in range(1, parts_ref.shape[0]):
        total += parts_ref[part].astype(F32)
    out_ref[...] = total.astype(BF16)


def total_of(parts):
    count, rows, width = parts.shape
    tile = BLOCK
    return pl.pallas_call(
        total_kernel,
        grid=(rows // tile,),
        in_specs=[pl.BlockSpec((count, tile, width), lambda i: (0, i, 0))],
        out_specs=pl.BlockSpec((tile, width), lambda i: (i, 0)),
        out_shape=jax.ShapeDtypeStruct((rows, width), BF16),
        compiler_params=params(),
        name="total_of",
    )(parts)


def time_kernel(pair, frames, parts_ref, mod_ref, weight_ref, out_weight_ref, out_ref,
                acc_ref, att_ref, mean_ref, rstd_ref):
    accumulate_qkv(parts_ref, mod_ref, weight_ref, acc_ref, mean_ref, rstd_ref, pair)

    @pl.when(pl.program_id(0) == pl.num_programs(0) - 1)
    def _():
        rows, packed_width = acc_ref.shape
        heads_width = packed_width // 3
        places = rows // frames
        group = 8
        span = frames * group
        row_place = lax.broadcasted_iota(jnp.int32, (span, span), 0) % group
        col_place = lax.broadcasted_iota(jnp.int32, (span, span), 1) % group
        bias = jnp.where(row_place == col_place, 0.0, -jnp.inf).astype(F32)
        packed = acc_ref[...].reshape(frames, places, packed_width)
        for start in range(0, places, group):
            chunk = packed[:, start : start + group, :].reshape(span, packed_width).astype(BF16)
            for head in range(heads_width // HD):
                low = head * HD
                query = chunk[:, low : low + HD]
                key = chunk[:, heads_width + low : heads_width + low + HD]
                value = chunk[:, 2 * heads_width + low : 2 * heads_width + low + HD]
                scores = lax.dot_general(
                    query, key, (((1,), (1,)), ((), ())), preferred_element_type=F32
                ) * SCALE + bias
                lifted = jnp.exp(scores - jnp.max(scores, axis=1, keepdims=True))
                norm = jnp.sum(lifted, axis=1, keepdims=True)
                mixed = jnp.dot(lifted.astype(BF16), value, preferred_element_type=F32) / norm
                att_ref[:, start : start + group, low : low + HD] = mixed.reshape(frames, group, HD)
        attended = att_ref[...].reshape(rows, heads_width).astype(BF16)
        project_out(attended, out_weight_ref, out_ref)


def time_layer(parts, mod, weight, out_weight, frames):
    count, rows, width = parts.shape
    pair = 2 if count % 2 == 0 else 1
    heads_width = weight.shape[2]
    return pl.pallas_call(
        functools.partial(time_kernel, pair, frames),
        grid=(count // pair,),
        in_specs=[
            whole((count, rows, width)),
            pl.BlockSpec((3, pair * width), lambda k: (0, k)),
            pl.BlockSpec((3, pair * width, heads_width), lambda k: (0, k, 0)),
            whole(out_weight.shape),
        ],
        out_specs=whole((count, rows, width)),
        out_shape=jax.ShapeDtypeStruct((count, rows, width), BF16),
        scratch_shapes=[
            pltpu.VMEM((rows, 3 * heads_width), F32),
            pltpu.VMEM((frames, rows // frames, heads_width), F32),
            pltpu.VMEM((rows, 1), F32),
            pltpu.VMEM((rows, 1), F32),
        ],
        compiler_params=params(),
        cost_estimate=pl.CostEstimate(
            flops=2 * rows * count * width * 4 * heads_width,
            bytes_accessed=2 * count * width * (2 * rows + 4 * heads_width),
            transcendentals=rows * BLOCK * heads_width // HD,
        ),
        name="time_layer",
    )(parts, mod, weight, out_weight)


def gathered(shard, count):
    copies = jnp.broadcast_to(shard[None], (count,) + shard.shape)
    return lax.all_to_all(copies, "fsdp", split_axis=0, concat_axis=0, tiled=True)


def on_device(tokens, block_mask, space_qkv, space_out, space_mod, time_qkv, time_out, time_mod):
    videos, rows, width = tokens.shape
    parts = lax.axis_size("fsdp")
    seq_count = lax.axis_size("seq")
    frames = seq_count // 2
    places = rows // frames
    seq_index = lax.axis_index("seq")
    where = jnp.stack([seq_index // 2, seq_index % 2, lax.axis_index("fsdp")]).astype(jnp.int32)
    same_half = [[2 * frame + half for frame in range(frames)] for half in range(2)]

    def across_frames(values):
        return lax.all_to_all(
            values.reshape(frames, places, width), "seq", split_axis=0, concat_axis=0, tiled=True,
            axis_index_groups=same_half,
        ).reshape(rows, width)

    def across_parts(values):
        return lax.all_to_all(values, "fsdp", split_axis=0, concat_axis=0, tiled=True)

    local = tokens.reshape(rows, width)
    queries, own = space_in(
        gathered(local.astype(BF16), parts), space_mod, jnp.swapaxes(space_qkv, 0, 1)
    )
    other = lax.ppermute(own, "seq", [(i, i ^ 1) for i in range(seq_count)])
    partial = space_attend(where, block_mask.reshape(-1), queries, own, other, space_out, parts)
    stream, sent = join(where, across_parts(partial), local, space_mod)
    partial_time = time_layer(
        gathered(across_frames(sent), parts), time_mod, jnp.swapaxes(time_qkv, 0, 1), time_out, frames
    )
    returned = across_frames(total_of(across_parts(partial_time)))
    gate = lax.dynamic_slice_in_dim(time_mod[2], lax.axis_index("fsdp") * width, width, 0)
    return (stream + gate * returned.astype(F32)).reshape(tokens.shape)


def solution(mesh):
    placed = (
        P(None, "seq", "fsdp"),
        P(),
        P(None, None, "fsdp"),
        P("fsdp", None),
        P(),
        P(None, None, "fsdp"),
        P("fsdp", None),
        P(),
    )
    return jax.shard_map(
        on_device, mesh=mesh, in_specs=placed, out_specs=P(None, "seq", "fsdp"), check_vma=False
    )
```

time: 465 us -> 202 us (0.43)
  waiting for transfers between devices: 311 us -> 10.6 us
  blocking collectives: 46.6 us -> 156 us
  local copies, waits for them, and re-layouts: 55.1 us -> 0.74 us
  Pallas kernels: 0 us -> 26.6 us
  matrix products: 22.7 us -> 0 us
  between operations: 13.4 us -> 0.16 us
  other arithmetic: 14.8 us -> 2.08 us
  starting transfers between devices: 0.4 us -> 5.38 us
    unnamed x6 -> x0, waiting for transfers between devices: 158 us -> none
    all_gather x2 -> x0, waiting for transfers between devices: 153 us -> none  [widen(): return lax.all_gather(shard, 'fsdp', axis=2, tiled=True)]
    all_to_all x2 -> x5, blocking collectives: 46.6 us -> 156 us  [the longest x2 72.1 us: gathered(): lax.all_to_all(copies, 'fsdp', split_axis=0, concat_axis=0, tiled=True)]
    unnamed x30 -> x13, local copies, waits for them, and re-layouts: 50 us -> 0.15 us
    pallas_call x0 -> x5, Pallas kernels: none -> 26.6 us  [the longest x1 11.5 us: time_layer(): pl.pallas_call(functools.partial(time_kernel, pair, frames), grid=(count...]
    dot_general x6 -> x0, matrix products: 18 us -> none  [the longest x2 9.34 us: project_inputs(): jnp.dot(flat_rows, qkv_weight.reshape(model_width, -1), preferred_element...]
    reduce_sum x4 -> x0, other arithmetic: 11.4 us -> none  [the longest x2 6.18 us: modulate(): variance = jnp.mean(centred * centred, axis=-1, keepdims=True)]
    all_to_all x0 -> x1, waiting for transfers between devices: none -> 9.24 us  [across_frames(): lax.all_to_all(values.reshape(frames, places, width), 'seq', split_axis=0...]
  transfers between devices with their start and end apart: 5 -> 2, of which waited for: 5 -> 2; matrix products, arithmetic and copies ran while one was open for 3% -> 0% of each run, Pallas kernels for 0% -> 0%
where the time goes in v1:
time: 202 us
  blocking collectives  156 us (77%)
  Pallas kernels  26.6 us (13%)
  waiting for transfers between devices  10.6 us (5%)
  starting transfers between devices  5.38 us (3%)
  other arithmetic  2.08 us (1%)
    all_to_all x2, blocking collectives, gathered(): lax.all_to_all(copies, 'fsdp', split_axis=0, concat_axis=0, tiled=True)  72.1 us
    all_to_all x2, blocking collectives, across_parts(): lax.all_to_all(values, 'fsdp', split_axis=0, concat_axis=0, tiled=True)  66.3 us
    all_to_all x1, blocking collectives, across_frames(): lax.all_to_all(values.reshape(frames, places, width), 'seq', split_axis=0...  17.8 us
    pallas_call x1, Pallas kernels, time_layer(): pl.pallas_call(functools.partial(time_kernel, pair, frames), grid=(count...  11.5 us
    all_to_all x1, waiting for transfers between devices, across_frames(): lax.all_to_all(values.reshape(frames, places, width), 'seq', split_axis=0...  9.24 us
    pallas_call x1, Pallas kernels, space_in(): pl.pallas_call(functools.partial(space_in_kernel, pair), grid=(count // p...  8.45 us
    all_to_all x1, starting transfers between devices, across_frames(): lax.all_to_all(values.reshape(frames, places, width), 'seq', split_axis=0...  5.29 us
  transfers between devices with their start and end apart: 2, of which 2 were waited for; matrix products, arithmetic and copies ran while one was open for 0% of the time, Pallas kernels for 0%

profile of v1, /device:TPU:32, one launch (start us, length us, event | category | flops | bytes accessed | tf_op | source)
XLA Modules:
  0.0 201.8 jit_solution(13115668116585708430)
XLA Ops:
  0.0 1.1 convert_bitcast_fusion
  1.1 0.2 broadcast_in_dim.17
  1.3 37.8 %all_to_all.30.parts_ref = bf16[8,384,384]{2,1,0:T(8,128)(2,1)S(1)} all-to-all(bf16[8,384,384]{2,1,0:T(8,128)(2,1)S(1)} %broadcast_in_dim.17), channel_id=1, replica_groups=mesh['seq'=32,'fsdp'=8] {'fsdp'}, dimensions={0} | all-to-all | bytes 4718592 | tf_op jit(solution)/shard_map/all_to_all | solution.py:317
  39.1 8.4 %space_in.1 = (bf16[384,256]{1,0:T(8,128)(2,1)S(1)}, bf16[384,512]{1,0:T(8,128)(2,1)S(1)}) custom-call(bf16[8,384,384]{2,1,0:T(8,128)(2,1)S(1)} %all_to_all.30.parts_ref, f32[3,3072]{1,0:T(4,128)S(1)} %copy-done.3, bf16[3,3072,256]{2,1,0:T(8,128)(2,1)} %bitcast.18), custom_call_target="tpu_custom_call" | custom-call | flops 1811939328 | bytes 7077888 | tf_op jit(solution)/shard_map/space_in/pallas_call | solution.py:90
  47.5 0.1 collective-permute-start
  47.7 0.1 copy.9
  47.8 0.1 reshape.21.mask_ref
  48.0 0.1 pad_add_fusion.where_ref
  48.0 1.3 collective-permute-done.other_ref
  49.4 3.7 %space_attend.1 = bf16[8,384,384]{2,1,0:T(8,128)(2,1)S(1)} custom-call(s32[3]{0:T(128)S(1)} %pad_add_fusion.where_ref, s32[576]{0:T(1024)S(1)} %reshape.21.mask_ref, bf16[384,256]{1,0:T(8,128)(2,1)S(1)} %get-tuple-element.9.q_ref, bf16[384,512]{1,0:T(8,128)(2,1)S(1)} %get-tuple-element.10.own_ref, bf16[384,512]{1,0:T(8,128)(2,1)S(1)} %collective-permute-done.other_ref, ...), custom_call_target="tpu_custom_call" | custom-call | flops 905969664 | bytes 4915200 | tf_op jit(solution)/shard_map/space_attend/pallas_call | solution.py:170
  53.1 0.0 copy-start
  53.1 34.5 %all_to_all.31.parts_ref = bf16[8,384,384]{2,1,0:T(8,128)(2,1)S(1)} all-to-all(bf16[8,384,384]{2,1,0:T(8,128)(2,1)S(1)} %space_attend.1), channel_id=1, replica_groups=mesh['seq'=32,'fsdp'=8] {'fsdp'}, dimensions={0} | all-to-all | bytes 4718592 | tf_op jit(solution)/shard_map/all_to_all | solution.py:337
  87.6 1.2 join.1
  88.8 17.8 %all_to_all.32 = bf16[16,24,384]{2,1,0:T(8,128)(2,1)S(1)} all-to-all(bf16[16,24,384]{2,1,0:T(8,128)(2,1)S(1)} %bitcast.17), channel_id=1, replica_groups={{0,16,32,48,64,80,96,112,128,144,160,176,192,208,224,240},{8,24,40,56,7..., dimensions={0} | all-to-all | bytes 589824 | tf_op jit(solution)/shard_map/all_to_all | solution.py:331
  106.7 0.2 broadcast_in_dim.19
  106.9 0.0 copy-start.2
  106.9 0.0 copy-start.4
  106.9 34.3 %all_to_all.33.parts_ref = bf16[8,384,384]{2,1,0:T(8,128)(2,1)} all-to-all(bf16[8,384,384]{2,1,0:T(8,128)(2,1)S(1)} %broadcast_in_dim.19), channel_id=1, replica_groups=mesh['seq'=32,'fsdp'=8] {'fsdp'}, dimensions={0} | all-to-all | bytes 4718592 | tf_op jit(solution)/shard_map/all_to_all | solution.py:317
  141.3 11.5 %time_layer.1 = bf16[8,384,384]{2,1,0:T(8,128)(2,1)S(1)} custom-call(bf16[8,384,384]{2,1,0:T(8,128)(2,1)} %all_to_all.33.parts_ref, f32[3,3072]{1,0:T(4,128)S(1)} %copy-done.4, bf16[3,3072,256]{2,1,0:T(8,128)(2,1)} %bitcast.19, bf16[256,3072]{1,0:T(8,128)(2,1)S(1)} %copy-done.2), custom_call_target="tpu_custom_call" | custom-call | flops 2415919104 | bytes 11010048 | tf_op jit(solution)/shard_map/time_layer/pallas_call | solution.py:288
  152.8 31.8 %all_to_all.34.parts_ref = bf16[8,384,384]{2,1,0:T(8,128)(2,1)S(1)} all-to-all(bf16[8,384,384]{2,1,0:T(8,128)(2,1)S(1)} %time_layer.1), channel_id=1, replica_groups=mesh['seq'=32,'fsdp'=8] {'fsdp'}, dimensions={0} | all-to-all | bytes 4718592 | tf_op jit(solution)/shard_map/all_to_all | solution.py:337
  184.6 1.7 total_of.1
  186.3 5.3 %all-to-all-start.5 = ((bf16[16,24,384]{2,1,0:T(8,128)(2,1)}), bf16[16,24,384]{2,1,0:T(8,128)(2,1)S(1)}, u32[]{:S(2)}, u32[]{:S(2)}) async-start(bf16[16,24,384]{2,1,0:T(8,128)(2,1)} %bitcast.9), calls=%async_computation.5 | async-start | bytes 589824 | tf_op jit(solution)/shard_map/all_to_all | solution.py:331
  191.6 9.2 %all-to-all-done.5 = bf16[16,24,384]{2,1,0:T(8,128)(2,1)S(1)} async-done(((bf16[16,24,384]{2,1,0:T(8,128)(2,1)}), bf16[16,24,384]{2,1,0:T(8,128)(2,1)S(1)}, u32[]{:S(2)}, u32[]{:S(2)}) %all-to-all-start.5) | async-done | bytes 294944 | tf_op jit(solution)/shard_map/all_to_all | solution.py:331
  200.9 0.9 fusion.1
  (11 shorter events, 0.1 us)
Async XLA Ops:
  1.3 37.8 %copy-start.3 = (f32[3,3072]{1,0:T(4,128)S(1)}, f32[3,3072]{1,0:T(4,128)}, u32[]{:S(2)}) copy-start(f32[3,3072]{1,0:T(4,128)} %mod_ref.4) | copy-start | bytes 110596
  39.1 8.6 %copy-start.5 = (s32[16,6,6]{0,2,1:T(8,128)S(1)}, s32[16,6,6]{0,2,1:T(8,128)}, u32[]{:S(2)}) copy-start(s32[16,6,6]{0,2,1:T(8,128)} %param.9) | copy-start | bytes 6916
  39.1 10.3 %copy-start.1 = (bf16[256,3072]{1,0:T(8,128)(2,1)S(1)}, bf16[256,3072]{1,0:T(8,128)(2,1)}, u32[]{:S(2)}) copy-start(bf16[256,3072]{1,0:T(8,128)(2,1)} %weight_ref.1) | copy-start | bytes 4718596
  47.5 1.8 collective-permute-start
  53.1 34.5 %copy-start = (f32[1,384,384]{2,1,0:T(8,128)S(1)}, f32[1,384,384]{2,1,0:T(8,128)}, u32[]{:S(2)}) copy-start(f32[1,384,384]{2,1,0:T(8,128)} %param.8) | copy-start | bytes 1769476
  106.9 34.4 %copy-start.2 = (bf16[256,3072]{1,0:T(8,128)(2,1)S(1)}, bf16[256,3072]{1,0:T(8,128)(2,1)}, u32[]{:S(2)}) copy-start(bf16[256,3072]{1,0:T(8,128)(2,1)} %out_weight_ref.1) | copy-start | bytes 4718596
  106.9 34.4 %copy-start.4 = (f32[3,3072]{1,0:T(4,128)S(1)}, f32[3,3072]{1,0:T(4,128)}, u32[]{:S(2)}) copy-start(f32[3,3072]{1,0:T(4,128)} %mod_ref.5) | copy-start | bytes 110596
  186.3 14.6 %all-to-all-start.5 = ((bf16[16,24,384]{2,1,0:T(8,128)(2,1)}), bf16[16,24,384]{2,1,0:T(8,128)(2,1)S(1)}, u32[]{:S(2)}, u32[]{:S(2)}) async-start(bf16[16,24,384]{2,1,0:T(8,128)(2,1)} %bitcast.9), calls=%async_computation.5 | async-start | bytes 589824 | tf_op jit(solution)/shard_map/all_to_all | solution.py:331

commit v2 on v1

v2 whole, which is shorter than its diff:
```python
import functools
import math

import jax
import jax.numpy as jnp
from jax import lax
from jax.experimental import pallas as pl
from jax.experimental.pallas import tpu as pltpu
from jax.sharding import PartitionSpec as P

HD = 128
BLOCK = 128
EPS = 1e-06
SCALE = 1.0 / math.sqrt(HD)
VMEM_LIMIT = 32 * 1024 * 1024
F32 = jnp.float32
BF16 = jnp.bfloat16
LINES = 16


def whole(shape):
    return pl.BlockSpec(shape, lambda *_: (0,) * len(shape))


def params():
    return pltpu.CompilerParams(vmem_limit_bytes=VMEM_LIMIT)


def spread_columns(columns, rows):
    lane = lax.broadcasted_iota(jnp.int32, (rows, 128), 1)
    table = jnp.zeros((rows, 128), F32)
    for index, column in enumerate(columns):
        table = jnp.where(lane == index, column, table)
    return table


def bf16_terms(values, count):
    terms = []
    for _ in range(count):
        term = values.astype(BF16).astype(F32)
        terms.append(term)
        values = values - term
    return terms


def centre(values):
    mean = jnp.sum(values, axis=1, keepdims=True) / values.shape[1]
    centred = values - mean
    squares = jnp.sum(centred * centred, axis=1, keepdims=True)
    table = spread_columns(bf16_terms(mean, 3) + bf16_terms(squares, 2), values.shape[0])
    return centred.astype(BF16), table


def pack_kernel(where_ref, tokens_ref, space_ref, time_ref, out_ref):
    parts, _, width = out_ref.shape
    rows = tokens_ref.shape[0]
    centred, table = centre(tokens_ref[...])
    stats = jnp.transpose(table)[:8].astype(BF16)
    second = jnp.full(space_ref.shape, where_ref[1], jnp.int32) == 1
    lines = jnp.where(second, time_ref[...].astype(F32), space_ref[...].astype(F32)).astype(BF16)
    for part in range(parts):
        out_ref[part, :rows, :] = centred
        out_ref[part, rows : rows + LINES, :] = lines[:, part * width : (part + 1) * width]
        out_ref[part, rows + LINES :, :] = stats


def pack(where, tokens, space_out, time_out):
    rows, width = tokens.shape
    model_width = space_out.shape[1]
    parts = model_width // width
    line_spec = pl.BlockSpec((LINES, model_width), lambda i, w: (w[0], 0))
    shape = (parts, rows + LINES + 8, width)
    return pl.pallas_call(
        pack_kernel,
        grid_spec=pltpu.PrefetchScalarGridSpec(
            num_scalar_prefetch=1,
            grid=(1,),
            in_specs=[whole(tokens.shape), line_spec, line_spec],
            out_specs=whole(shape),
        ),
        out_shape=jax.ShapeDtypeStruct(shape, BF16),
        compiler_params=params(),
        name="pack",
    )(where, tokens, space_out, time_out)


def repack_kernel(arrived_ref, out_ref):
    parts, _, width = out_ref.shape
    rows = arrived_ref.shape[0]
    stats = jnp.transpose(arrived_ref[:, width:].astype(F32))[:8].astype(BF16)
    for part in range(parts):
        out_ref[part, :rows, :] = arrived_ref[:, :width]
        out_ref[part, rows:, :] = stats


def repack(arrived, parts):
    rows, width = arrived.shape
    shape = (parts, rows + 8, width - 128)
    return pl.pallas_call(
        repack_kernel,
        grid=(1,),
        in_specs=[whole(arrived.shape)],
        out_specs=whole(shape),
        out_shape=jax.ShapeDtypeStruct(shape, BF16),
        compiler_params=params(),
        name="repack",
    )(arrived)


def row_stats(stats_ref, offset_ref, scale_ref, width):
    parts = stats_ref.shape[0]
    means, squares = [], 0.0
    for part in range(parts):
        lines = stats_ref[part].astype(F32)
        means.append(lines[0:1] + lines[1:2] + lines[2:3])
        squares = squares + (lines[3:4] + lines[4:5])
    mean = sum(means) / parts
    offsets = [part_mean - mean for part_mean in means]
    between = sum(offset * offset for offset in offsets) * width
    scale = lax.rsqrt((squares + between) / (parts * width) + EPS)
    rows = mean.shape[1]
    line = lax.broadcasted_iota(jnp.int32, (128, rows), 0)
    table = jnp.zeros((128, rows), F32)
    for index, entry in enumerate(offsets + [scale]):
        table = jnp.where(line == index, entry, table)
    table = jnp.transpose(table)
    for part in range(parts):
        offset_ref[part] = jnp.broadcast_to(table[:, part : part + 1], (rows, 128))
    scale_ref[...] = jnp.broadcast_to(table[:, parts : parts + 1], (rows, 128))


def accumulate_qkv(parts_ref, stats_ref, mod_ref, weight_ref, acc_ref, offset_ref, scale_ref):
    step = pl.program_id(0)
    pair, rows, width = parts_ref.shape

    @pl.when(step == 0)
    def _():
        row_stats(stats_ref, offset_ref, scale_ref, width)

    scale = scale_ref[...]
    pieces = []
    for index in range(pair):
        offset = offset_ref[step * pair + index]
        for start in range(0, width, 128):
            columns = slice(index * width + start, index * width + start + 128)
            values = parts_ref[index, :, start : start + 128].astype(F32)
            shift = mod_ref[0:1, columns]
            gain = 1.0 + mod_ref[1:2, columns]
            pieces.append((((values + offset) * scale) * gain + shift).astype(BF16))
    normed = jnp.concatenate(pieces, axis=1)
    heads_width = weight_ref.shape[2]
    for part in range(3):
        product = jnp.dot(normed, weight_ref[part], preferred_element_type=F32)
        columns = slice(part * heads_width, (part + 1) * heads_width)

        @pl.when(step == 0)
        def _():
            acc_ref[:, columns] = product

        @pl.when(step > 0)
        def _():
            acc_ref[:, columns] += product


def qkv_specs(parts, rows, width, heads_width):
    count, total_rows, _ = parts.shape
    pair = 2 if count % 2 == 0 else 1
    last = total_rows // 8 - 1
    grid = (count // pair,)
    in_specs = [
        pl.BlockSpec((pair, rows, width), lambda k: (k, 0, 0)),
        pl.BlockSpec((count, 8, width), lambda k: (0, last, 0)),
        pl.BlockSpec((3, pair * width), lambda k: (0, k)),
        pl.BlockSpec((3, pair * width, heads_width), lambda k: (0, k, 0)),
    ]
    scratch = [
        pltpu.VMEM((rows, 3 * heads_width), F32),
        pltpu.VMEM((count, rows, 128), F32),
        pltpu.VMEM((rows, 128), F32),
    ]
    cost = pl.CostEstimate(
        flops=2 * rows * count * width * 3 * heads_width,
        bytes_accessed=2 * count * width * (rows + 3 * heads_width),
        transcendentals=0,
    )
    return grid, in_specs, scratch, cost


def space_in_kernel(parts_ref, stats_ref, mod_ref, weight_ref, q_ref, kv_ref, *scratch):
    accumulate_qkv(parts_ref, stats_ref, mod_ref, weight_ref, *scratch)
    acc_ref = scratch[0]

    @pl.when(pl.program_id(0) == pl.num_programs(0) - 1)
    def _():
        width = q_ref.shape[1]
        q_ref[...] = acc_ref[:, :width].astype(BF16)
        kv_ref[...] = acc_ref[:, width:].astype(BF16)


def space_in(parts, mod, weight, rows):
    width, heads_width = parts.shape[2], weight.shape[2]
    grid, in_specs, scratch, cost = qkv_specs(parts, rows, width, heads_width)
    return pl.pallas_call(
        space_in_kernel,
        grid=grid,
        in_specs=in_specs,
        out_specs=[whole((rows, heads_width)), whole((rows, 2 * heads_width))],
        out_shape=[
            jax.ShapeDtypeStruct((rows, heads_width), BF16),
            jax.ShapeDtypeStruct((rows, 2 * heads_width), BF16),
        ],
        scratch_shapes=scratch,
        compiler_params=params(),
        cost_estimate=cost,
        name="space_in",
    )(parts, parts, mod, weight)


def project_out(attended, weight_ref, out_ref):
    blocks, _, width = out_ref.shape
    for block in range(blocks):
        out_ref[block] = jnp.dot(
            attended, weight_ref[:, block * width : (block + 1) * width], preferred_element_type=F32
        ).astype(BF16)


def space_attend_kernel(where_ref, mask_ref, q_ref, own_ref, other_ref, weight_ref, out_ref):
    rows, heads_width = q_ref.shape
    query_blocks = rows // BLOCK
    key_blocks = 2 * query_blocks
    frame, half = where_ref[0], where_ref[1]
    mask_base = (frame * key_blocks + half * query_blocks) * key_blocks
    heads = []
    for head in range(heads_width // HD):
        key_cols = slice(head * HD, (head + 1) * HD)
        value_cols = slice(heads_width + head * HD, heads_width + (head + 1) * HD)
        keys = [own_ref[:, key_cols], other_ref[:, key_cols]]
        values = [own_ref[:, value_cols], other_ref[:, value_cols]]
        pieces = []
        for block in range(query_blocks):
            query = q_ref[block * BLOCK : (block + 1) * BLOCK, key_cols]
            scored = []
            for side in range(2):
                scores = lax.dot_general(
                    query, keys[side], (((1,), (1,)), ((), ())), preferred_element_type=F32
                )
                side_half = half if side == 0 else 1 - half
                for key_block in range(query_blocks):
                    kept = mask_ref[
                        mask_base + block * key_blocks + side_half * query_blocks + key_block
                    ]
                    bias = jnp.where(kept == 1, 0.0, -jnp.inf).astype(F32)
                    scored.append(
                        scores[:, key_block * BLOCK : (key_block + 1) * BLOCK] * SCALE + bias
                    )
            scored = jnp.concatenate(scored, axis=1)
            row_max = jnp.max(scored, axis=1, keepdims=True)
            lifted = jnp.exp(scored - row_max)
            norm = jnp.sum(lifted, axis=1, keepdims=True)
            lifted = lifted.astype(BF16)
            mixed = jnp.dot(lifted[:, :rows], values[0], preferred_element_type=F32)
            mixed += jnp.dot(lifted[:, rows:], values[1], preferred_element_type=F32)
            pieces.append((mixed / norm).astype(BF16))
        heads.append(jnp.concatenate(pieces, axis=0))
    project_out(jnp.concatenate(heads, axis=1), weight_ref, out_ref)


def space_attend(where, mask, queries, own, other, weight, blocks):
    rows, heads_width = queries.shape
    width = weight.shape[1] // blocks
    return pl.pallas_call(
        space_attend_kernel,
        grid_spec=pltpu.PrefetchScalarGridSpec(
            num_scalar_prefetch=2,
            grid=(1,),
            in_specs=[
                whole(queries.shape),
                whole(own.shape),
                whole(other.shape),
                whole(weight.shape),
            ],
            out_specs=whole((blocks, rows, width)),
        ),
        out_shape=jax.ShapeDtypeStruct((blocks, rows, width), BF16),
        compiler_params=params(),
        cost_estimate=pl.CostEstimate(
            flops=2 * rows * heads_width * (4 * rows + weight.shape[1]),
            bytes_accessed=2 * (weight.size + rows * weight.shape[1] + 5 * rows * heads_width),
            transcendentals=2 * rows * rows * heads_width // HD,
        ),
        name="space_attend",
    )(where, mask, queries, own, other, weight)


def join_kernel(where_ref, parts_ref, tokens_ref, mod_ref, stream_ref, sent_ref):
    total = parts_ref[0].astype(F32)
    for part in range(1, parts_ref.shape[0]):
        total += parts_ref[part].astype(F32)
    stream = tokens_ref[...] + mod_ref[2:3, :] * total
    stream_ref[...] = stream
    centred, table = centre(stream)
    sent_ref[:, : stream.shape[1]] = centred
    sent_ref[:, stream.shape[1] :] = table.astype(BF16)


def join(where, parts, tokens, mod):
    count, rows, width = parts.shape
    tile = BLOCK
    return pl.pallas_call(
        join_kernel,
        grid_spec=pltpu.PrefetchScalarGridSpec(
            num_scalar_prefetch=1,
            grid=(rows // tile,),
            in_specs=[
                pl.BlockSpec((count, tile, width), lambda i, w: (0, i, 0)),
                pl.BlockSpec((tile, width), lambda i, w: (i, 0)),
                pl.BlockSpec((3, width), lambda i, w: (0, w[2])),
            ],
            out_specs=[
                pl.BlockSpec((tile, width), lambda i, w: (i, 0)),
                pl.BlockSpec((tile, width + 128), lambda i, w: (i, 0)),
            ],
        ),
        out_shape=[
            jax.ShapeDtypeStruct((rows, width), F32),
            jax.ShapeDtypeStruct((rows, width + 128), BF16),
        ],
        compiler_params=params(),
        name="join",
    )(where, parts, tokens, mod)


def time_kernel(frames, parts_ref, stats_ref, mod_ref, weight_ref, out_ref, att_ref, *scratch):
    accumulate_qkv(parts_ref, stats_ref, mod_ref, weight_ref, *scratch)
    acc_ref = scratch[0]

    @pl.when(pl.program_id(0) == pl.num_programs(0) - 1)
    def _():
        rows, packed_width = acc_ref.shape
        heads_width = packed_width // 3
        places = rows // frames
        group = 8
        span = frames * group
        row_place = lax.broadcasted_iota(jnp.int32, (span, span), 0) % group
        col_place = lax.broadcasted_iota(jnp.int32, (span, span), 1) % group
        bias = jnp.where(row_place == col_place, 0.0, -jnp.inf).astype(F32)
        packed = acc_ref[...].reshape(frames, places, packed_width)
        for start in range(0, places, group):
            chunk = packed[:, start : start + group, :].reshape(span, packed_width).astype(BF16)
            for head in range(heads_width // HD):
                low = head * HD
                query = chunk[:, low : low + HD]
                key = chunk[:, heads_width + low : heads_width + low + HD]
                value = chunk[:, 2 * heads_width + low : 2 * heads_width + low + HD]
                scores = lax.dot_general(
                    query, key, (((1,), (1,)), ((), ())), preferred_element_type=F32
                ) * SCALE + bias
                lifted = jnp.exp(scores - jnp.max(scores, axis=1, keepdims=True))
                norm = jnp.sum(lifted, axis=1, keepdims=True)
                mixed = jnp.dot(lifted.astype(BF16), value, preferred_element_type=F32) / norm
                att_ref[:, start : start + group, low : low + HD] = mixed.reshape(frames, group, HD)
        out_ref[...] = att_ref[...].reshape(rows, heads_width).astype(BF16)


def time_layer(parts, mod, weight, rows, frames):
    width, heads_width = parts.shape[2], weight.shape[2]
    grid, in_specs, scratch, cost = qkv_specs(parts, rows, width, heads_width)
    return pl.pallas_call(
        functools.partial(time_kernel, frames),
        grid=grid,
        in_specs=in_specs,
        out_specs=whole((rows, heads_width)),
        out_shape=jax.ShapeDtypeStruct((rows, heads_width), BF16),
        scratch_shapes=[pltpu.VMEM((frames, rows // frames, heads_width), F32)] + scratch,
        compiler_params=params(),
        cost_estimate=cost,
        name="time_layer",
    )(parts, parts, mod, weight)


def finish_kernel(where_ref, parts_ref, weight_ref, stream_ref, mod_ref, out_ref):
    count, rows, heads_width = parts_ref.shape
    width = out_ref.shape[1]
    total = jnp.zeros((rows, width), F32)
    for part in range(count):
        lines = weight_ref[:, 0, part].reshape(heads_width, width)
        total += jnp.dot(parts_ref[part], lines, preferred_element_type=F32)
    out_ref[...] = stream_ref[...] + mod_ref[2:3, :] * total


def finish(layer, where, parts, weight, stream, mod):
    count, rows, heads_width = parts.shape
    frames, layers, _, lines, width = weight.shape
    return pl.pallas_call(
        finish_kernel,
        grid_spec=pltpu.PrefetchScalarGridSpec(
            num_scalar_prefetch=1,
            grid=(1,),
            in_specs=[
                whole(parts.shape),
                pl.BlockSpec((frames, 1, count, lines, width), lambda i, w: (0, layer, 0, 0, 0)),
                whole(stream.shape),
                pl.BlockSpec((3, width), lambda i, w: (0, w[2])),
            ],
            out_specs=whole(stream.shape),
        ),
        out_shape=jax.ShapeDtypeStruct(stream.shape, F32),
        compiler_params=params(),
        cost_estimate=pl.CostEstimate(
            flops=2 * rows * count * heads_width * width,
            bytes_accessed=2 * count * heads_width * (rows + width) + 8 * rows * width,
            transcendentals=0,
        ),
        name="finish",
    )(where, parts, weight, stream, mod)


def on_device(tokens, block_mask, space_qkv, space_out, space_mod, time_qkv, time_out, time_mod):
    videos, rows, width = tokens.shape
    parts = lax.axis_size("fsdp")
    seq_count = lax.axis_size("seq")
    frames = seq_count // 2
    seq_index = lax.axis_index("seq")
    where = jnp.stack([seq_index // 2, seq_index % 2, lax.axis_index("fsdp")]).astype(jnp.int32)
    same_half = [[2 * frame + half for frame in range(frames)] for half in range(2)]

    def across_frames(values):
        return lax.all_to_all(
            values.reshape(frames, rows // frames, -1), "seq", split_axis=0, concat_axis=0,
            tiled=True, axis_index_groups=same_half,
        ).reshape(rows, -1)

    def across_parts(values):
        return lax.all_to_all(values, "fsdp", split_axis=0, concat_axis=0, tiled=True)

    local = tokens.reshape(rows, width)
    wide = across_parts(pack(where, local, space_out, time_out))
    lines = lax.all_gather(wide[:, rows : rows + LINES, :], "seq", axis=0, tiled=False)
    lines = lines.reshape(frames, 2, parts, LINES, width)
    queries, own = space_in(wide, space_mod, jnp.swapaxes(space_qkv, 0, 1), rows)
    other = lax.ppermute(own, "seq", [(i, i ^ 1) for i in range(seq_count)])
    partial = space_attend(where, block_mask.reshape(-1), queries, own, other, space_out, parts)
    stream, sent = join(where, across_parts(partial), local, space_mod)
    wide = across_parts(repack(across_frames(sent), parts))
    attended = time_layer(wide, time_mod, jnp.swapaxes(time_qkv, 0, 1), rows, frames)
    attended = across_frames(attended)
    attended = across_parts(jnp.broadcast_to(attended[None], (parts,) + attended.shape))
    return finish(1, where, attended, lines, stream, time_mod).reshape(tokens.shape)


def solution(mesh):
    placed = (
        P(None, "seq", "fsdp"),
        P(),
        P(None, None, "fsdp"),
        P("fsdp", None),
        P(),
        P(None, None, "fsdp"),
        P("fsdp", None),
        P(),
    )
    return jax.shard_map(
        on_device, mesh=mesh, in_specs=placed, out_specs=P(None, "seq", "fsdp"), check_vma=False
    )
```

time: 202 us -> 231 us (1.14)
  waiting for transfers between devices: 10.6 us -> 55.2 us
  blocking collectives: 156 us -> 114 us
  between operations: 0.16 us -> 13.5 us
  local copies, waits for them, and re-layouts: 0.74 us -> 13 us
  starting transfers between devices: 5.38 us -> 8.21 us
    all_to_all x3 -> x2, blocking collectives: 89.9 us -> 38.8 us  [across_frames(): lax.all_to_all(values.reshape(frames, rows // frames, -1), 'seq', split_a...]
    all_to_all x1 -> x2, waiting for transfers between devices: 9.24 us -> 55.2 us  [across_parts(): lax.all_to_all(values, 'fsdp', split_axis=0, concat_axis=0, tiled=True)]
    unnamed x13 -> x25, local copies, waits for them, and re-layouts: 0.15 us -> 10.1 us
    all_to_all x2, blocking collectives: 66.3 us -> 74.8 us  [across_parts(): lax.all_to_all(values, 'fsdp', split_axis=0, concat_axis=0, tiled=True)]
    pallas_call x3 -> x5, Pallas kernels: 21.6 us -> 18.8 us  [the longest x1 8.39 us: time_layer(): pl.pallas_call(functools.partial(time_kernel, frames), grid=grid, in_spec...]
    all_to_all x1 -> x2, starting transfers between devices: 5.29 us -> 8.07 us  [across_parts(): lax.all_to_all(values, 'fsdp', split_axis=0, concat_axis=0, tiled=True)]
    pallas_call x1, Pallas kernels: 1.22 us -> 3.67 us  [join(): pl.pallas_call(join_kernel, grid_spec=pltpu.PrefetchScalarGridSpec(num_sc...]
  transfers between devices with their start and end apart: 2 -> 4, of which waited for: 2 -> 2; matrix products, arithmetic and copies ran while one was open for 0% -> 2% of each run, Pallas kernels for 0% -> 5%
where the time goes in v2:
time: 231 us; the launch traced here: 230 us
  blocking collectives  114 us (49%)
  waiting for transfers between devices  55.2 us (24%)
  Pallas kernels  26.2 us (11%)
  between operations  13.5 us (6%)
  local copies, waits for them, and re-layouts  13 us (6%)
  starting transfers between devices  8.21 us (4%)
    all_to_all x2, blocking collectives, across_parts(): lax.all_to_all(values, 'fsdp', split_axis=0, concat_axis=0, tiled=True)  74.8 us
    all_to_all x2, waiting for transfers between devices, across_parts(): lax.all_to_all(values, 'fsdp', split_axis=0, concat_axis=0, tiled=True)  55.2 us
    all_to_all x2, blocking collectives, across_frames(): lax.all_to_all(values.reshape(frames, rows // frames, -1), 'seq', split_a...  38.8 us
    unnamed x25, local copies, waits for them, and re-layouts  10.1 us
    pallas_call x1, Pallas kernels, time_layer(): pl.pallas_call(functools.partial(time_kernel, frames), grid=grid, in_spec...  8.39 us
    all_to_all x2, starting transfers between devices, across_parts(): lax.all_to_all(values, 'fsdp', split_axis=0, concat_axis=0, tiled=True)  8.07 us
    pallas_call x1, Pallas kernels, space_in(): pl.pallas_call(space_in_kernel, grid=grid, in_specs=in_specs, out_specs=[...  6.88 us
  transfers between devices with their start and end apart: 4, of which 2 were waited for; matrix products, arithmetic and copies ran while one was open for 2% of the time, Pallas kernels for 5%

profile of v2, /device:TPU:32, one launch (start us, length us, event | category | flops | bytes accessed | tf_op | source)
XLA Modules:
  0.0 229.8 jit_solution(10531373674720868407)
XLA Ops:
  6.6 1.4 copy-done.1
  8.0 1.1 copy-done.5
  9.1 1.4 copy-done.7
  10.5 1.0 pack.1
  11.5 39.9 %all_to_all.30.parts_ref.stats_ref = bf16[8,408,384]{2,1,0:T(8,128)(2,1)S(1)} all-to-all(bf16[8,408,384]{2,1,0:T(8,128)(2,1)S(1)} %pack.1), channel_id=1, replica_groups=mesh['seq'=32,'fsdp'=8] {'fsdp'}, dimensions={0} | all-to-all | bytes 5013504 | tf_op jit(solution)/shard_map/all_to_all | solution.py:434
  51.4 6.9 %space_in.1 = (bf16[384,256]{1,0:T(8,128)(2,1)S(1)}, bf16[384,512]{1,0:T(8,128)(2,1)S(1)}) custom-call(bf16[8,408,384]{2,1,0:T(8,128)(2,1)S(1)} %all_to_all.30.parts_ref.stats_ref, bf16[8,408,384]{2,1,0:T(8,128)(2,1)S(1)} %all_to_all.30.parts_ref.stats_ref, f32[3,3072]{1,0:T(4,128)S(1)} %copy-done.9, bf16[3,3072,256]{2,1,0:T(8,128)(2,1)S(1)} %bitcast.12), custom_call_target="tpu_custom_call" | custom-call | flops 1811939328 | bytes 7077888 | tf_op jit(solution)/shard_map/space_in/pallas_call | solution.py:203
  58.3 1.5 copy.10
  59.8 1.0 reshape.22.mask_ref
  60.8 1.4 copy-done.2
  62.2 3.7 %space_attend.1 = bf16[8,384,384]{2,1,0:T(8,128)(2,1)S(1)} custom-call(s32[3]{0:T(128)S(1)} %pad_add_fusion.where_ref, s32[576]{0:T(1024)S(1)} %reshape.22.mask_ref, bf16[384,256]{1,0:T(8,128)(2,1)S(1)} %get-tuple-element.9.q_ref, bf16[384,512]{1,0:T(8,128)(2,1)S(1)} %get-tuple-element.10.own_ref, bf16[384,512]{1,0:T(8,128)(2,1)S(1)} %collective-permute-done.other_ref, ...), custom_call_target="tpu_custom_call" | custom-call | flops 905969664 | bytes 4915200 | tf_op jit(solution)/shard_map/space_attend/pallas_call | solution.py:271
  65.9 1.4 copy-done
  67.3 4.5 %all-to-all-start.1 = ((bf16[8,384,384]{2,1,0:T(8,128)(2,1)}), bf16[8,384,384]{2,1,0:T(8,128)(2,1)}, u32[]{:S(2)}, u32[]{:S(2)}) async-start(bf16[8,384,384]{2,1,0:T(8,128)(2,1)} %copy-done), calls=%async_computation.1 | async-start | bytes 4718592 | tf_op jit(solution)/shard_map/all_to_all | solution.py:434
  71.9 0.7 slice.4
  72.6 35.2 %all-to-all-done.1.parts_ref = bf16[8,384,384]{2,1,0:T(8,128)(2,1)} async-done(((bf16[8,384,384]{2,1,0:T(8,128)(2,1)}), bf16[8,384,384]{2,1,0:T(8,128)(2,1)}, u32[]{:S(2)}, u32[]{:S(2)}) %all-to-all-start.1) | async-done | bytes 2359328 | tf_op jit(solution)/shard_map/all_to_all | solution.py:434
  107.7 3.7 %join.1 = (f32[384,384]{1,0:T(8,128)S(1)}, bf16[384,512]{1,0:T(8,128)(2,1)S(1)}) custom-call(s32[3]{0:T(128)S(1)} %pad_add_fusion.where_ref, bf16[8,384,384]{2,1,0:T(8,128)(2,1)} %all-to-all-done.1.parts_ref, f32[384,384]{1,0:T(8,128)S(1)} %bitcast.18, f32[3,3072]{1,0:T(4,128)S(1)} %copy-done.9), custom_call_target="tpu_custom_call" | custom-call | tf_op jit(solution)/shard_map/join/pallas_call | solution.py:309
  111.4 23.9 %all_to_all.31 = bf16[16,24,512]{2,1,0:T(8,128)(2,1)S(1)} all-to-all(bf16[16,24,512]{2,1,0:T(8,128)(2,1)S(1)} %bitcast.21), channel_id=1, replica_groups={{0,16,32,48,64,80,96,112,128,144,160,176,192,208,224,240},{8,24,40,56,7..., dimensions={0} | all-to-all | bytes 786432 | tf_op jit(solution)/shard_map/all_to_all | solution.py:428
  135.6 34.9 %all_to_all.32.parts_ref.stats_ref = bf16[8,392,384]{2,1,0:T(8,128)(2,1)S(1)} all-to-all(bf16[8,392,384]{2,1,0:T(8,128)(2,1)S(1)} %repack.1), channel_id=1, replica_groups=mesh['seq'=32,'fsdp'=8] {'fsdp'}, dimensions={0} | all-to-all | bytes 4816896 | tf_op jit(solution)/shard_map/all_to_all | solution.py:434
  170.5 8.4 %time_layer.1 = bf16[384,256]{1,0:T(8,128)(2,1)S(1)} custom-call(bf16[8,392,384]{2,1,0:T(8,128)(2,1)S(1)} %all_to_all.32.parts_ref.stats_ref, bf16[8,392,384]{2,1,0:T(8,128)(2,1)S(1)} %all_to_all.32.parts_ref.stats_ref, f32[3,3072]{1,0:T(4,128)S(1)} %copy-done.8, bf16[3,3072,256]{2,1,0:T(8,128)(2,1)S(1)} %bitcast.15), custom_call_target="tpu_custom_call" | custom-call | flops 1811939328 | bytes 7077888 | tf_op jit(solution)/shard_map/time_layer/pallas_call | solution.py:368
  178.9 14.9 %all_to_all.33 = bf16[16,24,256]{2,1,0:T(8,128)(2,1)S(1)} all-to-all(bf16[16,24,256]{2,1,0:T(8,128)(2,1)S(1)} %bitcast.20), channel_id=1, replica_groups={{0,16,32,48,64,80,96,112,128,144,160,176,192,208,224,240},{8,24,40,56,7..., dimensions={0} | all-to-all | bytes 393216 | tf_op jit(solution)/shard_map/all_to_all | solution.py:428
  193.8 1.3 broadcast_in_dim.8
  195.1 3.6 %all-to-all-start.5 = ((bf16[8,384,256]{2,1,0:T(8,128)(2,1)}), bf16[8,384,256]{2,1,0:T(8,128)(2,1)S(1)}, u32[]{:S(2)}, u32[]{:S(2)}) async-start(bf16[8,384,256]{2,1,0:T(8,128)(2,1)} %broadcast_in_dim.8), calls=%async_computation.5 | async-start | bytes 3145728 | tf_op jit(solution)/shard_map/all_to_all | solution.py:434
  198.7 20.0 %all-to-all-done.5.parts_ref = bf16[8,384,256]{2,1,0:T(8,128)(2,1)S(1)} async-done(((bf16[8,384,256]{2,1,0:T(8,128)(2,1)}), bf16[8,384,256]{2,1,0:T(8,128)(2,1)S(1)}, u32[]{:S(2)}, u32[]{:S(2)}) %all-to-all-start.5) | async-done | bytes 1572896 | tf_op jit(solution)/shard_map/all_to_all | solution.py:434
  218.7 1.9 copy-done.4
  220.6 2.4 %finish.1 = f32[384,384]{1,0:T(8,128)} custom-call(s32[3]{0:T(128)S(1)} %pad_add_fusion.where_ref, bf16[8,384,256]{2,1,0:T(8,128)(2,1)S(1)} %all-to-all-done.5.parts_ref, bf16[16,2,8,16,384]{4,3,2,1,0:T(8,128)(2,1)S(1)} %bitcast.16, f32[384,384]{1,0:T(8,128)S(1)} %get-tuple-element.12.stream_ref, f32[3,3072]{1,0:T(4,128)S(1)} %copy-done.8), custom_call_target="tpu_custom_call" | custom-call | flops 603979776 | bytes 4325376 | tf_op jit(solution)/shard_map/finish/pallas_call | solution.py:394
  (26 shorter events, 0.5 us)
Async XLA Ops:
  6.6 1.4 copy-start.1
  8.0 1.1 copy-start.5
  9.1 1.4 copy-start.7
  11.5 39.9 %copy-start.3 = (bf16[3072,3,256]{2,0,1:T(8,128)(2,1)S(1)}, bf16[3072,3,256]{2,0,1:T(8,128)(2,1)}, u32[]{:S(2)}) copy-start(bf16[3072,3,256]{2,0,1:T(8,128)(2,1)} %param.10) | copy-start | bytes 14155780
  11.5 39.9 %copy-start.9 = (f32[3,3072]{1,0:T(4,128)S(1)}, f32[3,3072]{1,0:T(4,128)}, u32[]{:S(2)}) copy-start(f32[3,3072]{1,0:T(4,128)} %mod_ref.5) | copy-start | bytes 110596
  58.2 2.6 %collective-permute-start = (bf16[384,512]{1,0:T(8,128)(2,1)S(1)}, bf16[384,512]{1,0:T(8,128)(2,1)S(1)}, u32[]{:S(2)}, u32[]{:S(2)}) collective-permute-start(bf16[384,512]{1,0:T(8,128)(2,1)S(1)} %get-tuple-element.10.own_ref), channel_id=1, source_target_pairs={{0,8},{8,0},{16,24},{24,16},{32,40},{40,32},{48,56},{56,48},{64,72... | collective-permute-start | bytes 1179656 | tf_op jit(solution)/shard_map/ppermute | solution.py:441
  60.8 1.4 copy-start.2
  65.9 1.4 copy-start
  67.3 40.4 %copy-start.6 = (f32[1,384,384]{2,1,0:T(8,128)S(1)}, f32[1,384,384]{2,1,0:T(8,128)}, u32[]{:S(2)}) copy-start(f32[1,384,384]{2,1,0:T(8,128)} %param.8) | copy-start | bytes 1769476
  67.3 40.4 %all-to-all-start.1 = ((bf16[8,384,384]{2,1,0:T(8,128)(2,1)}), bf16[8,384,384]{2,1,0:T(8,128)(2,1)}, u32[]{:S(2)}, u32[]{:S(2)}) async-start(bf16[8,384,384]{2,1,0:T(8,128)(2,1)} %copy-done), calls=%async_computation.1 | async-start | bytes 4718592 | tf_op jit(solution)/shard_map/all_to_all | solution.py:434
  71.8 126.8 %all-gather.3.cloned.1.call-start = ((), (), s32[]{:S(2)}) async-start(), calls=%async_computation.6 | async-start | bytes 3244032 | tf_op jit(solution)/shard_map/all_gather | solution.py:438
  107.7 62.8 %slice-start = ((s8[4718592]{0:T(1024)(128)(4,1)}), s8[4194304]{0:T(1024)(128)(4,1)S(1)}, s32[]{:S(2)}) async-start(s8[4718592]{0:T(1024)(128)(4,1)} %bitcast.13), calls=%async_computation.7 | async-start | bytes 8388608
  135.3 35.2 %slice-start.1 = ((s8[4718592]{0:T(1024)(128)(4,1)}), s8[524288]{0:T(1024)(128)(4,1)S(1)}, s32[]{:S(2)}) async-start(s8[4718592]{0:T(1024)(128)(4,1)} %bitcast.13), calls=%async_computation.8 | async-start | bytes 1048576
  135.6 34.9 %copy-start.8 = (f32[3,3072]{1,0:T(4,128)S(1)}, f32[3,3072]{1,0:T(4,128)}, u32[]{:S(2)}) copy-start(f32[3,3072]{1,0:T(4,128)} %mod_ref.7) | copy-start | bytes 110596
  195.1 23.6 %all-to-all-start.5 = ((bf16[8,384,256]{2,1,0:T(8,128)(2,1)}), bf16[8,384,256]{2,1,0:T(8,128)(2,1)S(1)}, u32[]{:S(2)}, u32[]{:S(2)}) async-start(bf16[8,384,256]{2,1,0:T(8,128)(2,1)} %broadcast_in_dim.8), calls=%async_computation.5 | async-start | bytes 3145728 | tf_op jit(solution)/shard_map/all_to_all | solution.py:434
  218.7 1.9 copy-start.4
Sparse Core Ops, SparseCore 0:
  74.5 78.1 all-gather.2

commit v3 on v2

--- a/solution.py
+++ b/solution.py
@@ -12,10 +12,10 @@
 BLOCK = 128
 EPS = 1e-06
 SCALE = 1.0 / math.sqrt(HD)
-VMEM_LIMIT = 32 * 1024 * 1024
+VMEM_LIMIT = 48 * 1024 * 1024
 F32 = jnp.float32
 BF16 = jnp.bfloat16
-LINES = 16
+STAT_ROWS = 8
 
 
 def whole(shape):
@@ -51,43 +51,34 @@
     return centred.astype(BF16), table
 
 
-def pack_kernel(where_ref, tokens_ref, space_ref, time_ref, out_ref):
-    parts, _, width = out_ref.shape
+def pack_kernel(tokens_ref, out_ref):
+    parts, total_rows, _ = out_ref.shape
     rows = tokens_ref.shape[0]
     centred, table = centre(tokens_ref[...])
-    stats = jnp.transpose(table)[:8].astype(BF16)
-    second = jnp.full(space_ref.shape, where_ref[1], jnp.int32) == 1
-    lines = jnp.where(second, time_ref[...].astype(F32), space_ref[...].astype(F32)).astype(BF16)
+    stats = jnp.transpose(table)[: total_rows - rows].astype(BF16)
     for part in range(parts):
         out_ref[part, :rows, :] = centred
-        out_ref[part, rows : rows + LINES, :] = lines[:, part * width : (part + 1) * width]
-        out_ref[part, rows + LINES :, :] = stats
-
-
-def pack(where, tokens, space_out, time_out):
+        out_ref[part, rows:, :] = stats
+
+
+def pack(tokens, parts):
     rows, width = tokens.shape
-    model_width = space_out.shape[1]
-    parts = model_width // width
-    line_spec = pl.BlockSpec((LINES, model_width), lambda i, w: (w[0], 0))
-    shape = (parts, rows + LINES + 8, width)
+    shape = (parts, rows + STAT_ROWS, width)
     return pl.pallas_call(
         pack_kernel,
-        grid_spec=pltpu.PrefetchScalarGridSpec(
-            num_scalar_prefetch=1,
-            grid=(1,),
-            in_specs=[whole(tokens.shape), line_spec, line_spec],
-            out_specs=whole(shape),
-        ),
+        grid=(1,),
+        in_specs=[whole(tokens.shape)],
+        out_specs=whole(shape),
         out_shape=jax.ShapeDtypeStruct(shape, BF16),
         compiler_params=params(),
         name="pack",
-    )(where, tokens, space_out, time_out)
+    )(tokens)
 
 
 def repack_kernel(arrived_ref, out_ref):
     parts, _, width = out_ref.shape
     rows = arrived_ref.shape[0]
-    stats = jnp.transpose(arrived_ref[:, width:].astype(F32))[:8].astype(BF16)
+    stats = jnp.transpose(arrived_ref[:, width:].astype(F32))[:STAT_ROWS].astype(BF16)
     for part in range(parts):
         out_ref[part, :rows, :] = arrived_ref[:, :width]
         out_ref[part, rows:, :] = stats
@@ -95,7 +86,7 @@
 
 def repack(arrived, parts):
     rows, width = arrived.shape
-    shape = (parts, rows + 8, width - 128)
+    shape = (parts, rows + STAT_ROWS, width - 128)
     return pl.pallas_call(
         repack_kernel,
         grid=(1,),
@@ -107,77 +98,130 @@
     )(arrived)
 
 
-def row_stats(stats_ref, offset_ref, scale_ref, width):
-    parts = stats_ref.shape[0]
-    means, squares = [], 0.0
+def fold_kernel(mod_ref, weight_ref, folded_ref, offset_ref, shift_ref, gain_sums_ref, shift_sums_ref):
+    step, last = pl.program_id(0), pl.num_programs(0) - 1
+    _, width, heads_width = weight_ref.shape
+    shift = mod_ref[0:1, :]
+    gain = 1.0 + mod_ref[1:2, :]
+    columns = jnp.transpose(jnp.broadcast_to(gain, (128, width)))
+    line = lax.broadcasted_iota(jnp.int32, (16, width), 0)
+    lines = jnp.zeros((16, width), F32)
+    for index, entry in enumerate(bf16_terms(gain, 2) + bf16_terms(shift, 2)):
+        lines = jnp.where(line == index, entry, lines)
+    lines = lines.astype(BF16)
+
+    @pl.when(step == 0)
+    def _():
+        shift_sums_ref[...] = jnp.zeros_like(shift_sums_ref)
+
+    for part in range(3):
+        base = part * heads_width
+        for start in range(0, heads_width, 128):
+            chunk = weight_ref[part, :, start : start + 128].astype(F32)
+            folded_ref[part, :, start : start + 128] = (chunk * columns).astype(BF16)
+        sums = jnp.dot(lines, weight_ref[part], preferred_element_type=F32)
+        gain_sums_ref[pl.ds(step, 1), base : base + heads_width] = sums[0:1] + sums[1:2]
+        shift_sums_ref[:, base : base + heads_width] += jnp.broadcast_to(
+            sums[2:3] + sums[3:4], (8, heads_width)
+        )
+
+    @pl.when(step == last)
+    def _():
+        high, low = bf16_terms(gain_sums_ref[...], 2)
+        rest = jnp.zeros((128 - 3 * high.shape[0], high.shape[1]), F32)
+        offset_ref[...] = jnp.concatenate([high, high, low, rest], axis=0).astype(BF16)
+        shift_ref[...] = shift_sums_ref[...]
+
+
+def fold(mod, weight, parts):
+    _, model_width, heads_width = weight.shape
+    width = model_width // parts
+    packed_width = 3 * heads_width
+    block = pl.BlockSpec((3, width, heads_width), lambda k: (0, k, 0))
+    return pl.pallas_call(
+        fold_kernel,
+        grid=(parts,),
+        in_specs=[pl.BlockSpec((3, width), lambda k: (0, k)), block],
+        out_specs=[block, whole((128, packed_width)), whole((8, packed_width))],
+        out_shape=[
+            jax.ShapeDtypeStruct(weight.shape, BF16),
+            jax.ShapeDtypeStruct((128, packed_width), BF16),
+            jax.ShapeDtypeStruct((8, packed_width), F32),
+        ],
+        scratch_shapes=[pltpu.VMEM((parts, packed_width), F32), pltpu.VMEM((8, packed_width), F32)],
+        compiler_params=params(),
+        cost_estimate=pl.CostEstimate(
+            flops=32 * weight.size, bytes_accessed=4 * weight.size, transcendentals=0
+        ),
+        name="fold",
+    )(mod, weight)
+
+
+def row_table(stats_ref, width):
+    parts, _, rows = stats_ref.shape
+    line = lax.broadcasted_iota(jnp.int32, (parts, rows), 0)
+    means = jnp.zeros((parts, rows), F32)
+    squares = 0.0
     for part in range(parts):
         lines = stats_ref[part].astype(F32)
-        means.append(lines[0:1] + lines[1:2] + lines[2:3])
+        means = jnp.where(line == part, lines[0:1] + lines[1:2] + lines[2:3], means)
         squares = squares + (lines[3:4] + lines[4:5])
-    mean = sum(means) / parts
-    offsets = [part_mean - mean for part_mean in means]
-    between = sum(offset * offset for offset in offsets) * width
+    offsets = means - jnp.sum(means, axis=0, keepdims=True) / parts
+    between = jnp.sum(offsets * offsets, axis=0, keepdims=True) * width
     scale = lax.rsqrt((squares + between) / (parts * width) + EPS)
-    rows = mean.shape[1]
-    line = lax.broadcasted_iota(jnp.int32, (128, rows), 0)
-    table = jnp.zeros((128, rows), F32)
-    for index, entry in enumerate(offsets + [scale]):
-        table = jnp.where(line == index, entry, table)
-    table = jnp.transpose(table)
-    for part in range(parts):
-        offset_ref[part] = jnp.broadcast_to(table[:, part : part + 1], (rows, 128))
-    scale_ref[...] = jnp.broadcast_to(table[:, parts : parts + 1], (rows, 128))
-
-
-def accumulate_qkv(parts_ref, stats_ref, mod_ref, weight_ref, acc_ref, offset_ref, scale_ref):
-    step = pl.program_id(0)
+    high, low = bf16_terms(offsets, 2)
+    scales = jnp.broadcast_to(scale, (128 - 3 * parts, rows))
+    return jnp.transpose(jnp.concatenate([high, low, high, scales], axis=0))
+
+
+def accumulate_qkv(parts_ref, stats_ref, weight_ref, offset_ref, shift_ref, acc_ref, table_ref):
+    step, last = pl.program_id(0), pl.num_programs(0) - 1
     pair, rows, width = parts_ref.shape
+    heads_width = weight_ref.shape[2]
 
     @pl.when(step == 0)
     def _():
-        row_stats(stats_ref, offset_ref, scale_ref, width)
-
-    scale = scale_ref[...]
-    pieces = []
-    for index in range(pair):
-        offset = offset_ref[step * pair + index]
-        for start in range(0, width, 128):
-            columns = slice(index * width + start, index * width + start + 128)
-            values = parts_ref[index, :, start : start + 128].astype(F32)
-            shift = mod_ref[0:1, columns]
-            gain = 1.0 + mod_ref[1:2, columns]
-            pieces.append((((values + offset) * scale) * gain + shift).astype(BF16))
-    normed = jnp.concatenate(pieces, axis=1)
-    heads_width = weight_ref.shape[2]
+        table_ref[...] = row_table(stats_ref, width)
+
+    values = jnp.concatenate([parts_ref[index] for index in range(pair)], axis=1)
     for part in range(3):
-        product = jnp.dot(normed, weight_ref[part], preferred_element_type=F32)
+        product = jnp.dot(values, weight_ref[part], preferred_element_type=F32)
         columns = slice(part * heads_width, (part + 1) * heads_width)
 
         @pl.when(step == 0)
         def _():
-            acc_ref[:, columns] = product
+            terms = jnp.where(
+                lax.broadcasted_iota(jnp.int32, (rows, 128), 1) < 3 * stats_ref.shape[0], table_ref[...], 0.0
+            ).astype(BF16)
+            acc_ref[:, columns] = product + jnp.dot(
+                terms, offset_ref[:, columns], preferred_element_type=F32
+            )
 
         @pl.when(step > 0)
         def _():
             acc_ref[:, columns] += product
 
-
-def qkv_specs(parts, rows, width, heads_width):
-    count, total_rows, _ = parts.shape
+    @pl.when(step == last)
+    def _():
+        scale = jnp.broadcast_to(table_ref[:, 127:128], (rows, 128))
+        for start in range(0, 3 * heads_width, 128):
+            columns = slice(start, start + 128)
+            acc_ref[:, columns] = acc_ref[:, columns] * scale + shift_ref[0:1, columns]
+
+
+def qkv_specs(parts, rows, heads_width):
+    count, total_rows, width = parts.shape
     pair = 2 if count % 2 == 0 else 1
-    last = total_rows // 8 - 1
+    last = total_rows // STAT_ROWS - 1
     grid = (count // pair,)
     in_specs = [
         pl.BlockSpec((pair, rows, width), lambda k: (k, 0, 0)),
-        pl.BlockSpec((count, 8, width), lambda k: (0, last, 0)),
-        pl.BlockSpec((3, pair * width), lambda k: (0, k)),
+        pl.BlockSpec((count, STAT_ROWS, width), lambda k: (0, last, 0)),
         pl.BlockSpec((3, pair * width, heads_width), lambda k: (0, k, 0)),
+        whole((128, 3 * heads_width)),
+        whole((8, 3 * heads_width)),
     ]
-    scratch = [
-        pltpu.VMEM((rows, 3 * heads_width), F32),
-        pltpu.VMEM((count, rows, 128), F32),
-        pltpu.VMEM((rows, 128), F32),
-    ]
+    scratch = [pltpu.VMEM((rows, 3 * heads_width), F32), pltpu.VMEM((rows, 128), F32)]
     cost = pl.CostEstimate(
         flops=2 * rows * count * width * 3 * heads_width,
         bytes_accessed=2 * count * width * (rows + 3 * heads_width),
@@ -186,9 +230,9 @@
     return grid, in_specs, scratch, cost
 
 
-def space_in_kernel(parts_ref, stats_ref, mod_ref, weight_ref, q_ref, kv_ref, *scratch):
-    accumulate_qkv(parts_ref, stats_ref, mod_ref, weight_ref, *scratch)
-    acc_ref = scratch[0]
+def space_in_kernel(parts_ref, stats_ref, weight_ref, offset_ref, shift_ref, q_ref, kv_ref,
+                    acc_ref, table_ref):
+    accumulate_qkv(parts_ref, stats_ref, weight_ref, offset_ref, shift_ref, acc_ref, table_ref)
 
     @pl.when(pl.program_id(0) == pl.num_programs(0) - 1)
     def _():
@@ -197,9 +241,9 @@
         kv_ref[...] = acc_ref[:, width:].astype(BF16)
 
 
-def space_in(parts, mod, weight, rows):
-    width, heads_width = parts.shape[2], weight.shape[2]
-    grid, in_specs, scratch, cost = qkv_specs(parts, rows, width, heads_width)
+def space_in(parts, folded, rows):
+    heads_width = folded[0].shape[2]
+    grid, in_specs, scratch, cost = qkv_specs(parts, rows, heads_width)
     return pl.pallas_call(
         space_in_kernel,
         grid=grid,
@@ -213,7 +257,7 @@
         compiler_params=params(),
         cost_estimate=cost,
         name="space_in",
-    )(parts, parts, mod, weight)
+    )(parts, parts, *folded)
 
 
 def project_out(attended, weight_ref, out_ref):
@@ -330,9 +374,30 @@
     )(where, parts, tokens, mod)
 
 
-def time_kernel(frames, parts_ref, stats_ref, mod_ref, weight_ref, out_ref, att_ref, *scratch):
-    accumulate_qkv(parts_ref, stats_ref, mod_ref, weight_ref, *scratch)
-    acc_ref = scratch[0]
+def total_kernel(parts_ref, out_ref):
+    total = parts_ref[0].astype(F32)
+    for part in range(1, parts_ref.shape[0]):
+        total += parts_ref[part].astype(F32)
+    out_ref[...] = total.astype(BF16)
+
+
+def total_of(parts):
+    count, rows, width = parts.shape
+    tile = BLOCK
+    return pl.pallas_call(
+        total_kernel,
+        grid=(rows // tile,),
+        in_specs=[pl.BlockSpec((count, tile, width), lambda i: (0, i, 0))],
+        out_specs=pl.BlockSpec((tile, width), lambda i: (i, 0)),
+        out_shape=jax.ShapeDtypeStruct((rows, width), BF16),
+        compiler_params=params(),
+        name="total_of",
+    )(parts)
+
+
+def time_kernel(frames, parts_ref, stats_ref, weight_ref, offset_ref, shift_ref, out_weight_ref, out_ref,
+                att_ref, acc_ref, table_ref):
+    accumulate_qkv(parts_ref, stats_ref, weight_ref, offset_ref, shift_ref, acc_ref, table_ref)
 
     @pl.when(pl.program_id(0) == pl.num_programs(0) - 1)
     def _():
@@ -359,60 +424,25 @@
                 norm = jnp.sum(lifted, axis=1, keepdims=True)
                 mixed = jnp.dot(lifted.astype(BF16), value, preferred_element_type=F32) / norm
                 att_ref[:, start : start + group, low : low + HD] = mixed.reshape(frames, group, HD)
-        out_ref[...] = att_ref[...].reshape(rows, heads_width).astype(BF16)
-
-
-def time_layer(parts, mod, weight, rows, frames):
-    width, heads_width = parts.shape[2], weight.shape[2]
-    grid, in_specs, scratch, cost = qkv_specs(parts, rows, width, heads_width)
+        attended = att_ref[...].reshape(rows, heads_width).astype(BF16)
+        project_out(attended, out_weight_ref, out_ref)
+
+
+def time_layer(parts, folded, out_weight, rows, frames):
+    count, _, width = parts.shape
+    heads_width = folded[0].shape[2]
+    grid, in_specs, scratch, cost = qkv_specs(parts, rows, heads_width)
     return pl.pallas_call(
         functools.partial(time_kernel, frames),
         grid=grid,
-        in_specs=in_specs,
-        out_specs=whole((rows, heads_width)),
-        out_shape=jax.ShapeDtypeStruct((rows, heads_width), BF16),
+        in_specs=in_specs + [whole(out_weight.shape)],
+        out_specs=whole((count, rows, width)),
+        out_shape=jax.ShapeDtypeStruct((count, rows, width), BF16),
         scratch_shapes=[pltpu.VMEM((frames, rows // frames, heads_width), F32)] + scratch,
         compiler_params=params(),
         cost_estimate=cost,
         name="time_layer",
-    )(parts, parts, mod, weight)
-
-
-def finish_kernel(where_ref, parts_ref, weight_ref, stream_ref, mod_ref, out_ref):
-    count, rows, heads_width = parts_ref.shape
-    width = out_ref.shape[1]
-    total = jnp.zeros((rows, width), F32)
-    for part in range(count):
-        lines = weight_ref[:, 0, part].reshape(heads_width, width)
-        total += jnp.dot(parts_ref[part], lines, preferred_element_type=F32)
-    out_ref[...] = stream_ref[...] + mod_ref[2:3, :] * total
-
-
-def finish(layer, where, parts, weight, stream, mod):
-    count, rows, heads_width = parts.shape
-    frames, layers, _, lines, width = weight.shape
-    return pl.pallas_call(
-        finish_kernel,
-        grid_spec=pltpu.PrefetchScalarGridSpec(
-            num_scalar_prefetch=1,
-            grid=(1,),
-            in_specs=[
-                whole(parts.shape),
-                pl.BlockSpec((frames, 1, count, lines, width), lambda i, w: (0, layer, 0, 0, 0)),
-                whole(stream.shape),
-                pl.BlockSpec((3, width), lambda i, w: (0, w[2])),
-            ],
-            out_specs=whole(stream.shape),
-        ),
-        out_shape=jax.ShapeDtypeStruct(stream.shape, F32),
-        compiler_params=params(),
-        cost_estimate=pl.CostEstimate(
-            flops=2 * rows * count * heads_width * width,
-            bytes_accessed=2 * count * heads_width * (rows + width) + 8 * rows * width,
-            transcendentals=0,
-        ),
-        name="finish",
-    )(where, parts, weight, stream, mod)
+    )(parts, parts, *folded, out_weight)
 
 
 def on_device(tokens, block_mask, space_qkv, space_out, space_mod, time_qkv, time_out, time_mod):
@@ -434,18 +464,17 @@
         return lax.all_to_all(values, "fsdp", split_axis=0, concat_axis=0, tiled=True)
 
     local = tokens.reshape(rows, width)
-    wide = across_parts(pack(where, local, space_out, time_out))
-    lines = lax.all_gather(wide[:, rows : rows + LINES, :], "seq", axis=0, tiled=False)
-    lines = lines.reshape(frames, 2, parts, LINES, width)
-    queries, own = space_in(wide, space_mod, jnp.swapaxes(space_qkv, 0, 1), rows)
+    space_folded = fold(space_mod, jnp.swapaxes(space_qkv, 0, 1), parts)
+    time_folded = fold(time_mod, jnp.swapaxes(time_qkv, 0, 1), parts)
+    queries, own = space_in(across_parts(pack(local, parts)), space_folded, rows)
     other = lax.ppermute(own, "seq", [(i, i ^ 1) for i in range(seq_count)])
     partial = space_attend(where, block_mask.reshape(-1), queries, own, other, space_out, parts)
     stream, sent = join(where, across_parts(partial), local, space_mod)
     wide = across_parts(repack(across_frames(sent), parts))
-    attended = time_layer(wide, time_mod, jnp.swapaxes(time_qkv, 0, 1), rows, frames)
-    attended = across_frames(attended)
-    attended = across_parts(jnp.broadcast_to(attended[None], (parts,) + attended.shape))
-    return finish(1, where, attended, lines, stream, time_mod).reshape(tokens.shape)
+    partial_time = time_layer(wide, time_folded, time_out, rows, frames)
+    returned = across_frames(total_of(across_parts(partial_time)))
+    gate = lax.dynamic_slice_in_dim(time_mod[2], lax.axis_index("fsdp") * width, width, 0)
+    return (stream + gate * returned.astype(F32)).reshape(tokens.shape)
 
 
 def solution(mesh):

time: 231 us -> 216 us (0.935)
  blocking collectives: 114 us -> 86.2 us
  between operations: 13.5 us -> 0.16 us
  Pallas kernels: 26.2 us -> 39.3 us
  starting transfers between devices: 8.21 us -> 17.2 us
  waiting for transfers between devices: 55.2 us -> 62.3 us
  local copies, waits for them, and re-layouts: 13 us -> 8.49 us
    all_to_all x2 -> x1, blocking collectives: 38.8 us -> 19.7 us  [across_frames(): lax.all_to_all(values.reshape(frames, rows // frames, -1), 'seq', split_a...]
    pallas_call x2 -> x4, Pallas kernels: 3.34 us -> 15.9 us  [the longest x2 13.8 us: fold(): pl.pallas_call(fold_kernel, grid=(parts,), in_specs=[pl.BlockSpec((3, wid...]
    all_to_all x0 -> x1, waiting for transfers between devices: none -> 9.24 us  [across_frames(): lax.all_to_all(values.reshape(frames, rows // frames, -1), 'seq', split_a...]
    all_to_all x2, blocking collectives: 74.8 us -> 66.5 us  [across_parts(): lax.all_to_all(values, 'fsdp', split_axis=0, concat_axis=0, tiled=True)]
    all_to_all x0 -> x1, starting transfers between devices: none -> 5.47 us  [across_frames(): lax.all_to_all(values.reshape(frames, rows // frames, -1), 'seq', split_a...]
    all_to_all x2, starting transfers between devices: 8.07 us -> 11.7 us  [across_parts(): lax.all_to_all(values, 'fsdp', split_axis=0, concat_axis=0, tiled=True)]
    all_to_all x2, waiting for transfers between devices: 55.2 us -> 51.7 us  [across_parts(): lax.all_to_all(values, 'fsdp', split_axis=0, concat_axis=0, tiled=True)]
    unnamed x25 -> x21, local copies, waits for them, and re-layouts: 10.1 us -> 8.31 us
  transfers between devices with their start and end apart: 4 -> 4, of which waited for: 2 -> 4; matrix products, arithmetic and copies ran while one was open for 2% -> 0% of each run, Pallas kernels for 5% -> 6%
where the time goes in v3:
time: 216 us; the launch traced here: 215 us
  blocking collectives  86.2 us (40%)
  waiting for transfers between devices  62.3 us (29%)
  Pallas kernels  39.3 us (18%)
  starting transfers between devices  17.2 us (8%)
  local copies, waits for them, and re-layouts  8.49 us (4%)
    all_to_all x2, blocking collectives, across_parts(): lax.all_to_all(values, 'fsdp', split_axis=0, concat_axis=0, tiled=True)  66.5 us
    all_to_all x2, waiting for transfers between devices, across_parts(): lax.all_to_all(values, 'fsdp', split_axis=0, concat_axis=0, tiled=True)  51.7 us
    all_to_all x1, blocking collectives, across_frames(): lax.all_to_all(values.reshape(frames, rows // frames, -1), 'seq', split_a...  19.7 us
    pallas_call x2, Pallas kernels, fold(): pl.pallas_call(fold_kernel, grid=(parts,), in_specs=[pl.BlockSpec((3, wid...  13.8 us
    all_to_all x2, starting transfers between devices, across_parts(): lax.all_to_all(values, 'fsdp', split_axis=0, concat_axis=0, tiled=True)  11.7 us
    pallas_call x1, Pallas kernels, time_layer(): pl.pallas_call(functools.partial(time_kernel, frames), grid=grid, in_spec...  9.52 us
    all_to_all x1, waiting for transfers between devices, across_frames(): lax.all_to_all(values.reshape(frames, rows // frames, -1), 'seq', split_a...  9.24 us
    unnamed x21, local copies, waits for them, and re-layouts  8.31 us
  transfers between devices with their start and end apart: 4, of which 4 were waited for; matrix products, arithmetic and copies ran while one was open for 0% of the time, Pallas kernels for 6%

profile of v3, /device:TPU:32, one launch (start us, length us, event | category | flops | bytes accessed | tf_op | source)
XLA Modules:
  0.0 214.6 jit_solution(1365946012388635601)
XLA Ops:
  0.0 1.1 copy-done.3
  1.5 1.5 copy-done
  3.0 7.1 %all-to-all-start = ((bf16[8,392,384]{2,1,0:T(8,128)(2,1)}), bf16[8,392,384]{2,1,0:T(8,128)(2,1)S(1)}, u32[]{:S(2)}, u32[]{:S(2)}) async-start(bf16[8,392,384]{2,1,0:T(8,128)(2,1)} %copy-done), calls=%async_computation | async-start | bytes 4816896 | tf_op jit(solution)/shard_map/all_to_all | solution.py:464
  10.0 6.8 %fold.2 = (bf16[3,3072,256]{2,1,0:T(8,128)(2,1)S(1)}, bf16[128,768]{1,0:T(8,128)(2,1)S(1)}, f32[8,768]{1,0:T(8,128)S(1)}) custom-call(f32[3,3072]{1,0:T(4,128)S(1)} %copy-done.7, bf16[3,3072,256]{2,1,0:T(8,128)(2,1)} %bitcast.18), custom_call_target="tpu_custom_call" | custom-call | flops 75497472 | bytes 9437184 | tf_op jit(solution)/shard_map/fold/pallas_call | solution.py:141
  16.9 2.1 copy-done.2
  19.0 26.6 %all-to-all-done.parts_ref.stats_ref = bf16[8,392,384]{2,1,0:T(8,128)(2,1)S(1)} async-done(((bf16[8,392,384]{2,1,0:T(8,128)(2,1)}), bf16[8,392,384]{2,1,0:T(8,128)(2,1)S(1)}, u32[]{:S(2)}, u32[]{:S(2)}) %all-to-all-start) | async-done | bytes 2408480 | tf_op jit(solution)/shard_map/all_to_all | solution.py:464
  45.6 6.9 %space_in.1 = (bf16[384,256]{1,0:T(8,128)(2,1)S(1)}, bf16[384,512]{1,0:T(8,128)(2,1)S(1)}) custom-call(bf16[8,392,384]{2,1,0:T(8,128)(2,1)S(1)} %all-to-all-done.parts_ref.stats_ref, bf16[8,392,384]{2,1,0:T(8,128)(2,1)S(1)} %all-to-all-done.parts_ref.stats_ref, bf16[3,3072,256]{2,1,0:T(8,128)(2,1)} %copy-done.2, ...), custom_call_target="tpu_custom_call" | custom-call | flops 1811939328 | bytes 7077888 | tf_op jit(solution)/shard_map/space_in/pallas_call | solution.py:247
  52.9 1.3 collective-permute-done.other_ref
  54.3 1.4 copy-done.6
  55.7 3.7 %space_attend.1 = bf16[8,384,384]{2,1,0:T(8,128)(2,1)S(1)} custom-call(s32[3]{0:T(128)S(1)} %pad_add_fusion.where_ref, s32[576]{0:T(1024)S(1)} %reshape.23.mask_ref, bf16[384,256]{1,0:T(8,128)(2,1)S(1)} %get-tuple-element.18.q_ref, bf16[384,512]{1,0:T(8,128)(2,1)S(1)} %get-tuple-element.19.own_ref, bf16[384,512]{1,0:T(8,128)(2,1)S(1)} %collective-permute-done.other_ref, ...), custom_call_target="tpu_custom_call" | custom-call | flops 905969664 | bytes 4915200 | tf_op jit(solution)/shard_map/space_attend/pallas_call | solution.py:315
  59.4 34.3 %all_to_all.30.parts_ref = bf16[8,384,384]{2,1,0:T(8,128)(2,1)S(1)} all-to-all(bf16[8,384,384]{2,1,0:T(8,128)(2,1)S(1)} %space_attend.1), channel_id=1, replica_groups=mesh['seq'=32,'fsdp'=8] {'fsdp'}, dimensions={0} | all-to-all | bytes 4718592 | tf_op jit(solution)/shard_map/all_to_all | solution.py:464
  93.7 1.6 join.1
  95.3 19.7 %all_to_all.31 = bf16[16,24,512]{2,1,0:T(8,128)(2,1)S(1)} all-to-all(bf16[16,24,512]{2,1,0:T(8,128)(2,1)S(1)} %bitcast.17), channel_id=1, replica_groups={{0,16,32,48,64,80,96,112,128,144,160,176,192,208,224,240},{8,24,40,56,7..., dimensions={0} | all-to-all | bytes 786432 | tf_op jit(solution)/shard_map/all_to_all | solution.py:458
  115.0 1.7 repack.1
  116.7 4.6 %all-to-all-start.3 = ((bf16[8,392,384]{2,1,0:T(8,128)(2,1)}), bf16[8,392,384]{2,1,0:T(8,128)(2,1)}, u32[]{:S(2)}, u32[]{:S(2)}) async-start(bf16[8,392,384]{2,1,0:T(8,128)(2,1)} %repack.1), calls=%async_computation.3 | async-start | bytes 4816896 | tf_op jit(solution)/shard_map/all_to_all | solution.py:464
  121.3 7.0 %fold.3 = (bf16[3,3072,256]{2,1,0:T(8,128)(2,1)S(1)}, bf16[128,768]{1,0:T(8,128)(2,1)S(1)}, f32[8,768]{1,0:T(8,128)S(1)}) custom-call(f32[3,3072]{1,0:T(4,128)S(1)} %copy-done.8, bf16[3,3072,256]{2,1,0:T(8,128)(2,1)} %bitcast.19), custom_call_target="tpu_custom_call" | custom-call | flops 75497472 | bytes 9437184 | tf_op jit(solution)/shard_map/fold/pallas_call | solution.py:141
  128.3 2.1 copy-done.1
  130.4 25.1 %all-to-all-done.3.parts_ref.stats_ref = bf16[8,392,384]{2,1,0:T(8,128)(2,1)} async-done(((bf16[8,392,384]{2,1,0:T(8,128)(2,1)}), bf16[8,392,384]{2,1,0:T(8,128)(2,1)}, u32[]{:S(2)}, u32[]{:S(2)}) %all-to-all-start.3) | async-done | bytes 2408480 | tf_op jit(solution)/shard_map/all_to_all | solution.py:464
  155.5 9.5 %time_layer.1 = bf16[8,384,384]{2,1,0:T(8,128)(2,1)S(1)} custom-call(bf16[8,392,384]{2,1,0:T(8,128)(2,1)} %all-to-all-done.3.parts_ref.stats_ref, bf16[8,392,384]{2,1,0:T(8,128)(2,1)} %all-to-all-done.3.parts_ref.stats_ref, bf16[3,3072,256]{2,1,0:T(8,128)(2,1)} %copy-done.1, bf16[128,768]{1,0:T(8,128)(2,1)S(1)} %get-tuple-element.23.offset_ref, ...), custom_call_target="tpu_custom_call" | custom-call | flops 1811939328 | bytes 7077888 | tf_op jit(solution)/shard_map/time_layer/pallas_call | solution.py:435
  165.1 32.2 %all_to_all.32.parts_ref = bf16[8,384,384]{2,1,0:T(8,128)(2,1)S(1)} all-to-all(bf16[8,384,384]{2,1,0:T(8,128)(2,1)S(1)} %time_layer.1), channel_id=1, replica_groups=mesh['seq'=32,'fsdp'=8] {'fsdp'}, dimensions={0} | all-to-all | bytes 4718592 | tf_op jit(solution)/shard_map/all_to_all | solution.py:464
  197.3 1.7 total_of.1
  199.0 5.5 %all-to-all-start.5 = ((bf16[16,24,384]{2,1,0:T(8,128)(2,1)}), bf16[16,24,384]{2,1,0:T(8,128)(2,1)S(1)}, u32[]{:S(2)}, u32[]{:S(2)}) async-start(bf16[16,24,384]{2,1,0:T(8,128)(2,1)} %bitcast.8), calls=%async_computation.5 | async-start | bytes 589824 | tf_op jit(solution)/shard_map/all_to_all | solution.py:458
  204.5 9.2 %all-to-all-done.5 = bf16[16,24,384]{2,1,0:T(8,128)(2,1)S(1)} async-done(((bf16[16,24,384]{2,1,0:T(8,128)(2,1)}), bf16[16,24,384]{2,1,0:T(8,128)(2,1)S(1)}, u32[]{:S(2)}, u32[]{:S(2)}) %all-to-all-start.5) | async-done | bytes 294944 | tf_op jit(solution)/shard_map/all_to_all | solution.py:458
  213.7 0.9 fusion.1
  (22 shorter events, 0.9 us)
Async XLA Ops:
  0.0 1.1 copy-start.3
  1.5 1.5 copy-start
  3.0 7.1 %copy-start.7 = (f32[3,3072]{1,0:T(4,128)S(1)}, f32[3,3072]{1,0:T(4,128)}, u32[]{:S(2)}) copy-start(f32[3,3072]{1,0:T(4,128)} %mod_ref.4) | copy-start | bytes 110596
  3.0 42.6 %all-to-all-start = ((bf16[8,392,384]{2,1,0:T(8,128)(2,1)}), bf16[8,392,384]{2,1,0:T(8,128)(2,1)S(1)}, u32[]{:S(2)}, u32[]{:S(2)}) async-start(bf16[8,392,384]{2,1,0:T(8,128)(2,1)} %copy-done), calls=%async_computation | async-start | bytes 4816896 | tf_op jit(solution)/shard_map/all_to_all | solution.py:464
  16.9 2.1 copy-start.2
  45.6 7.0 %copy-start.9 = (s32[16,6,6]{0,2,1:T(8,128)S(1)}, s32[16,6,6]{0,2,1:T(8,128)}, u32[]{:S(2)}) copy-start(s32[16,6,6]{0,2,1:T(8,128)} %param.9) | copy-start | bytes 6916
  52.5 1.8 collective-permute-start
  54.3 1.4 copy-start.6
  59.4 34.3 %copy-start.4 = (f32[1,384,384]{2,1,0:T(8,128)S(1)}, f32[1,384,384]{2,1,0:T(8,128)}, u32[]{:S(2)}) copy-start(f32[1,384,384]{2,1,0:T(8,128)} %param.8) | copy-start | bytes 1769476
  116.7 4.6 %copy-start.8 = (f32[3,3072]{1,0:T(4,128)S(1)}, f32[3,3072]{1,0:T(4,128)}, u32[]{:S(2)}) copy-start(f32[3,3072]{1,0:T(4,128)} %mod_ref.5) | copy-start | bytes 110596
  116.7 38.8 %all-to-all-start.3 = ((bf16[8,392,384]{2,1,0:T(8,128)(2,1)}), bf16[8,392,384]{2,1,0:T(8,128)(2,1)}, u32[]{:S(2)}, u32[]{:S(2)}) async-start(bf16[8,392,384]{2,1,0:T(8,128)(2,1)} %repack.1), calls=%async_computation.3 | async-start | bytes 4816896 | tf_op jit(solution)/shard_map/all_to_all | solution.py:464
  121.3 34.2 %copy-start.5 = (bf16[256,3072]{1,0:T(8,128)(2,1)S(1)}, bf16[256,3072]{1,0:T(8,128)(2,1)}, u32[]{:S(2)}) copy-start(bf16[256,3072]{1,0:T(8,128)(2,1)} %out_weight_ref.1) | copy-start | bytes 4718596
  128.3 2.1 copy-start.1
  199.0 14.8 %all-to-all-start.5 = ((bf16[16,24,384]{2,1,0:T(8,128)(2,1)}), bf16[16,24,384]{2,1,0:T(8,128)(2,1)S(1)}, u32[]{:S(2)}, u32[]{:S(2)}) async-start(bf16[16,24,384]{2,1,0:T(8,128)(2,1)} %bitcast.8), calls=%async_computation.5 | async-start | bytes 589824 | tf_op jit(solution)/shard_map/all_to_all | solution.py:458

commit v4 on v3

v4 whole, which is shorter than its diff:
```python
import functools
import math

import jax
import jax.numpy as jnp
from jax import lax
from jax.experimental import pallas as pl
from jax.experimental.pallas import tpu as pltpu
from jax.sharding import PartitionSpec as P

HD = 128
BLOCK = 128
EPS = 1e-06
SCALE = 1.0 / math.sqrt(HD)
VMEM_LIMIT = 48 * 1024 * 1024
F32 = jnp.float32
BF16 = jnp.bfloat16
STAT_ROWS = 8


def whole(shape):
    return pl.BlockSpec(shape, lambda *_: (0,) * len(shape))


def params():
    return pltpu.CompilerParams(vmem_limit_bytes=VMEM_LIMIT)


def spread_columns(columns, rows):
    lane = lax.broadcasted_iota(jnp.int32, (rows, 128), 1)
    table = jnp.zeros((rows, 128), F32)
    for index, column in enumerate(columns):
        table = jnp.where(lane == index, column, table)
    return table


def bf16_terms(values, count):
    terms = []
    for _ in range(count):
        term = values.astype(BF16).astype(F32)
        terms.append(term)
        values = values - term
    return terms


def centre(values):
    mean = jnp.sum(values, axis=1, keepdims=True) / values.shape[1]
    centred = values - mean
    squares = jnp.sum(centred * centred, axis=1, keepdims=True)
    table = spread_columns(bf16_terms(mean, 3) + bf16_terms(squares, 2), values.shape[0])
    return centred.astype(BF16), table


def pack_kernel(tokens_ref, out_ref):
    rows = tokens_ref.shape[0]
    centred, table = centre(tokens_ref[...])
    out_ref[:rows, :] = centred
    out_ref[rows:, :] = jnp.transpose(table)[:STAT_ROWS].astype(BF16)


def pack(tokens):
    rows, width = tokens.shape
    shape = (rows + STAT_ROWS, width)
    return pl.pallas_call(
        pack_kernel,
        grid=(1,),
        in_specs=[whole(tokens.shape)],
        out_specs=whole(shape),
        out_shape=jax.ShapeDtypeStruct(shape, BF16),
        compiler_params=params(),
        name="pack",
    )(tokens)


def repack_kernel(arrived_ref, out_ref):
    rows = arrived_ref.shape[0]
    width = out_ref.shape[1]
    out_ref[:rows, :] = arrived_ref[:, :width]
    out_ref[rows:, :] = jnp.transpose(arrived_ref[:, width:].astype(F32))[:STAT_ROWS].astype(BF16)


def repack(arrived):
    rows, width = arrived.shape
    shape = (rows + STAT_ROWS, width - 128)
    return pl.pallas_call(
        repack_kernel,
        grid=(1,),
        in_specs=[whole(arrived.shape)],
        out_specs=whole(shape),
        out_shape=jax.ShapeDtypeStruct(shape, BF16),
        compiler_params=params(),
        name="repack",
    )(arrived)


def row_table(stats_ref, width):
    parts, _, rows = stats_ref.shape
    line = lax.broadcasted_iota(jnp.int32, (parts, rows), 0)
    means = jnp.zeros((parts, rows), F32)
    squares = 0.0
    for part in range(parts):
        lines = stats_ref[part].astype(F32)
        means = jnp.where(line == part, lines[0:1] + lines[1:2] + lines[2:3], means)
        squares = squares + (lines[3:4] + lines[4:5])
    offsets = means - jnp.sum(means, axis=0, keepdims=True) / parts
    between = jnp.sum(offsets * offsets, axis=0, keepdims=True) * width
    scale = lax.rsqrt((squares + between) / (parts * width) + EPS)
    scales = jnp.broadcast_to(scale, (128 - parts, rows))
    return jnp.transpose(jnp.concatenate([offsets, scales], axis=0))


def modulate(parts_ref, mod_ref, normed_ref):
    parts, total_rows, width = parts_ref.shape
    rows = normed_ref.shape[0]
    table = row_table(parts_ref.at[:, rows:total_rows, :], width)
    scale = jnp.broadcast_to(table[:, 127:128], (rows, 128))
    for part in range(parts):
        offset = jnp.broadcast_to(table[:, part : part + 1], (rows, 128))
        for start in range(0, width, 128):
            columns = slice(part * width + start, part * width + start + 128)
            values = parts_ref[part, :rows, start : start + 128].astype(F32)
            gain = 1.0 + mod_ref[1:2, columns]
            normed_ref[:, columns] = (
                ((values + offset) * scale) * gain + mod_ref[0:1, columns]
            ).astype(BF16)


def qkv_specs(parts, mod, weight):
    count, _, width = parts.shape
    model_width, heads_width = weight.shape[1:]
    in_specs = [
        whole(parts.shape),
        whole(mod.shape),
        pl.BlockSpec((1, model_width, heads_width), lambda k: (k, 0, 0)),
    ]
    return in_specs


def space_in_kernel(parts_ref, mod_ref, weight_ref, q_ref, kv_ref, normed_ref):
    step = pl.program_id(0)

    @pl.when(step == 0)
    def _():
        modulate(parts_ref, mod_ref, normed_ref)

    product = jnp.dot(normed_ref[...], weight_ref[0], preferred_element_type=F32).astype(BF16)

    @pl.when(step == 0)
    def _():
        q_ref[0] = product

    @pl.when(step > 0)
    def _():
        kv_ref[step - 1] = product


def space_in(parts, mod, weight, rows):
    model_width, heads_width = weight.shape[1:]
    return pl.pallas_call(
        space_in_kernel,
        grid=(3,),
        in_specs=qkv_specs(parts, mod, weight),
        out_specs=[whole((1, rows, heads_width)), whole((2, rows, heads_width))],
        out_shape=[
            jax.ShapeDtypeStruct((1, rows, heads_width), BF16),
            jax.ShapeDtypeStruct((2, rows, heads_width), BF16),
        ],
        scratch_shapes=[pltpu.VMEM((rows, model_width), BF16)],
        compiler_params=params(),
        cost_estimate=pl.CostEstimate(
            flops=2 * rows * weight.size,
            bytes_accessed=2 * (weight.size + parts.size),
            transcendentals=0,
        ),
        name="space_in",
    )(parts, mod, weight)


def project_out(attended, weight_ref, out_ref):
    blocks, _, width = out_ref.shape
    for block in range(blocks):
        out_ref[block] = jnp.dot(
            attended, weight_ref[:, block * width : (block + 1) * width], preferred_element_type=F32
        ).astype(BF16)


def space_attend_kernel(where_ref, mask_ref, q_ref, own_ref, other_ref, weight_ref, out_ref):
    _, rows, heads_width = q_ref.shape
    query_blocks = rows // BLOCK
    key_blocks = 2 * query_blocks
    frame, half = where_ref[0], where_ref[1]
    mask_base = (frame * key_blocks + half * query_blocks) * key_blocks
    heads = []
    for head in range(heads_width // HD):
        key_cols = slice(head * HD, (head + 1) * HD)
        keys = [own_ref[0, :, key_cols], other_ref[0, :, key_cols]]
        values = [own_ref[1, :, key_cols], other_ref[1, :, key_cols]]
        pieces = []
        for block in range(query_blocks):
            query = q_ref[0, block * BLOCK : (block + 1) * BLOCK, key_cols]
            scored = []
            for side in range(2):
                scores = lax.dot_general(
                    query, keys[side], (((1,), (1,)), ((), ())), preferred_element_type=F32
                )
                side_half = half if side == 0 else 1 - half
                for key_block in range(query_blocks):
                    kept = mask_ref[
                        mask_base + block * key_blocks + side_half * query_blocks + key_block
                    ]
                    bias = jnp.where(kept == 1, 0.0, -jnp.inf).astype(F32)
                    scored.append(
                        scores[:, key_block * BLOCK : (key_block + 1) * BLOCK] * SCALE + bias
                    )
            scored = jnp.concatenate(scored, axis=1)
            row_max = jnp.max(scored, axis=1, keepdims=True)
            lifted = jnp.exp(scored - row_max)
            norm = jnp.sum(lifted, axis=1, keepdims=True)
            lifted = lifted.astype(BF16)
            mixed = jnp.dot(lifted[:, :rows], values[0], preferred_element_type=F32)
            mixed += jnp.dot(lifted[:, rows:], values[1], preferred_element_type=F32)
            pieces.append((mixed / norm).astype(BF16))
        heads.append(jnp.concatenate(pieces, axis=0))
    project_out(jnp.concatenate(heads, axis=1), weight_ref, out_ref)


def space_attend(where, mask, queries, own, other, weight, blocks):
    _, rows, heads_width = queries.shape
    width = weight.shape[1] // blocks
    return pl.pallas_call(
        space_attend_kernel,
        grid_spec=pltpu.PrefetchScalarGridSpec(
            num_scalar_prefetch=2,
            grid=(1,),
            in_specs=[
                whole(queries.shape),
                whole(own.shape),
                whole(other.shape),
                whole(weight.shape),
            ],
            out_specs=whole((blocks, rows, width)),
        ),
        out_shape=jax.ShapeDtypeStruct((blocks, rows, width), BF16),
        compiler_params=params(),
        cost_estimate=pl.CostEstimate(
            flops=2 * rows * heads_width * (4 * rows + weight.shape[1]),
            bytes_accessed=2 * (weight.size + rows * weight.shape[1] + 5 * rows * heads_width),
            transcendentals=2 * rows * rows * heads_width // HD,
        ),
        name="space_attend",
    )(where, mask, queries, own, other, weight)


def join_kernel(where_ref, parts_ref, tokens_ref, mod_ref, stream_ref, sent_ref):
    total = parts_ref[0].astype(F32)
    for part in range(1, parts_ref.shape[0]):
        total += parts_ref[part].astype(F32)
    stream = tokens_ref[...] + mod_ref[2:3, :] * total
    stream_ref[...] = stream
    centred, table = centre(stream)
    sent_ref[:, : stream.shape[1]] = centred
    sent_ref[:, stream.shape[1] :] = table.astype(BF16)


def join(where, parts, tokens, mod):
    count, rows, width = parts.shape
    tile = BLOCK
    return pl.pallas_call(
        join_kernel,
        grid_spec=pltpu.PrefetchScalarGridSpec(
            num_scalar_prefetch=1,
            grid=(rows // tile,),
            in_specs=[
                pl.BlockSpec((count, tile, width), lambda i, w: (0, i, 0)),
                pl.BlockSpec((tile, width), lambda i, w: (i, 0)),
                pl.BlockSpec((3, width), lambda i, w: (0, w[2])),
            ],
            out_specs=[
                pl.BlockSpec((tile, width), lambda i, w: (i, 0)),
                pl.BlockSpec((tile, width + 128), lambda i, w: (i, 0)),
            ],
        ),
        out_shape=[
            jax.ShapeDtypeStruct((rows, width), F32),
            jax.ShapeDtypeStruct((rows, width + 128), BF16),
        ],
        compiler_params=params(),
        name="join",
    )(where, parts, tokens, mod)


def total_kernel(parts_ref, out_ref):
    total = parts_ref[0].astype(F32)
    for part in range(1, parts_ref.shape[0]):
        total += parts_ref[part].astype(F32)
    out_ref[...] = total.astype(BF16)


def total_of(parts):
    count, rows, width = parts.shape
    tile = BLOCK
    return pl.pallas_call(
        total_kernel,
        grid=(rows // tile,),
        in_specs=[pl.BlockSpec((count, tile, width), lambda i: (0, i, 0))],
        out_specs=pl.BlockSpec((tile, width), lambda i: (i, 0)),
        out_shape=jax.ShapeDtypeStruct((rows, width), BF16),
        compiler_params=params(),
        name="total_of",
    )(parts)


def time_kernel(frames, parts_ref, mod_ref, weight_ref, out_weight_ref, out_ref,
                normed_ref, packed_ref, att_ref):
    step, last = pl.program_id(0), pl.num_programs(0) - 1

    @pl.when(step == 0)
    def _():
        modulate(parts_ref, mod_ref, normed_ref)

    packed_ref[step] = jnp.dot(
        normed_ref[...], weight_ref[0], preferred_element_type=F32
    ).reshape(packed_ref.shape[1:])

    @pl.when(step == last)
    def _():
        _, _, places, heads_width = packed_ref.shape
        group = 8
        span = frames * group
        row_place = lax.broadcasted_iota(jnp.int32, (span, span), 0) % group
        col_place = lax.broadcasted_iota(jnp.int32, (span, span), 1) % group
        bias = jnp.where(row_place == col_place, 0.0, -jnp.inf).astype(F32)
        for start in range(0, places, group):
            for low in range(0, heads_width, HD):
                query, key, value = [
                    packed_ref[part, :, start : start + group, low : low + HD]
                    .reshape(span, HD)
                    .astype(BF16)
                    for part in range(3)
                ]
                scores = lax.dot_general(
                    query, key, (((1,), (1,)), ((), ())), preferred_element_type=F32
                ) * SCALE + bias
                lifted = jnp.exp(scores - jnp.max(scores, axis=1, keepdims=True))
                norm = jnp.sum(lifted, axis=1, keepdims=True)
                mixed = jnp.dot(lifted.astype(BF16), value, preferred_element_type=F32) / norm
                att_ref[:, start : start + group, low : low + HD] = mixed.reshape(frames, group, HD)
        attended = att_ref[...].reshape(frames * places, heads_width).astype(BF16)
        project_out(attended, out_weight_ref, out_ref)


def time_layer(parts, mod, weight, out_weight, rows, frames):
    count, _, width = parts.shape
    model_width, heads_width = weight.shape[1:]
    return pl.pallas_call(
        functools.partial(time_kernel, frames),
        grid=(3,),
        in_specs=qkv_specs(parts, mod, weight) + [whole(out_weight.shape)],
        out_specs=whole((count, rows, width)),
        out_shape=jax.ShapeDtypeStruct((count, rows, width), BF16),
        scratch_shapes=[
            pltpu.VMEM((rows, model_width), BF16),
            pltpu.VMEM((3, frames, rows // frames, heads_width), F32),
            pltpu.VMEM((frames, rows // frames, heads_width), F32),
        ],
        compiler_params=params(),
        cost_estimate=pl.CostEstimate(
            flops=2 * rows * (weight.size + out_weight.size),
            bytes_accessed=2 * (weight.size + out_weight.size + 2 * parts.size),
            transcendentals=rows * BLOCK * heads_width // HD,
        ),
        name="time_layer",
    )(parts, mod, weight, out_weight)


def on_device(tokens, block_mask, space_qkv, space_out, space_mod, time_qkv, time_out, time_mod):
    videos, rows, width = tokens.shape
    parts = lax.axis_size("fsdp")
    seq_count = lax.axis_size("seq")
    frames = seq_count // 2
    seq_index = lax.axis_index("seq")
    where = jnp.stack([seq_index // 2, seq_index % 2, lax.axis_index("fsdp")]).astype(jnp.int32)
    same_half = [[2 * frame + half for frame in range(frames)] for half in range(2)]

    def across_frames(values):
        return lax.all_to_all(
            values.reshape(frames, rows // frames, -1), "seq", split_axis=0, concat_axis=0,
            tiled=True, axis_index_groups=same_half,
        ).reshape(rows, -1)

    def across_parts(values):
        return lax.all_to_all(values, "fsdp", split_axis=0, concat_axis=0, tiled=True)

    def gathered(shard):
        return across_parts(jnp.broadcast_to(shard[None], (parts,) + shard.shape))

    local = tokens.reshape(rows, width)
    queries, own = space_in(gathered(pack(local)), space_mod, jnp.swapaxes(space_qkv, 0, 1), rows)
    other = lax.ppermute(own, "seq", [(i, i ^ 1) for i in range(seq_count)])
    partial = space_attend(where, block_mask.reshape(-1), queries, own, other, space_out, parts)
    stream, sent = join(where, across_parts(partial), local, space_mod)
    wide = gathered(repack(across_frames(sent)))
    partial_time = time_layer(wide, time_mod, jnp.swapaxes(time_qkv, 0, 1), time_out, rows, frames)
    returned = across_frames(total_of(across_parts(partial_time)))
    gate = lax.dynamic_slice_in_dim(time_mod[2], lax.axis_index("fsdp") * width, width, 0)
    return (stream + gate * returned.astype(F32)).reshape(tokens.shape)


def solution(mesh):
    placed = (
        P(None, "seq", "fsdp"),
        P(),
        P(None, None, "fsdp"),
        P("fsdp", None),
        P(),
        P(None, None, "fsdp"),
        P("fsdp", None),
        P(),
    )
    return jax.shard_map(
        on_device, mesh=mesh, in_specs=placed, out_specs=P(None, "seq", "fsdp"), check_vma=False
    )
```

time: 216 us -> 201 us (0.931)
  blocking collectives: 86.2 us -> 159 us
  waiting for transfers between devices: 62.3 us -> 10.6 us
  Pallas kernels: 39.3 us -> 21.9 us
  starting transfers between devices: 17.2 us -> 5.4 us
  local copies, waits for them, and re-layouts: 8.49 us -> 1.81 us
    all_to_all x2 -> x4, blocking collectives: 66.5 us -> 139 us  [across_parts(): lax.all_to_all(values, 'fsdp', split_axis=0, concat_axis=0, tiled=True)]
    all_to_all x2 -> x0, waiting for transfers between devices: 51.7 us -> none  [across_parts(): lax.all_to_all(values, 'fsdp', split_axis=0, concat_axis=0, tiled=True)]
    pallas_call x4 -> x2, Pallas kernels: 30.2 us -> 14.5 us  [the longest x1 8.81 us: time_layer(): pl.pallas_call(functools.partial(time_kernel, frames), grid=(3,), in_spec...]
    all_to_all x2 -> x0, starting transfers between devices: 11.7 us -> none  [across_parts(): lax.all_to_all(values, 'fsdp', split_axis=0, concat_axis=0, tiled=True)]
    unnamed x21 -> x15, local copies, waits for them, and re-layouts: 8.31 us -> 1.22 us
  transfers between devices with their start and end apart: 4 -> 2, of which waited for: 4 -> 2; matrix products, arithmetic and copies ran while one was open for 0% -> 0% of each run, Pallas kernels for 6% -> 0%
where the time goes in v4:
time: 201 us; the launch traced here: 200 us
  blocking collectives  159 us (79%)
  Pallas kernels  21.9 us (11%)
  waiting for transfers between devices  10.6 us (5%)
  starting transfers between devices  5.4 us (3%)
    all_to_all x4, blocking collectives, across_parts(): lax.all_to_all(values, 'fsdp', split_axis=0, concat_axis=0, tiled=True)  139 us
    all_to_all x1, blocking collectives, across_frames(): lax.all_to_all(values.reshape(frames, rows // frames, -1), 'seq', split_a...  20.3 us
    all_to_all x1, waiting for transfers between devices, across_frames(): lax.all_to_all(values.reshape(frames, rows // frames, -1), 'seq', split_a...  9.24 us
    pallas_call x1, Pallas kernels, time_layer(): pl.pallas_call(functools.partial(time_kernel, frames), grid=(3,), in_spec...  8.81 us
    pallas_call x1, Pallas kernels, space_in(): pl.pallas_call(space_in_kernel, grid=(3,), in_specs=qkv_specs(parts, mod,...  5.7 us
    all_to_all x1, starting transfers between devices, across_frames(): lax.all_to_all(values.reshape(frames, rows // frames, -1), 'seq', split_a...  5.31 us
  transfers between devices with their start and end apart: 2, of which 2 were waited for; matrix products, arithmetic and copies ran while one was open for 0% of the time, Pallas kernels for 0%

profile of v4, /device:TPU:32, one launch (start us, length us, event | category | flops | bytes accessed | tf_op | source)
XLA Modules:
  0.0 200.2 jit_solution(11726197946520242257)
XLA Ops:
  0.0 1.1 copy-done
  1.1 0.3 pack.1
  1.4 0.2 broadcast_in_dim.4
  1.6 39.0 %all_to_all.30.parts_ref = bf16[8,392,384]{2,1,0:T(8,128)(2,1)S(1)} all-to-all(bf16[8,392,384]{2,1,0:T(8,128)(2,1)S(1)} %broadcast_in_dim.4), channel_id=1, replica_groups=mesh['seq'=32,'fsdp'=8] {'fsdp'}, dimensions={0} | all-to-all | bytes 4816896 | tf_op jit(solution)/shard_map/all_to_all | solution.py:392
  40.7 5.7 %space_in.1 = (bf16[1,384,256]{2,1,0:T(8,128)(2,1)S(1)}, bf16[2,384,256]{2,1,0:T(8,128)(2,1)S(1)}) custom-call(bf16[8,392,384]{2,1,0:T(8,128)(2,1)S(1)} %all_to_all.30.parts_ref, f32[3,3072]{1,0:T(4,128)S(1)} %copy-done.4, bf16[3,3072,256]{2,1,0:T(8,128)(2,1)} %bitcast.18), custom_call_target="tpu_custom_call" | custom-call | flops 1811939328 | bytes 7127040 | tf_op jit(solution)/shard_map/space_in/pallas_call | solution.py:159
  46.4 0.1 collective-permute-start
  46.5 0.1 copy.9
  46.6 0.1 reshape.25.mask_ref
  46.8 0.1 pad_add_fusion.where_ref
  46.9 1.3 collective-permute-done.other_ref
  48.2 3.7 %space_attend.1 = bf16[8,384,384]{2,1,0:T(8,128)(2,1)S(1)} custom-call(s32[3]{0:T(128)S(1)} %pad_add_fusion.where_ref, s32[576]{0:T(1024)S(1)} %reshape.25.mask_ref, bf16[1,384,256]{2,1,0:T(8,128)(2,1)S(1)} %get-tuple-element.9.q_ref, bf16[2,384,256]{2,1,0:T(8,128)(2,1)S(1)} %get-tuple-element.10.own_ref, ...), custom_call_target="tpu_custom_call" | custom-call | flops 905969664 | bytes 4915200 | tf_op jit(solution)/shard_map/space_attend/pallas_call | solution.py:230
  51.9 0.0 copy-start.1
  51.9 34.1 %all_to_all.31.parts_ref = bf16[8,384,384]{2,1,0:T(8,128)(2,1)S(1)} all-to-all(bf16[8,384,384]{2,1,0:T(8,128)(2,1)S(1)} %space_attend.1), channel_id=1, replica_groups=mesh['seq'=32,'fsdp'=8] {'fsdp'}, dimensions={0} | all-to-all | bytes 4718592 | tf_op jit(solution)/shard_map/all_to_all | solution.py:392
  86.0 1.6 join.1
  87.6 20.3 %all_to_all.32 = bf16[16,24,512]{2,1,0:T(8,128)(2,1)S(1)} all-to-all(bf16[16,24,512]{2,1,0:T(8,128)(2,1)S(1)} %bitcast.17), channel_id=1, replica_groups={{0,16,32,48,64,80,96,112,128,144,160,176,192,208,224,240},{8,24,40,56,7..., dimensions={0} | all-to-all | bytes 786432 | tf_op jit(solution)/shard_map/all_to_all | solution.py:386
  107.9 0.1 repack.1
  107.9 0.2 broadcast_in_dim.5
  108.2 34.8 %all_to_all.33.parts_ref = bf16[8,392,384]{2,1,0:T(8,128)(2,1)} all-to-all(bf16[8,392,384]{2,1,0:T(8,128)(2,1)S(1)} %broadcast_in_dim.5), channel_id=1, replica_groups=mesh['seq'=32,'fsdp'=8] {'fsdp'}, dimensions={0} | all-to-all | bytes 4816896 | tf_op jit(solution)/shard_map/all_to_all | solution.py:392
  143.0 8.8 %time_layer.1 = bf16[8,384,384]{2,1,0:T(8,128)(2,1)S(1)} custom-call(bf16[8,392,384]{2,1,0:T(8,128)(2,1)} %all_to_all.33.parts_ref, f32[3,3072]{1,0:T(4,128)S(1)} %copy-done.5, bf16[3,3072,256]{2,1,0:T(8,128)(2,1)} %bitcast.19, bf16[256,3072]{1,0:T(8,128)(2,1)S(1)} %copy-done.3), custom_call_target="tpu_custom_call" | custom-call | flops 2415919104 | bytes 11108352 | tf_op jit(solution)/shard_map/time_layer/pallas_call | solution.py:355
  151.8 31.2 %all_to_all.34.parts_ref = bf16[8,384,384]{2,1,0:T(8,128)(2,1)S(1)} all-to-all(bf16[8,384,384]{2,1,0:T(8,128)(2,1)S(1)} %time_layer.1), channel_id=1, replica_groups=mesh['seq'=32,'fsdp'=8] {'fsdp'}, dimensions={0} | all-to-all | bytes 4718592 | tf_op jit(solution)/shard_map/all_to_all | solution.py:392
  183.1 1.7 total_of.1
  184.7 5.3 %all-to-all-start.5 = ((bf16[16,24,384]{2,1,0:T(8,128)(2,1)}), bf16[16,24,384]{2,1,0:T(8,128)(2,1)S(1)}, u32[]{:S(2)}, u32[]{:S(2)}) async-start(bf16[16,24,384]{2,1,0:T(8,128)(2,1)} %bitcast.8), calls=%async_computation.5 | async-start | bytes 589824 | tf_op jit(solution)/shard_map/all_to_all | solution.py:386
  190.1 9.2 %all-to-all-done.5 = bf16[16,24,384]{2,1,0:T(8,128)(2,1)S(1)} async-done(((bf16[16,24,384]{2,1,0:T(8,128)(2,1)}), bf16[16,24,384]{2,1,0:T(8,128)(2,1)S(1)}, u32[]{:S(2)}, u32[]{:S(2)}) %all-to-all-start.5) | async-done | bytes 294944 | tf_op jit(solution)/shard_map/all_to_all | solution.py:386
  199.3 0.9 fusion.1
  (14 shorter events, 0.1 us)
Async XLA Ops:
  0.0 1.1 copy-start
  1.6 39.1 %copy-start.4 = (f32[3,3072]{1,0:T(4,128)S(1)}, f32[3,3072]{1,0:T(4,128)}, u32[]{:S(2)}) copy-start(f32[3,3072]{1,0:T(4,128)} %mod_ref.4) | copy-start | bytes 110596
  40.6 5.8 %copy-start.6 = (s32[16,6,6]{0,2,1:T(8,128)S(1)}, s32[16,6,6]{0,2,1:T(8,128)}, u32[]{:S(2)}) copy-start(s32[16,6,6]{0,2,1:T(8,128)} %param.9) | copy-start | bytes 6916
  40.7 7.5 %copy-start.2 = (bf16[256,3072]{1,0:T(8,128)(2,1)S(1)}, bf16[256,3072]{1,0:T(8,128)(2,1)}, u32[]{:S(2)}) copy-start(bf16[256,3072]{1,0:T(8,128)(2,1)} %weight_ref.1) | copy-start | bytes 4718596
  46.4 1.8 collective-permute-start
  51.9 34.1 %copy-start.1 = (f32[1,384,384]{2,1,0:T(8,128)S(1)}, f32[1,384,384]{2,1,0:T(8,128)}, u32[]{:S(2)}) copy-start(f32[1,384,384]{2,1,0:T(8,128)} %param.8) | copy-start | bytes 1769476
  108.1 34.9 %copy-start.3 = (bf16[256,3072]{1,0:T(8,128)(2,1)S(1)}, bf16[256,3072]{1,0:T(8,128)(2,1)}, u32[]{:S(2)}) copy-start(bf16[256,3072]{1,0:T(8,128)(2,1)} %out_weight_ref.1) | copy-start | bytes 4718596
  108.2 34.9 %copy-start.5 = (f32[3,3072]{1,0:T(4,128)S(1)}, f32[3,3072]{1,0:T(4,128)}, u32[]{:S(2)}) copy-start(f32[3,3072]{1,0:T(4,128)} %mod_ref.5) | copy-start | bytes 110596
  184.7 14.6 %all-to-all-start.5 = ((bf16[16,24,384]{2,1,0:T(8,128)(2,1)}), bf16[16,24,384]{2,1,0:T(8,128)(2,1)S(1)}, u32[]{:S(2)}, u32[]{:S(2)}) async-start(bf16[16,24,384]{2,1,0:T(8,128)(2,1)} %bitcast.8), calls=%async_computation.5 | async-start | bytes 589824 | tf_op jit(solution)/shard_map/all_to_all | solution.py:386

commit v5 on v4

--- a/solution.py
+++ b/solution.py
@@ -53,7 +53,7 @@
 
 def pack_kernel(tokens_ref, out_ref):
     rows = tokens_ref.shape[0]
-    centred, table = centre(tokens_ref[...])
+    centred, table = centre(tokens_ref[...].astype(F32))
     out_ref[:rows, :] = centred
     out_ref[rows:, :] = jnp.transpose(table)[:STAT_ROWS].astype(BF16)
 
@@ -70,27 +70,6 @@
         compiler_params=params(),
         name="pack",
     )(tokens)
-
-
-def repack_kernel(arrived_ref, out_ref):
-    rows = arrived_ref.shape[0]
-    width = out_ref.shape[1]
-    out_ref[:rows, :] = arrived_ref[:, :width]
-    out_ref[rows:, :] = jnp.transpose(arrived_ref[:, width:].astype(F32))[:STAT_ROWS].astype(BF16)
-
-
-def repack(arrived):
-    rows, width = arrived.shape
-    shape = (rows + STAT_ROWS, width - 128)
-    return pl.pallas_call(
-        repack_kernel,
-        grid=(1,),
-        in_specs=[whole(arrived.shape)],
-        out_specs=whole(shape),
-        out_shape=jax.ShapeDtypeStruct(shape, BF16),
-        compiler_params=params(),
-        name="repack",
-    )(arrived)
 
 
 def row_table(stats_ref, width):
@@ -257,9 +236,7 @@
         total += parts_ref[part].astype(F32)
     stream = tokens_ref[...] + mod_ref[2:3, :] * total
     stream_ref[...] = stream
-    centred, table = centre(stream)
-    sent_ref[:, : stream.shape[1]] = centred
-    sent_ref[:, stream.shape[1] :] = table.astype(BF16)
+    sent_ref[...] = stream.astype(BF16)
 
 
 def join(where, parts, tokens, mod):
@@ -277,37 +254,16 @@
             ],
             out_specs=[
                 pl.BlockSpec((tile, width), lambda i, w: (i, 0)),
-                pl.BlockSpec((tile, width + 128), lambda i, w: (i, 0)),
+                pl.BlockSpec((tile, width), lambda i, w: (i, 0)),
             ],
         ),
         out_shape=[
             jax.ShapeDtypeStruct((rows, width), F32),
-            jax.ShapeDtypeStruct((rows, width + 128), BF16),
+            jax.ShapeDtypeStruct((rows, width), BF16),
         ],
         compiler_params=params(),
         name="join",
     )(where, parts, tokens, mod)
-
-
-def total_kernel(parts_ref, out_ref):
-    total = parts_ref[0].astype(F32)
-    for part in range(1, parts_ref.shape[0]):
-        total += parts_ref[part].astype(F32)
-    out_ref[...] = total.astype(BF16)
-
-
-def total_of(parts):
-    count, rows, width = parts.shape
-    tile = BLOCK
-    return pl.pallas_call(
-        total_kernel,
-        grid=(rows // tile,),
-        in_specs=[pl.BlockSpec((count, tile, width), lambda i: (0, i, 0))],
-        out_specs=pl.BlockSpec((tile, width), lambda i: (i, 0)),
-        out_shape=jax.ShapeDtypeStruct((rows, width), BF16),
-        compiler_params=params(),
-        name="total_of",
-    )(parts)
 
 
 def time_kernel(frames, parts_ref, mod_ref, weight_ref, out_weight_ref, out_ref,
@@ -399,9 +355,10 @@
     other = lax.ppermute(own, "seq", [(i, i ^ 1) for i in range(seq_count)])
     partial = space_attend(where, block_mask.reshape(-1), queries, own, other, space_out, parts)
     stream, sent = join(where, across_parts(partial), local, space_mod)
-    wide = gathered(repack(across_frames(sent)))
+    wide = gathered(pack(across_frames(sent)))
     partial_time = time_layer(wide, time_mod, jnp.swapaxes(time_qkv, 0, 1), time_out, rows, frames)
-    returned = across_frames(total_of(across_parts(partial_time)))
+    total = jnp.sum(across_parts(partial_time).astype(F32), axis=0).astype(BF16)
+    returned = across_frames(total)
     gate = lax.dynamic_slice_in_dim(time_mod[2], lax.axis_index("fsdp") * width, width, 0)
     return (stream + gate * returned.astype(F32)).reshape(tokens.shape)
 

time: 201 us -> 198 us (0.985)
  no operation moved by 1% of the time
where the time goes in v5:
time: 198 us; the launch traced here: 197 us
  blocking collectives  157 us (79%)
  Pallas kernels  20.1 us (10%)
  waiting for transfers between devices  10.6 us (5%)
  starting transfers between devices  5.32 us (3%)
  other arithmetic  2.08 us (1%)
    all_to_all x4, blocking collectives, across_parts(): lax.all_to_all(values, 'fsdp', split_axis=0, concat_axis=0, tiled=True)  139 us
    all_to_all x1, blocking collectives, across_frames(): lax.all_to_all(values.reshape(frames, rows // frames, -1), 'seq', split_a...  18.7 us
    all_to_all x1, waiting for transfers between devices, across_frames(): lax.all_to_all(values.reshape(frames, rows // frames, -1), 'seq', split_a...  9.24 us
    pallas_call x1, Pallas kernels, time_layer(): pl.pallas_call(functools.partial(time_kernel, frames), grid=(3,), in_spec...  8.81 us
    pallas_call x1, Pallas kernels, space_in(): pl.pallas_call(space_in_kernel, grid=(3,), in_specs=qkv_specs(parts, mod,...  5.7 us
    all_to_all x1, starting transfers between devices, across_frames(): lax.all_to_all(values.reshape(frames, rows // frames, -1), 'seq', split_a...  5.22 us
  transfers between devices with their start and end apart: 2, of which 2 were waited for; matrix products, arithmetic and copies ran while one was open for 0% of the time, Pallas kernels for 0%

profile of v5, /device:TPU:32, one launch (start us, length us, event | category | flops | bytes accessed | tf_op | source)
XLA Modules:
  0.0 197.4 jit_solution(15626080872313990379)
XLA Ops:
  0.0 1.1 copy-done
  1.1 0.3 pack.2
  1.4 0.2 broadcast_in_dim.4
  1.6 39.0 %all_to_all.30.parts_ref = bf16[8,392,384]{2,1,0:T(8,128)(2,1)S(1)} all-to-all(bf16[8,392,384]{2,1,0:T(8,128)(2,1)S(1)} %broadcast_in_dim.4), channel_id=1, replica_groups=mesh['seq'=32,'fsdp'=8] {'fsdp'}, dimensions={0} | all-to-all | bytes 4816896 | tf_op jit(solution)/shard_map/all_to_all | solution.py:348
  40.7 5.7 %space_in.1 = (bf16[1,384,256]{2,1,0:T(8,128)(2,1)S(1)}, bf16[2,384,256]{2,1,0:T(8,128)(2,1)S(1)}) custom-call(bf16[8,392,384]{2,1,0:T(8,128)(2,1)S(1)} %all_to_all.30.parts_ref, f32[3,3072]{1,0:T(4,128)S(1)} %copy-done.4, bf16[3,3072,256]{2,1,0:T(8,128)(2,1)} %bitcast.18), custom_call_target="tpu_custom_call" | custom-call | flops 1811939328 | bytes 7127040 | tf_op jit(solution)/shard_map/space_in/pallas_call | solution.py:138
  46.4 0.1 collective-permute-start
  46.5 0.1 copy.9
  46.6 0.1 reshape.25.mask_ref
  46.8 0.1 pad_add_fusion.where_ref
  46.9 1.3 collective-permute-done.other_ref
  48.2 3.7 %space_attend.1 = bf16[8,384,384]{2,1,0:T(8,128)(2,1)S(1)} custom-call(s32[3]{0:T(128)S(1)} %pad_add_fusion.where_ref, s32[576]{0:T(1024)S(1)} %reshape.25.mask_ref, bf16[1,384,256]{2,1,0:T(8,128)(2,1)S(1)} %get-tuple-element.9.q_ref, bf16[2,384,256]{2,1,0:T(8,128)(2,1)S(1)} %get-tuple-element.10.own_ref, ...), custom_call_target="tpu_custom_call" | custom-call | flops 905969664 | bytes 4915200 | tf_op jit(solution)/shard_map/space_attend/pallas_call | solution.py:209
  51.9 0.0 copy-start.1
  51.9 34.1 %all_to_all.31.parts_ref = bf16[8,384,384]{2,1,0:T(8,128)(2,1)S(1)} all-to-all(bf16[8,384,384]{2,1,0:T(8,128)(2,1)S(1)} %space_attend.1), channel_id=1, replica_groups=mesh['seq'=32,'fsdp'=8] {'fsdp'}, dimensions={0} | all-to-all | bytes 4718592 | tf_op jit(solution)/shard_map/all_to_all | solution.py:348
  86.0 1.2 join.1
  87.2 18.7 %all_to_all.32 = bf16[16,24,384]{2,1,0:T(8,128)(2,1)S(1)} all-to-all(bf16[16,24,384]{2,1,0:T(8,128)(2,1)S(1)} %bitcast.17), channel_id=1, replica_groups={{0,16,32,48,64,80,96,112,128,144,160,176,192,208,224,240},{8,24,40,56,7..., dimensions={0} | all-to-all | bytes 589824 | tf_op jit(solution)/shard_map/all_to_all | solution.py:342
  105.9 0.3 pack.3
  106.2 0.2 broadcast_in_dim.5
  106.4 34.5 %all_to_all.33.parts_ref = bf16[8,392,384]{2,1,0:T(8,128)(2,1)} all-to-all(bf16[8,392,384]{2,1,0:T(8,128)(2,1)S(1)} %broadcast_in_dim.5), channel_id=1, replica_groups=mesh['seq'=32,'fsdp'=8] {'fsdp'}, dimensions={0} | all-to-all | bytes 4816896 | tf_op jit(solution)/shard_map/all_to_all | solution.py:348
  140.9 8.8 %time_layer.1 = bf16[8,384,384]{2,1,0:T(8,128)(2,1)S(1)} custom-call(bf16[8,392,384]{2,1,0:T(8,128)(2,1)} %all_to_all.33.parts_ref, f32[3,3072]{1,0:T(4,128)S(1)} %copy-done.5, bf16[3,3072,256]{2,1,0:T(8,128)(2,1)} %bitcast.19, bf16[256,3072]{1,0:T(8,128)(2,1)S(1)} %copy-done.3), custom_call_target="tpu_custom_call" | custom-call | flops 2415919104 | bytes 11108352 | tf_op jit(solution)/shard_map/time_layer/pallas_call | solution.py:311
  149.7 31.2 %all_to_all.34 = bf16[8,384,384]{2,1,0:T(8,128)(2,1)S(1)} all-to-all(bf16[8,384,384]{2,1,0:T(8,128)(2,1)S(1)} %time_layer.1), channel_id=1, replica_groups=mesh['seq'=32,'fsdp'=8] {'fsdp'}, dimensions={0} | all-to-all | bytes 4718592 | tf_op jit(solution)/shard_map/all_to_all | solution.py:348
  180.9 1.1 reduce_sum.12
  182.0 5.2 %all-to-all-start.5 = ((bf16[16,24,384]{2,1,0:T(8,128)(2,1)}), bf16[16,24,384]{2,1,0:T(8,128)(2,1)S(1)}, u32[]{:S(2)}, u32[]{:S(2)}) async-start(bf16[16,24,384]{2,1,0:T(8,128)(2,1)} %bitcast.8), calls=%async_computation.5 | async-start | bytes 589824 | tf_op jit(solution)/shard_map/all_to_all | solution.py:342
  187.2 9.2 %all-to-all-done.5 = bf16[16,24,384]{2,1,0:T(8,128)(2,1)S(1)} async-done(((bf16[16,24,384]{2,1,0:T(8,128)(2,1)}), bf16[16,24,384]{2,1,0:T(8,128)(2,1)S(1)}, u32[]{:S(2)}, u32[]{:S(2)}) %all-to-all-start.5) | async-done | bytes 294944 | tf_op jit(solution)/shard_map/all_to_all | solution.py:342
  196.5 0.9 fusion.1
  (14 shorter events, 0.1 us)
Async XLA Ops:
  0.0 1.1 copy-start
  1.6 39.1 %copy-start.4 = (f32[3,3072]{1,0:T(4,128)S(1)}, f32[3,3072]{1,0:T(4,128)}, u32[]{:S(2)}) copy-start(f32[3,3072]{1,0:T(4,128)} %mod_ref.4) | copy-start | bytes 110596
  40.6 5.8 %copy-start.6 = (s32[16,6,6]{0,2,1:T(8,128)S(1)}, s32[16,6,6]{0,2,1:T(8,128)}, u32[]{:S(2)}) copy-start(s32[16,6,6]{0,2,1:T(8,128)} %param.9) | copy-start | bytes 6916
  40.7 7.5 %copy-start.2 = (bf16[256,3072]{1,0:T(8,128)(2,1)S(1)}, bf16[256,3072]{1,0:T(8,128)(2,1)}, u32[]{:S(2)}) copy-start(bf16[256,3072]{1,0:T(8,128)(2,1)} %weight_ref.1) | copy-start | bytes 4718596
  46.4 1.8 collective-permute-start
  51.9 34.1 %copy-start.1 = (f32[1,384,384]{2,1,0:T(8,128)S(1)}, f32[1,384,384]{2,1,0:T(8,128)}, u32[]{:S(2)}) copy-start(f32[1,384,384]{2,1,0:T(8,128)} %param.8) | copy-start | bytes 1769476
  106.4 34.5 %copy-start.3 = (bf16[256,3072]{1,0:T(8,128)(2,1)S(1)}, bf16[256,3072]{1,0:T(8,128)(2,1)}, u32[]{:S(2)}) copy-start(bf16[256,3072]{1,0:T(8,128)(2,1)} %out_weight_ref.1) | copy-start | bytes 4718596
  106.4 34.5 %copy-start.5 = (f32[3,3072]{1,0:T(4,128)S(1)}, f32[3,3072]{1,0:T(4,128)}, u32[]{:S(2)}) copy-start(f32[3,3072]{1,0:T(4,128)} %mod_ref.5) | copy-start | bytes 110596
  182.0 14.5 %all-to-all-start.5 = ((bf16[16,24,384]{2,1,0:T(8,128)(2,1)}), bf16[16,24,384]{2,1,0:T(8,128)(2,1)S(1)}, u32[]{:S(2)}, u32[]{:S(2)}) async-start(bf16[16,24,384]{2,1,0:T(8,128)(2,1)} %bitcast.8), calls=%async_computation.5 | async-start | bytes 589824 | tf_op jit(solution)/shard_map/all_to_all | solution.py:342

commit v6 on v5

v6 whole, which is shorter than its diff:
```python
import functools
import math

import jax
import jax.numpy as jnp
from jax import lax
from jax.experimental import pallas as pl
from jax.experimental.pallas import tpu as pltpu
from jax.sharding import PartitionSpec as P

HD = 128
BLOCK = 128
EPS = 1e-06
SCALE = 1.0 / math.sqrt(HD)
VMEM_LIMIT = 24 * 1024 * 1024
ROW_TILE = 192
F32 = jnp.float32
BF16 = jnp.bfloat16
STAT_ROWS = 8


def vmem(count):
    return [pl.BlockSpec(memory_space=pltpu.VMEM)] * count


def smem(count):
    return [pl.BlockSpec(memory_space=pltpu.SMEM)] * count


def params():
    return pltpu.CompilerParams(vmem_limit_bytes=VMEM_LIMIT)


def spread_columns(columns, rows):
    lane = lax.broadcasted_iota(jnp.int32, (rows, 128), 1)
    table = jnp.zeros((rows, 128), F32)
    for index, column in enumerate(columns):
        table = jnp.where(lane == index, column, table)
    return table


def bf16_terms(values, count):
    terms = []
    for _ in range(count):
        term = values.astype(BF16).astype(F32)
        terms.append(term)
        values = values - term
    return terms


def centre(values):
    mean = jnp.sum(values, axis=1, keepdims=True) / values.shape[1]
    centred = values - mean
    squares = jnp.sum(centred * centred, axis=1, keepdims=True)
    table = spread_columns(bf16_terms(mean, 3) + bf16_terms(squares, 2), values.shape[0])
    return centred.astype(BF16), table


def pack_kernel(tokens_ref, out_ref):
    rows = tokens_ref.shape[0]
    centred, table = centre(tokens_ref[...].astype(F32))
    out_ref[:rows, :] = centred
    out_ref[rows:, :] = jnp.transpose(table)[:STAT_ROWS].astype(BF16)


def pack(tokens):
    rows, width = tokens.shape
    shape = (rows + STAT_ROWS, width)
    return pl.pallas_call(
        pack_kernel,
        in_specs=vmem(1),
        out_specs=vmem(1)[0],
        out_shape=jax.ShapeDtypeStruct(shape, BF16),
        compiler_params=params(),
        name="pack",
    )(tokens)


def row_table(stats_ref, width):
    parts, _, rows = stats_ref.shape
    line = lax.broadcasted_iota(jnp.int32, (parts, rows), 0)
    means = jnp.zeros((parts, rows), F32)
    squares = 0.0
    for part in range(parts):
        lines = stats_ref[part].astype(F32)
        means = jnp.where(line == part, lines[0:1] + lines[1:2] + lines[2:3], means)
        squares = squares + (lines[3:4] + lines[4:5])
    offsets = means - jnp.sum(means, axis=0, keepdims=True) / parts
    between = jnp.sum(offsets * offsets, axis=0, keepdims=True) * width
    scale = lax.rsqrt((squares + between) / (parts * width) + EPS)
    scales = jnp.broadcast_to(scale, (128 - parts, rows))
    return jnp.transpose(jnp.concatenate([offsets, scales], axis=0))


def modulate(parts_ref, mod_ref, normed_ref):
    parts, total_rows, width = parts_ref.shape
    rows = normed_ref.shape[0]
    table = row_table(parts_ref.at[:, rows:total_rows, :], width)
    scale = jnp.broadcast_to(table[:, 127:128], (rows, 128))
    for part in range(parts):
        offset = jnp.broadcast_to(table[:, part : part + 1], (rows, 128))
        for start in range(0, width, 128):
            columns = slice(part * width + start, part * width + start + 128)
            values = parts_ref[part, :rows, start : start + 128].astype(F32)
            gain = 1.0 + mod_ref[1:2, columns]
            normed_ref[:, columns] = (
                ((values + offset) * scale) * gain + mod_ref[0:1, columns]
            ).astype(BF16)


def qkv_rows(normed_ref, weight_ref):
    rows = normed_ref.shape[0]
    tile = ROW_TILE if rows % ROW_TILE == 0 else rows
    for which in range(3):
        for start in range(0, rows, tile):
            span = slice(start, start + tile)
            yield which, span, jnp.dot(
                normed_ref[span, :], weight_ref[which], preferred_element_type=F32
            )


def space_in_kernel(parts_ref, mod_ref, weight_ref, q_ref, kv_ref, normed_ref):
    modulate(parts_ref, mod_ref, normed_ref)
    for which, span, values in qkv_rows(normed_ref, weight_ref):
        if which == 0:
            q_ref[span, :] = values.astype(BF16)
        else:
            kv_ref[which - 1, span, :] = values.astype(BF16)


def space_in(parts, mod, weight, rows):
    model_width, heads_width = weight.shape[1:]
    return pl.pallas_call(
        space_in_kernel,
        in_specs=vmem(3),
        out_specs=vmem(2),
        out_shape=[
            jax.ShapeDtypeStruct((rows, heads_width), BF16),
            jax.ShapeDtypeStruct((2, rows, heads_width), BF16),
        ],
        scratch_shapes=[pltpu.VMEM((rows, model_width), BF16)],
        compiler_params=params(),
        cost_estimate=pl.CostEstimate(
            flops=2 * rows * weight.size,
            bytes_accessed=2 * (weight.size + parts.size),
            transcendentals=0,
        ),
        name="space_in",
    )(parts, mod, weight)


def project_out(attended, weight_ref, out_ref):
    blocks, _, width = out_ref.shape
    for block in range(blocks):
        out_ref[block] = jnp.dot(
            attended, weight_ref[:, block * width : (block + 1) * width], preferred_element_type=F32
        ).astype(BF16)


def soft(scores):
    lifted = [jnp.exp(entry - jnp.max(entry, axis=1, keepdims=True)) for entry in scores]
    norms = [jnp.sum(entry, axis=1, keepdims=True) for entry in lifted]
    return [entry.astype(BF16) for entry in lifted], norms


def against(query, keys):
    return lax.dot_general(query, keys, (((1,), (1,)), ((), ())), preferred_element_type=F32)


def space_attend_kernel(where_ref, mask_ref, q_ref, own_ref, other_ref, weight_ref, out_ref):
    rows, heads_width = q_ref.shape
    query_blocks = rows // BLOCK
    key_blocks = 2 * query_blocks
    half = where_ref[1]
    mask_base = (where_ref[0] * key_blocks + half * query_blocks) * key_blocks
    biases = []
    for block in range(query_blocks):
        line = []
        for side in range(2):
            first = (half if side == 0 else 1 - half) * query_blocks
            for key_block in range(query_blocks):
                kept = mask_ref[mask_base + block * key_blocks + first + key_block]
                line.append(jnp.where(kept == 1, 0.0, -jnp.inf).astype(F32))
        biases.append(line)
    heads = [slice(start, start + HD) for start in range(0, heads_width, HD)]
    keys = [jnp.concatenate([own_ref[0, :, head], other_ref[0, :, head]], axis=0) for head in heads]
    values = [jnp.concatenate([own_ref[1, :, head], other_ref[1, :, head]], axis=0) for head in heads]
    units = [(head, block) for head in range(len(heads)) for block in range(query_blocks)]
    scores = [
        against(q_ref[block * BLOCK : (block + 1) * BLOCK, heads[head]], keys[head])
        for head, block in units
    ]
    scores = [
        jnp.concatenate(
            [
                entry[:, index * BLOCK : (index + 1) * BLOCK] * SCALE + bias
                for index, bias in enumerate(biases[block])
            ],
            axis=1,
        )
        for (_, block), entry in zip(units, scores)
    ]
    lifted, norms = soft(scores)
    mixed = [
        (jnp.dot(entry, values[head], preferred_element_type=F32) / norm).astype(BF16)
        for (head, _), entry, norm in zip(units, lifted, norms)
    ]
    attended = [
        jnp.concatenate(mixed[head * query_blocks : (head + 1) * query_blocks], axis=0)
        for head in range(len(heads))
    ]
    project_out(jnp.concatenate(attended, axis=1), weight_ref, out_ref)


def space_attend(where, mask, queries, own, other, weight, blocks):
    rows, heads_width = queries.shape
    width = weight.shape[1] // blocks
    return pl.pallas_call(
        space_attend_kernel,
        in_specs=smem(2) + vmem(4),
        out_specs=vmem(1)[0],
        out_shape=jax.ShapeDtypeStruct((blocks, rows, width), BF16),
        compiler_params=params(),
        cost_estimate=pl.CostEstimate(
            flops=2 * rows * heads_width * (4 * rows + weight.shape[1]),
            bytes_accessed=2 * (weight.size + rows * weight.shape[1] + 5 * rows * heads_width),
            transcendentals=2 * rows * rows * heads_width // HD,
        ),
        name="space_attend",
    )(where, mask, queries, own, other, weight)


def local_gate(where_ref, mod_ref, width):
    return mod_ref[2:3, pl.ds(pl.multiple_of(where_ref[2] * width, 128), width)]


def join_kernel(where_ref, parts_ref, tokens_ref, mod_ref, stream_ref, sent_ref):
    total = parts_ref[0].astype(F32)
    for part in range(1, parts_ref.shape[0]):
        total += parts_ref[part].astype(F32)
    stream = tokens_ref[...] + local_gate(where_ref, mod_ref, total.shape[1]) * total
    stream_ref[...] = stream
    sent_ref[...] = stream.astype(BF16)


def join(where, parts, tokens, mod):
    count, rows, width = parts.shape
    return pl.pallas_call(
        join_kernel,
        in_specs=smem(1) + vmem(3),
        out_specs=vmem(2),
        out_shape=[
            jax.ShapeDtypeStruct((rows, width), F32),
            jax.ShapeDtypeStruct((rows, width), BF16),
        ],
        compiler_params=params(),
        name="join",
    )(where, parts, tokens, mod)


def time_kernel(parts_ref, mod_ref, weight_ref, out_weight_ref, out_ref, normed_ref, packed_ref, att_ref):
    modulate(parts_ref, mod_ref, normed_ref)
    frames, places, heads_width = att_ref.shape
    for which, span, values in qkv_rows(normed_ref, weight_ref):
        first = span.start // places
        count = values.shape[0] // places
        packed_ref[which, first : first + count] = values.reshape(count, places, heads_width)
    group = 8
    span = frames * group
    row_place = lax.broadcasted_iota(jnp.int32, (span, span), 0) % group
    col_place = lax.broadcasted_iota(jnp.int32, (span, span), 1) % group
    bias = jnp.where(row_place == col_place, 0.0, -jnp.inf).astype(F32)
    units = [(start, low) for start in range(0, places, group) for low in range(0, heads_width, HD)]

    def chosen(which, start, low):
        block = packed_ref[which, :, start : start + group, low : low + HD]
        return block.reshape(span, HD).astype(BF16)

    scores = [against(chosen(0, *unit), chosen(1, *unit)) * SCALE + bias for unit in units]
    lifted, norms = soft(scores)
    for unit, entry, norm in zip(units, lifted, norms):
        mixed = jnp.dot(entry, chosen(2, *unit), preferred_element_type=F32) / norm
        start, low = unit
        att_ref[:, start : start + group, low : low + HD] = mixed.reshape(frames, group, HD)
    project_out(att_ref[...].reshape(frames * places, heads_width).astype(BF16), out_weight_ref, out_ref)


def time_layer(parts, mod, weight, out_weight, rows, frames):
    count, _, width = parts.shape
    model_width, heads_width = weight.shape[1:]
    return pl.pallas_call(
        time_kernel,
        in_specs=vmem(4),
        out_specs=vmem(1)[0],
        out_shape=jax.ShapeDtypeStruct((count, rows, width), BF16),
        scratch_shapes=[
            pltpu.VMEM((rows, model_width), BF16),
            pltpu.VMEM((3, frames, rows // frames, heads_width), F32),
            pltpu.VMEM((frames, rows // frames, heads_width), F32),
        ],
        compiler_params=params(),
        cost_estimate=pl.CostEstimate(
            flops=2 * rows * (weight.size + out_weight.size),
            bytes_accessed=2 * (weight.size + out_weight.size + 2 * parts.size),
            transcendentals=rows * BLOCK * heads_width // HD,
        ),
        name="time_layer",
    )(parts, mod, weight, out_weight)


def on_device(tokens, block_mask, space_qkv, space_out, space_mod, time_qkv, time_out, time_mod):
    videos, rows, width = tokens.shape
    parts = lax.axis_size("fsdp")
    seq_count = lax.axis_size("seq")
    frames = seq_count // 2
    seq_index = lax.axis_index("seq")
    where = jnp.stack([seq_index // 2, seq_index % 2, lax.axis_index("fsdp")]).astype(jnp.int32)
    same_half = [[2 * frame + half for frame in range(frames)] for half in range(2)]

    def across_frames(values):
        return lax.all_to_all(
            values.reshape(frames, rows // frames, -1), "seq", split_axis=0, concat_axis=0,
            tiled=True, axis_index_groups=same_half,
        ).reshape(rows, -1)

    def across_parts(values):
        return lax.all_to_all(values, "fsdp", split_axis=0, concat_axis=0, tiled=True)

    def gathered(shard):
        return across_parts(jnp.broadcast_to(shard[None], (parts,) + shard.shape))

    local = tokens.reshape(rows, width)
    queries, own = space_in(gathered(pack(local)), space_mod, jnp.swapaxes(space_qkv, 0, 1), rows)
    other = lax.ppermute(own, "seq", [(i, i ^ 1) for i in range(seq_count)])
    partial = space_attend(where, block_mask.reshape(-1), queries, own, other, space_out, parts)
    stream, sent = join(where, across_parts(partial), local, space_mod)
    wide = gathered(pack(across_frames(sent)))
    partial_time = time_layer(wide, time_mod, jnp.swapaxes(time_qkv, 0, 1), time_out, rows, frames)
    total = jnp.sum(across_parts(partial_time).astype(F32), axis=0).astype(BF16)
    returned = across_frames(total)
    gate = lax.dynamic_slice_in_dim(time_mod[2], lax.axis_index("fsdp") * width, width, 0)
    return (stream + gate * returned.astype(F32)).reshape(tokens.shape)


def solution(mesh):
    placed = (
        P(None, "seq", "fsdp"),
        P(),
        P(None, None, "fsdp"),
        P("fsdp", None),
        P(),
        P(None, None, "fsdp"),
        P("fsdp", None),
        P(),
    )
    return jax.shard_map(
        on_device, mesh=mesh, in_specs=placed, out_specs=P(None, "seq", "fsdp"), check_vma=False
    )
```

time: 198 us -> 189 us (0.955)
  Pallas kernels: 20.1 us -> 11 us
    pallas_call x6, Pallas kernels: 20.1 us -> 11 us  [the longest x1 4.07 us: time_layer(): pl.pallas_call(time_kernel, in_specs=vmem(4), out_specs=vmem(1)[0], out_s...]
where the time goes in v6:
time: 189 us
  blocking collectives  158 us (84%)
  Pallas kernels  11 us (6%)
  waiting for transfers between devices  10.6 us (6%)
  starting transfers between devices  5.36 us (3%)
  other arithmetic  2.08 us (1%)
    all_to_all x4, blocking collectives, across_parts(): lax.all_to_all(values, 'fsdp', split_axis=0, concat_axis=0, tiled=True)  139 us
    all_to_all x1, blocking collectives, across_frames(): lax.all_to_all(values.reshape(frames, rows // frames, -1), 'seq', split_a...  18.8 us
    all_to_all x1, waiting for transfers between devices, across_frames(): lax.all_to_all(values.reshape(frames, rows // frames, -1), 'seq', split_a...  9.24 us
    all_to_all x1, starting transfers between devices, across_frames(): lax.all_to_all(values.reshape(frames, rows // frames, -1), 'seq', split_a...  5.26 us
    pallas_call x1, Pallas kernels, time_layer(): pl.pallas_call(time_kernel, in_specs=vmem(4), out_specs=vmem(1)[0], out_s...  4.07 us
  transfers between devices with their start and end apart: 2, of which 2 were waited for; matrix products, arithmetic and copies ran while one was open for 0% of the time, Pallas kernels for 0%

profile of v6, /device:TPU:32, one launch (start us, length us, event | category | flops | bytes accessed | tf_op | source)
XLA Modules:
  0.0 188.8 jit_solution(4730320956648460601)
XLA Ops:
  0.0 1.1 copy-done.1
  1.1 0.3 pack.2
  1.4 0.2 broadcast_in_dim.4
  1.6 39.2 %all_to_all.30.parts_ref = bf16[8,392,384]{2,1,0:T(8,128)(2,1)S(1)} all-to-all(bf16[8,392,384]{2,1,0:T(8,128)(2,1)S(1)} %broadcast_in_dim.4), channel_id=1, replica_groups=mesh['seq'=32,'fsdp'=8] {'fsdp'}, dimensions={0} | all-to-all | bytes 4816896 | tf_op jit(solution)/shard_map/all_to_all | solution.py:327
  40.8 2.8 %space_in.1 = (bf16[384,256]{1,0:T(8,128)(2,1)S(1)}, bf16[2,384,256]{2,1,0:T(8,128)(2,1)S(1)}) custom-call(bf16[8,392,384]{2,1,0:T(8,128)(2,1)S(1)} %all_to_all.30.parts_ref, f32[3,3072]{1,0:T(4,128)S(1)} %copy-done.5, bf16[3,3072,256]{2,1,0:T(8,128)(2,1)S(1)} %bitcast.14), custom_call_target="tpu_custom_call" | custom-call | flops 1811939328 | bytes 7127040 | tf_op jit(solution)/shard_map/space_in/pallas_call | solution.py:133
  43.6 0.1 collective-permute-start
  43.8 0.1 copy.9
  43.9 0.1 reshape.25.mask_ref
  44.1 0.1 pad_add_fusion.where_ref
  44.1 1.3 collective-permute-done.other_ref
  45.5 2.6 %space_attend.1 = bf16[8,384,384]{2,1,0:T(8,128)(2,1)S(1)} custom-call(s32[3]{0:T(128)S(1)} %pad_add_fusion.where_ref, s32[576]{0:T(1024)S(1)} %reshape.25.mask_ref, bf16[384,256]{1,0:T(8,128)(2,1)S(1)} %get-tuple-element.9.q_ref, bf16[2,384,256]{2,1,0:T(8,128)(2,1)S(1)} %get-tuple-element.10.own_ref, ...), custom_call_target="tpu_custom_call" | custom-call | flops 905969664 | bytes 4915200 | tf_op jit(solution)/shard_map/space_attend/pallas_call | solution.py:218
  48.1 34.2 %all_to_all.31.parts_ref = bf16[8,384,384]{2,1,0:T(8,128)(2,1)S(1)} all-to-all(bf16[8,384,384]{2,1,0:T(8,128)(2,1)S(1)} %space_attend.1), channel_id=1, replica_groups=mesh['seq'=32,'fsdp'=8] {'fsdp'}, dimensions={0} | all-to-all | bytes 4718592 | tf_op jit(solution)/shard_map/all_to_all | solution.py:327
  82.3 0.9 join.1
  83.2 0.0 slice-start.1
  83.2 18.8 %all_to_all.32 = bf16[16,24,384]{2,1,0:T(8,128)(2,1)S(1)} all-to-all(bf16[16,24,384]{2,1,0:T(8,128)(2,1)S(1)} %bitcast.21), channel_id=1, replica_groups={{0,16,32,48,64,80,96,112,128,144,160,176,192,208,224,240},{8,24,40,56,7..., dimensions={0} | all-to-all | bytes 589824 | tf_op jit(solution)/shard_map/all_to_all | solution.py:321
  102.0 0.3 pack.3
  102.3 0.2 broadcast_in_dim.5
  102.6 34.3 %all_to_all.33.parts_ref = bf16[8,392,384]{2,1,0:T(8,128)(2,1)S(1)} all-to-all(bf16[8,392,384]{2,1,0:T(8,128)(2,1)S(1)} %broadcast_in_dim.5), channel_id=1, replica_groups=mesh['seq'=32,'fsdp'=8] {'fsdp'}, dimensions={0} | all-to-all | bytes 4816896 | tf_op jit(solution)/shard_map/all_to_all | solution.py:327
  136.9 4.1 %time_layer.1 = bf16[8,384,384]{2,1,0:T(8,128)(2,1)S(1)} custom-call(bf16[8,392,384]{2,1,0:T(8,128)(2,1)S(1)} %all_to_all.33.parts_ref, f32[3,3072]{1,0:T(4,128)S(1)} %copy-done.6, bf16[3,3072,256]{2,1,0:T(8,128)(2,1)S(1)} %bitcast.17, bf16[256,3072]{1,0:T(8,128)(2,1)S(1)} %copy-done.4), custom_call_target="tpu_custom_call" | custom-call | flops 2415919104 | bytes 11108352 | tf_op jit(solution)/shard_map/time_layer/pallas_call | solution.py:291
  141.0 31.2 %all_to_all.34 = bf16[8,384,384]{2,1,0:T(8,128)(2,1)S(1)} all-to-all(bf16[8,384,384]{2,1,0:T(8,128)(2,1)S(1)} %time_layer.1), channel_id=1, replica_groups=mesh['seq'=32,'fsdp'=8] {'fsdp'}, dimensions={0} | all-to-all | bytes 4718592 | tf_op jit(solution)/shard_map/all_to_all | solution.py:327
  172.2 1.1 reduce_sum.12
  173.3 5.3 %all-to-all-start.5 = ((bf16[16,24,384]{2,1,0:T(8,128)(2,1)}), bf16[16,24,384]{2,1,0:T(8,128)(2,1)S(1)}, u32[]{:S(2)}, u32[]{:S(2)}) async-start(bf16[16,24,384]{2,1,0:T(8,128)(2,1)} %bitcast.8), calls=%async_computation.5 | async-start | bytes 589824 | tf_op jit(solution)/shard_map/all_to_all | solution.py:321
  178.6 9.2 %all-to-all-done.5 = bf16[16,24,384]{2,1,0:T(8,128)(2,1)S(1)} async-done(((bf16[16,24,384]{2,1,0:T(8,128)(2,1)}), bf16[16,24,384]{2,1,0:T(8,128)(2,1)S(1)}, u32[]{:S(2)}, u32[]{:S(2)}) %all-to-all-start.5) | async-done | bytes 294944 | tf_op jit(solution)/shard_map/all_to_all | solution.py:321
  187.8 0.9 fusion.1
  (21 shorter events, 0.1 us)
Async XLA Ops:
  0.0 1.1 copy-start.1
  1.6 39.2 %copy-start = (bf16[3072,3,256]{2,0,1:T(8,128)(2,1)S(1)}, bf16[3072,3,256]{2,0,1:T(8,128)(2,1)}, u32[]{:S(2)}) copy-start(bf16[3072,3,256]{2,0,1:T(8,128)(2,1)} %param.10) | copy-start | bytes 14155780
  1.6 39.2 %copy-start.5 = (f32[3,3072]{1,0:T(4,128)S(1)}, f32[3,3072]{1,0:T(4,128)}, u32[]{:S(2)}) copy-start(f32[3,3072]{1,0:T(4,128)} %mod_ref.4) | copy-start | bytes 110596
  40.8 3.0 %copy-start.7 = (s32[16,6,6]{0,2,1:T(8,128)S(1)}, s32[16,6,6]{0,2,1:T(8,128)}, u32[]{:S(2)}) copy-start(s32[16,6,6]{0,2,1:T(8,128)} %param.9) | copy-start | bytes 6916
  40.8 4.7 %copy-start.3 = (bf16[256,3072]{1,0:T(8,128)(2,1)S(1)}, bf16[256,3072]{1,0:T(8,128)(2,1)}, u32[]{:S(2)}) copy-start(bf16[256,3072]{1,0:T(8,128)(2,1)} %weight_ref.1) | copy-start | bytes 4718596
  43.6 1.8 collective-permute-start
  45.5 36.8 %copy-start.2 = (f32[1,384,384]{2,1,0:T(8,128)S(1)}, f32[1,384,384]{2,1,0:T(8,128)}, u32[]{:S(2)}) copy-start(f32[1,384,384]{2,1,0:T(8,128)} %param.8) | copy-start | bytes 1769476
  48.1 88.9 %slice-start = ((s8[4718592]{0:T(1024)(128)(4,1)}), s8[4194304]{0:T(1024)(128)(4,1)S(1)}, s32[]{:S(2)}) async-start(s8[4718592]{0:T(1024)(128)(4,1)} %bitcast.15), calls=%async_computation.6 | async-start | bytes 8388608
  83.2 53.8 %slice-start.1 = ((s8[4718592]{0:T(1024)(128)(4,1)}), s8[524288]{0:T(1024)(128)(4,1)S(1)}, s32[]{:S(2)}) async-start(s8[4718592]{0:T(1024)(128)(4,1)} %bitcast.15), calls=%async_computation.7 | async-start | bytes 1048576
  102.6 34.4 %copy-start.4 = (bf16[256,3072]{1,0:T(8,128)(2,1)S(1)}, bf16[256,3072]{1,0:T(8,128)(2,1)}, u32[]{:S(2)}) copy-start(bf16[256,3072]{1,0:T(8,128)(2,1)} %out_weight_ref.1) | copy-start | bytes 4718596
  102.6 34.4 %copy-start.6 = (f32[3,3072]{1,0:T(4,128)S(1)}, f32[3,3072]{1,0:T(4,128)}, u32[]{:S(2)}) copy-start(f32[3,3072]{1,0:T(4,128)} %mod_ref.5) | copy-start | bytes 110596
  173.3 14.6 %all-to-all-start.5 = ((bf16[16,24,384]{2,1,0:T(8,128)(2,1)}), bf16[16,24,384]{2,1,0:T(8,128)(2,1)S(1)}, u32[]{:S(2)}, u32[]{:S(2)}) async-start(bf16[16,24,384]{2,1,0:T(8,128)(2,1)} %bitcast.8), calls=%async_computation.5 | async-start | bytes 589824 | tf_op jit(solution)/shard_map/all_to_all | solution.py:321

commit v7 on v6

--- a/solution.py
+++ b/solution.py
@@ -149,14 +149,6 @@
     )(parts, mod, weight)
 
 
-def project_out(attended, weight_ref, out_ref):
-    blocks, _, width = out_ref.shape
-    for block in range(blocks):
-        out_ref[block] = jnp.dot(
-            attended, weight_ref[:, block * width : (block + 1) * width], preferred_element_type=F32
-        ).astype(BF16)
-
-
 def soft(scores):
     lifted = [jnp.exp(entry - jnp.max(entry, axis=1, keepdims=True)) for entry in scores]
     norms = [jnp.sum(entry, axis=1, keepdims=True) for entry in lifted]
@@ -167,7 +159,7 @@
     return lax.dot_general(query, keys, (((1,), (1,)), ((), ())), preferred_element_type=F32)
 
 
-def space_attend_kernel(where_ref, mask_ref, q_ref, own_ref, other_ref, weight_ref, out_ref):
+def space_attend_kernel(where_ref, mask_ref, q_ref, own_ref, other_ref, out_ref):
     rows, heads_width = q_ref.shape
     query_blocks = rows // BLOCK
     key_blocks = 2 * query_blocks
@@ -201,64 +193,109 @@
         for (_, block), entry in zip(units, scores)
     ]
     lifted, norms = soft(scores)
-    mixed = [
-        (jnp.dot(entry, values[head], preferred_element_type=F32) / norm).astype(BF16)
-        for (head, _), entry, norm in zip(units, lifted, norms)
-    ]
-    attended = [
-        jnp.concatenate(mixed[head * query_blocks : (head + 1) * query_blocks], axis=0)
-        for head in range(len(heads))
-    ]
-    project_out(jnp.concatenate(attended, axis=1), weight_ref, out_ref)
-
-
-def space_attend(where, mask, queries, own, other, weight, blocks):
+    for (head, block), entry, norm in zip(units, lifted, norms):
+        mixed = jnp.dot(entry, values[head], preferred_element_type=F32) / norm
+        out_ref[block * BLOCK : (block + 1) * BLOCK, heads[head]] = mixed.astype(BF16)
+
+
+def space_attend(where, mask, queries, own, other):
     rows, heads_width = queries.shape
-    width = weight.shape[1] // blocks
     return pl.pallas_call(
         space_attend_kernel,
-        in_specs=smem(2) + vmem(4),
+        in_specs=smem(2) + vmem(3),
         out_specs=vmem(1)[0],
-        out_shape=jax.ShapeDtypeStruct((blocks, rows, width), BF16),
+        out_shape=jax.ShapeDtypeStruct((rows, heads_width), BF16),
         compiler_params=params(),
         cost_estimate=pl.CostEstimate(
-            flops=2 * rows * heads_width * (4 * rows + weight.shape[1]),
-            bytes_accessed=2 * (weight.size + rows * weight.shape[1] + 5 * rows * heads_width),
+            flops=8 * rows * rows * heads_width,
+            bytes_accessed=12 * rows * heads_width,
             transcendentals=2 * rows * rows * heads_width // HD,
         ),
         name="space_attend",
-    )(where, mask, queries, own, other, weight)
+    )(where, mask, queries, own, other)
+
+
+def lend_kernel(where_ref, weight_ref, out_ref):
+    groups, count, width = out_ref.shape
+    lines = pl.ds(pl.multiple_of(where_ref[1] * count, 128), count)
+    other_side = 1 - where_ref[2] % 2
+    for group in range(groups):
+        first = pl.multiple_of((2 * group + other_side) * width, 128)
+        out_ref[group] = weight_ref[lines, pl.ds(first, width)]
+
+
+def lend(where, weight, width):
+    heads_width, model_width = weight.shape
+    return pl.pallas_call(
+        lend_kernel,
+        in_specs=smem(1) + vmem(1),
+        out_specs=vmem(1)[0],
+        out_shape=jax.ShapeDtypeStruct((model_width // (2 * width), heads_width // 2, width), BF16),
+        compiler_params=params(),
+        cost_estimate=pl.CostEstimate(flops=0, bytes_accessed=2 * weight.size, transcendentals=0),
+        name="lend",
+    )(where, weight)
+
+
+def project_kernel(where_ref, own_ref, partner_ref, weight_ref, half_ref, other_half_ref, out_ref, lent_ref):
+    groups, _, width = out_ref.shape
+    count = half_ref.shape[1]
+    core, side = where_ref[1], where_ref[2] % 2
+    lent_ref[:, pl.ds(pl.multiple_of(core * count, 128), count), :] = half_ref[...]
+    lent_ref[:, pl.ds(pl.multiple_of((1 - core) * count, 128), count), :] = other_half_ref[...]
+    for group in range(groups):
+        first = pl.multiple_of((2 * group + side) * width, 128)
+        product = jnp.dot(own_ref[...], weight_ref[:, pl.ds(first, width)], preferred_element_type=F32)
+        product += jnp.dot(partner_ref[...], lent_ref[group], preferred_element_type=F32)
+        out_ref[group] = product.astype(BF16)
+
+
+def project(where, own, partner, weight, half, other_half):
+    rows, heads_width = own.shape
+    groups, _, width = half.shape
+    return pl.pallas_call(
+        project_kernel,
+        in_specs=smem(1) + vmem(5),
+        out_specs=vmem(1)[0],
+        out_shape=jax.ShapeDtypeStruct((groups, rows, width), BF16),
+        scratch_shapes=[pltpu.VMEM((groups, heads_width, width), BF16)],
+        compiler_params=params(),
+        cost_estimate=pl.CostEstimate(
+            flops=4 * rows * heads_width * groups * width,
+            bytes_accessed=2 * groups * width * (rows + 2 * heads_width),
+            transcendentals=0,
+        ),
+        name="project",
+    )(where, own, partner, weight, half, other_half)
 
 
 def local_gate(where_ref, mod_ref, width):
     return mod_ref[2:3, pl.ds(pl.multiple_of(where_ref[2] * width, 128), width)]
 
 
-def join_kernel(where_ref, parts_ref, tokens_ref, mod_ref, stream_ref, sent_ref):
+def join_kernel(where_ref, parts_ref, tokens_ref, mod_ref, stream_ref, *sent_refs):
     total = parts_ref[0].astype(F32)
     for part in range(1, parts_ref.shape[0]):
         total += parts_ref[part].astype(F32)
     stream = tokens_ref[...] + local_gate(where_ref, mod_ref, total.shape[1]) * total
     stream_ref[...] = stream
-    sent_ref[...] = stream.astype(BF16)
-
-
-def join(where, parts, tokens, mod):
+    for sent_ref in sent_refs:
+        sent_ref[...] = stream.astype(BF16)
+
+
+def join(where, parts, tokens, mod, dtypes):
     count, rows, width = parts.shape
     return pl.pallas_call(
         join_kernel,
         in_specs=smem(1) + vmem(3),
-        out_specs=vmem(2),
-        out_shape=[
-            jax.ShapeDtypeStruct((rows, width), F32),
-            jax.ShapeDtypeStruct((rows, width), BF16),
-        ],
+        out_specs=vmem(len(dtypes)),
+        out_shape=[jax.ShapeDtypeStruct((rows, width), dtype) for dtype in dtypes],
         compiler_params=params(),
         name="join",
     )(where, parts, tokens, mod)
 
 
-def time_kernel(parts_ref, mod_ref, weight_ref, out_weight_ref, out_ref, normed_ref, packed_ref, att_ref):
+def time_kernel(parts_ref, mod_ref, weight_ref, out_ref, normed_ref, packed_ref, att_ref):
     modulate(parts_ref, mod_ref, normed_ref)
     frames, places, heads_width = att_ref.shape
     for which, span, values in qkv_rows(normed_ref, weight_ref):
@@ -282,17 +319,16 @@
         mixed = jnp.dot(entry, chosen(2, *unit), preferred_element_type=F32) / norm
         start, low = unit
         att_ref[:, start : start + group, low : low + HD] = mixed.reshape(frames, group, HD)
-    project_out(att_ref[...].reshape(frames * places, heads_width).astype(BF16), out_weight_ref, out_ref)
-
-
-def time_layer(parts, mod, weight, out_weight, rows, frames):
-    count, _, width = parts.shape
+    out_ref[...] = att_ref[...].reshape(frames * places, heads_width).astype(BF16)
+
+
+def time_layer(parts, mod, weight, rows, frames):
     model_width, heads_width = weight.shape[1:]
     return pl.pallas_call(
         time_kernel,
-        in_specs=vmem(4),
+        in_specs=vmem(3),
         out_specs=vmem(1)[0],
-        out_shape=jax.ShapeDtypeStruct((count, rows, width), BF16),
+        out_shape=jax.ShapeDtypeStruct((rows, heads_width), BF16),
         scratch_shapes=[
             pltpu.VMEM((rows, model_width), BF16),
             pltpu.VMEM((3, frames, rows // frames, heads_width), F32),
@@ -300,12 +336,12 @@
         ],
         compiler_params=params(),
         cost_estimate=pl.CostEstimate(
-            flops=2 * rows * (weight.size + out_weight.size),
-            bytes_accessed=2 * (weight.size + out_weight.size + 2 * parts.size),
+            flops=2 * rows * weight.size,
+            bytes_accessed=2 * (weight.size + parts.size),
             transcendentals=rows * BLOCK * heads_width // HD,
         ),
         name="time_layer",
-    )(parts, mod, weight, out_weight)
+    )(parts, mod, weight)
 
 
 def on_device(tokens, block_mask, space_qkv, space_out, space_mod, time_qkv, time_out, time_mod):
@@ -329,17 +365,37 @@
     def gathered(shard):
         return across_parts(jnp.broadcast_to(shard[None], (parts,) + shard.shape))
 
+    def from_other_core(values):
+        return lax.ppermute(values, "seq", [(i, i ^ 1) for i in range(seq_count)])
+
+    def from_other_side(values):
+        return lax.ppermute(values, "fsdp", [(i, i ^ 1) for i in range(parts)])
+
+    def projected(attended, weight, half):
+        return project(
+            where, attended, from_other_side(attended), weight, half, from_other_core(half)
+        )
+
+    def across_x(values):
+        same_side = [[2 * group + side for group in range(parts // 2)] for side in range(2)]
+        return lax.all_to_all(
+            values, "fsdp", split_axis=0, concat_axis=0, tiled=True, axis_index_groups=same_side
+        )
+
     local = tokens.reshape(rows, width)
-    queries, own = space_in(gathered(pack(local)), space_mod, jnp.swapaxes(space_qkv, 0, 1), rows)
-    other = lax.ppermute(own, "seq", [(i, i ^ 1) for i in range(seq_count)])
-    partial = space_attend(where, block_mask.reshape(-1), queries, own, other, space_out, parts)
-    stream, sent = join(where, across_parts(partial), local, space_mod)
-    wide = gathered(pack(across_frames(sent)))
-    partial_time = time_layer(wide, time_mod, jnp.swapaxes(time_qkv, 0, 1), time_out, rows, frames)
-    total = jnp.sum(across_parts(partial_time).astype(F32), axis=0).astype(BF16)
-    returned = across_frames(total)
-    gate = lax.dynamic_slice_in_dim(time_mod[2], lax.axis_index("fsdp") * width, width, 0)
-    return (stream + gate * returned.astype(F32)).reshape(tokens.shape)
+    packed, lent = lax.optimization_barrier((pack(local), lend(where, space_out, width)))
+    half = from_other_side(lent)
+    queries, own = space_in(gathered(packed), space_mod, jnp.swapaxes(space_qkv, 0, 1), rows)
+    attended = space_attend(where, block_mask.reshape(-1), queries, own, from_other_core(own))
+    attended, time_weight = lax.optimization_barrier((attended, time_out))
+    lent = lend(where, time_weight, width)
+    partial, lent = lax.optimization_barrier((projected(attended, space_out, half), lent))
+    half = from_other_side(lent)
+    stream, sent = join(where, across_x(partial), local, space_mod, (F32, BF16))
+    packed, half = lax.optimization_barrier((pack(across_frames(sent)), half))
+    attended = time_layer(gathered(packed), time_mod, jnp.swapaxes(time_qkv, 0, 1), rows, frames)
+    arrived = across_x(projected(across_frames(attended), time_out, half))
+    return join(where, arrived, stream, time_mod, (F32,))[0].reshape(tokens.shape)
 
 
 def solution(mesh):

time: 189 us -> 192 us (1.016)
  blocking collectives: 158 us -> 66.7 us
  waiting for transfers between devices: 10.6 us -> 63.3 us
  starting transfers between devices: 5.36 us -> 32.8 us
  local copies, waits for them, and re-layouts: 1.83 us -> 10.7 us
  Pallas kernels: 11 us -> 17.6 us
  other arithmetic: 2.08 us -> 0.08 us
    all_to_all x4 -> x1, blocking collectives: 139 us -> 34 us  [across_parts(): lax.all_to_all(values, 'fsdp', split_axis=0, concat_axis=0, tiled=True)]
    all_to_all x0 -> x1, waiting for transfers between devices: none -> 32.1 us  [across_parts(): lax.all_to_all(values, 'fsdp', split_axis=0, concat_axis=0, tiled=True)]
    all_to_all x1 -> x2, blocking collectives: 18.8 us -> 32.7 us  [across_x(): lax.all_to_all(values, 'fsdp', split_axis=0, concat_axis=0, tiled=True, a...]
    ppermute x1 -> x7, waiting for transfers between devices: 1.32 us -> 15.2 us  [the longest x4 14 us: from_other_side(): return lax.ppermute(values, 'fsdp', [(i, i ^ 1) for i in range(parts)])]
    all_to_all x1 -> x2, starting transfers between devices: 5.26 us -> 16.6 us  [across_frames(): lax.all_to_all(values.reshape(frames, rows // frames, -1), 'seq', split_a...]
    ppermute x1 -> x7, starting transfers between devices: 0.09 us -> 9.13 us  [the longest x4 8.62 us: from_other_side(): return lax.ppermute(values, 'fsdp', [(i, i ^ 1) for i in range(parts)])]
    unnamed x21 -> x23, local copies, waits for them, and re-layouts: 1.24 us -> 8.71 us
    all_to_all x0 -> x1, starting transfers between devices: none -> 7.06 us  [across_parts(): lax.all_to_all(values, 'fsdp', split_axis=0, concat_axis=0, tiled=True)]
  transfers between devices with their start and end apart: 2 -> 10, of which waited for: 2 -> 7; matrix products, arithmetic and copies ran while one was open for 0% -> 0% of each run, Pallas kernels for 0% -> 3%
where the time goes in v7:
time: 192 us; the launch traced here: 191 us
  blocking collectives  66.7 us (35%)
  waiting for transfers between devices  63.3 us (33%)
  starting transfers between devices  32.8 us (17%)
  Pallas kernels  17.6 us (9%)
  local copies, waits for them, and re-layouts  10.7 us (6%)
    all_to_all x1, blocking collectives, across_parts(): lax.all_to_all(values, 'fsdp', split_axis=0, concat_axis=0, tiled=True)  34 us
    all_to_all x2, blocking collectives, across_x(): lax.all_to_all(values, 'fsdp', split_axis=0, concat_axis=0, tiled=True, a...  32.7 us
    all_to_all x1, waiting for transfers between devices, across_parts(): lax.all_to_all(values, 'fsdp', split_axis=0, concat_axis=0, tiled=True)  32.1 us
    all_to_all x2, starting transfers between devices, across_frames(): lax.all_to_all(values.reshape(frames, rows // frames, -1), 'seq', split_a...  16.6 us
    all_to_all x2, waiting for transfers between devices, across_frames(): lax.all_to_all(values.reshape(frames, rows // frames, -1), 'seq', split_a...  16 us
    ppermute x4, waiting for transfers between devices, from_other_side(): return lax.ppermute(values, 'fsdp', [(i, i ^ 1) for i in range(parts)])  14 us
    unnamed x23, local copies, waits for them, and re-layouts  8.71 us
    ppermute x4, starting transfers between devices, from_other_side(): return lax.ppermute(values, 'fsdp', [(i, i ^ 1) for i in range(parts)])  8.62 us
  transfers between devices with their start and end apart: 10, of which 7 were waited for; matrix products, arithmetic and copies ran while one was open for 0% of the time, Pallas kernels for 3%

profile of v7, /device:TPU:32, one launch (start us, length us, event | category | flops | bytes accessed | tf_op | source)
XLA Modules:
  0.0 191.2 jit_solution(10314149725379876552)
XLA Ops:
  3.5 1.7 broadcast_in_dim.4
  5.1 7.1 %all-to-all-start = ((bf16[8,392,384]{2,1,0:T(8,128)(2,1)}), bf16[8,392,384]{2,1,0:T(8,128)(2,1)S(1)}, u32[]{:S(2)}, u32[]{:S(2)}) async-start(bf16[8,392,384]{2,1,0:T(8,128)(2,1)} %broadcast_in_dim.4), calls=%async_computation | async-start | bytes 4816896 | tf_op jit(solution)/shard_map/all_to_all | solution.py:363
  12.2 3.5 %collective-permute-start.2 = (bf16[4,128,384]{2,1,0:T(8,128)(2,1)S(1)}, bf16[4,128,384]{2,1,0:T(8,128)(2,1)S(1)}, u32[]{:S(2)}, u32[]{:S(2)}) collective-permute-start(bf16[4,128,384]{2,1,0:T(8,128)(2,1)S(1)} %lend.2), channel_id=1, source_target_pairs={{0,1},{1,0},{2,3},{3,2},{4,5},{5,4},{6,7},{7,6},{8,9},{9,8},{10,11... | collective-permute-start | bytes 1179656 | tf_op jit(solution)/shard_map/ppermute | solution.py:372
  15.7 32.1 %all-to-all-done.parts_ref = bf16[8,392,384]{2,1,0:T(8,128)(2,1)S(1)} async-done(((bf16[8,392,384]{2,1,0:T(8,128)(2,1)}), bf16[8,392,384]{2,1,0:T(8,128)(2,1)S(1)}, u32[]{:S(2)}, u32[]{:S(2)}) %all-to-all-start) | async-done | bytes 2408480 | tf_op jit(solution)/shard_map/all_to_all | solution.py:363
  47.8 2.3 %copy-done.5 = bf16[3072,3,256]{2,0,1:T(8,128)(2,1)S(1)} copy-done((bf16[3072,3,256]{2,0,1:T(8,128)(2,1)S(1)}, bf16[3072,3,256]{2,0,1:T(8,128)(2,1)}, u32[]{:S(2)}) %copy-start.5) | copy-done | bytes 4718616
  50.1 3.6 %space_in.1 = (bf16[384,256]{1,0:T(8,128)(2,1)S(1)}, bf16[2,384,256]{2,1,0:T(8,128)(2,1)}) custom-call(bf16[8,392,384]{2,1,0:T(8,128)(2,1)S(1)} %all-to-all-done.parts_ref, f32[3,3072]{1,0:T(4,128)S(1)} %copy-done.8, bf16[3,3072,256]{2,1,0:T(8,128)(2,1)S(1)} %bitcast.12), custom_call_target="tpu_custom_call" | custom-call | flops 1811939328 | bytes 7127040 | tf_op jit(solution)/shard_map/space_in/pallas_call | solution.py:133
  55.7 2.2 %space_attend.1.own_ref = bf16[384,256]{1,0:T(8,128)(2,1)S(1)} custom-call(s32[3]{0:T(128)S(1)} %pad_add_fusion.where_ref, s32[576]{0:T(1024)S(1)} %reshape.23.mask_ref, bf16[384,256]{1,0:T(8,128)(2,1)S(1)} %get-tuple-element.18.q_ref, bf16[2,384,256]{2,1,0:T(8,128)(2,1)} %get-tuple-element.19.own_ref, bf16[2,384,256]{2,1,0:T(8,128)(2,1)S(1)} %collective-permute-done.other_ref), custom_call_target="tpu_custom_call" | custom-call | flops 301989888 | bytes 1179648 | tf_op jit(solution)/shard_map/space_attend/pallas_call | solution.py:203
  57.8 1.7 collective-permute-start.1
  61.5 4.8 %collective-permute-done.1.partner_ref = bf16[384,256]{1,0:T(8,128)(2,1)S(1)} collective-permute-done((bf16[384,256]{1,0:T(8,128)(2,1)S(1)}, bf16[384,256]{1,0:T(8,128)(2,1)S(1)}, u32[]{:S(2)}, u32[]{:S(2)}) %collective-permute-start.1) | collective-permute-done | bytes 196640 | tf_op jit(solution)/shard_map/ppermute | solution.py:372
  66.4 1.6 project.2
  68.0 18.7 %all_to_all.30.parts_ref = bf16[4,384,384]{2,1,0:T(8,128)(2,1)S(1)} all-to-all(bf16[4,384,384]{2,1,0:T(8,128)(2,1)S(1)} %project.2), channel_id=1, replica_groups={{0,2,4,6},{1,3,5,7},{8,10,12,14},{9,11,13,15},{16,18,20,22},{17,19,21,2..., dimensions={0} | all-to-all | bytes 2359296 | tf_op jit(solution)/shard_map/all_to_all | solution.py:381
  88.1 8.7 %all-to-all-start.2 = ((bf16[16,24,384]{2,1,0:T(8,128)(2,1)}), bf16[16,24,384]{2,1,0:T(8,128)(2,1)S(1)}, u32[]{:S(2)}, u32[]{:S(2)}) async-start(bf16[16,24,384]{2,1,0:T(8,128)(2,1)} %bitcast.5), calls=%async_computation.2 | async-start | bytes 589824 | tf_op jit(solution)/shard_map/all_to_all | solution.py:357
  96.8 2.2 %collective-permute-start.4 = (bf16[4,128,384]{2,1,0:T(8,128)(2,1)S(1)}, bf16[4,128,384]{2,1,0:T(8,128)(2,1)S(1)}, u32[]{:S(2)}, u32[]{:S(2)}) collective-permute-start(bf16[4,128,384]{2,1,0:T(8,128)(2,1)S(1)} %lend.3), channel_id=1, source_target_pairs={{0,1},{1,0},{2,3},{3,2},{4,5},{5,4},{6,7},{7,6},{8,9},{9,8},{10,11... | collective-permute-start | bytes 1179656 | tf_op jit(solution)/shard_map/ppermute | solution.py:372
  99.0 7.4 %all-to-all-done.2 = bf16[16,24,384]{2,1,0:T(8,128)(2,1)S(1)} async-done(((bf16[16,24,384]{2,1,0:T(8,128)(2,1)}), bf16[16,24,384]{2,1,0:T(8,128)(2,1)S(1)}, u32[]{:S(2)}, u32[]{:S(2)}) %all-to-all-start.2) | async-done | bytes 294944 | tf_op jit(solution)/shard_map/all_to_all | solution.py:357
  106.7 3.3 %collective-permute-done.4.half_ref = bf16[4,128,384]{2,1,0:T(8,128)(2,1)S(1)} collective-permute-done((bf16[4,128,384]{2,1,0:T(8,128)(2,1)S(1)}, bf16[4,128,384]{2,1,0:T(8,128)(2,1)S(1)}, u32[]{:S(2)}, u32[]{:S(2)}) %collective-permute-start.4) | collective-permute-done | bytes 393248 | tf_op jit(solution)/shard_map/ppermute | solution.py:372
  110.2 34.0 %all_to_all.31.parts_ref = bf16[8,392,384]{2,1,0:T(8,128)(2,1)S(1)} all-to-all(bf16[8,392,384]{2,1,0:T(8,128)(2,1)S(1)} %broadcast_in_dim.5), channel_id=1, replica_groups=mesh['seq'=32,'fsdp'=8] {'fsdp'}, dimensions={0} | all-to-all | bytes 4816896 | tf_op jit(solution)/shard_map/all_to_all | solution.py:363
  144.2 2.3 %copy-done.4 = bf16[3072,3,256]{2,0,1:T(8,128)(2,1)S(1)} copy-done((bf16[3072,3,256]{2,0,1:T(8,128)(2,1)S(1)}, bf16[3072,3,256]{2,0,1:T(8,128)(2,1)}, u32[]{:S(2)}) %copy-start.4) | copy-done | bytes 4718616
  146.5 3.8 %time_layer.1 = bf16[384,256]{1,0:T(8,128)(2,1)} custom-call(bf16[8,392,384]{2,1,0:T(8,128)(2,1)S(1)} %all_to_all.31.parts_ref, f32[3,3072]{1,0:T(4,128)S(1)} %copy-done.9, bf16[3,3072,256]{2,1,0:T(8,128)(2,1)S(1)} %bitcast.11), custom_call_target="tpu_custom_call" | custom-call | flops 1811939328 | bytes 7127040 | tf_op jit(solution)/shard_map/time_layer/pallas_call | solution.py:327
  150.4 7.9 %all-to-all-start.4 = ((bf16[16,24,256]{2,1,0:T(8,128)(2,1)}), bf16[16,24,256]{2,1,0:T(8,128)(2,1)S(1)}, u32[]{:S(2)}, u32[]{:S(2)}) async-start(bf16[16,24,256]{2,1,0:T(8,128)(2,1)} %bitcast.8), calls=%async_computation.4 | async-start | bytes 393216 | tf_op jit(solution)/shard_map/all_to_all | solution.py:357
  158.2 8.6 %all-to-all-done.4 = bf16[16,24,256]{2,1,0:T(8,128)(2,1)S(1)} async-done(((bf16[16,24,256]{2,1,0:T(8,128)(2,1)}), bf16[16,24,256]{2,1,0:T(8,128)(2,1)S(1)}, u32[]{:S(2)}, u32[]{:S(2)}) %all-to-all-start.4) | async-done | bytes 196640 | tf_op jit(solution)/shard_map/all_to_all | solution.py:357
  168.1 5.9 %collective-permute-done.5.partner_ref = bf16[384,256]{1,0:T(8,128)(2,1)S(1)} collective-permute-done((bf16[384,256]{1,0:T(8,128)(2,1)S(1)}, bf16[384,256]{1,0:T(8,128)(2,1)S(1)}, u32[]{:S(2)}, u32[]{:S(2)}) %collective-permute-start.5) | collective-permute-done | bytes 196640 | tf_op jit(solution)/shard_map/ppermute | solution.py:372
  174.0 1.6 project.3
  175.7 14.0 %all_to_all.32.parts_ref = bf16[4,384,384]{2,1,0:T(8,128)(2,1)S(1)} all-to-all(bf16[4,384,384]{2,1,0:T(8,128)(2,1)S(1)} %project.3), channel_id=1, replica_groups={{0,2,4,6},{1,3,5,7},{8,10,12,14},{9,11,13,15},{16,18,20,22},{17,19,21,2..., dimensions={0} | all-to-all | bytes 2359296 | tf_op jit(solution)/shard_map/all_to_all | solution.py:381
  189.7 1.5 join.3
  (37 shorter events, 10.7 us)
Async XLA Ops:
  0.0 1.1 copy-start.6
  1.5 1.4 copy-start
  5.1 42.7 %copy-start.8 = (f32[3,3072]{1,0:T(4,128)S(1)}, f32[3,3072]{1,0:T(4,128)}, u32[]{:S(2)}) copy-start(f32[3,3072]{1,0:T(4,128)} %mod_ref.5) | copy-start | bytes 110596
  5.1 42.7 %all-to-all-start = ((bf16[8,392,384]{2,1,0:T(8,128)(2,1)}), bf16[8,392,384]{2,1,0:T(8,128)(2,1)S(1)}, u32[]{:S(2)}, u32[]{:S(2)}) async-start(bf16[8,392,384]{2,1,0:T(8,128)(2,1)} %broadcast_in_dim.4), calls=%async_computation | async-start | bytes 4816896 | tf_op jit(solution)/shard_map/all_to_all | solution.py:363
  12.2 41.5 %collective-permute-start.2 = (bf16[4,128,384]{2,1,0:T(8,128)(2,1)S(1)}, bf16[4,128,384]{2,1,0:T(8,128)(2,1)S(1)}, u32[]{:S(2)}, u32[]{:S(2)}) collective-permute-start(bf16[4,128,384]{2,1,0:T(8,128)(2,1)S(1)} %lend.2), channel_id=1, source_target_pairs={{0,1},{1,0},{2,3},{3,2},{4,5},{5,4},{6,7},{7,6},{8,9},{9,8},{10,11... | collective-permute-start | bytes 1179656 | tf_op jit(solution)/shard_map/ppermute | solution.py:372
  47.8 2.3 %copy-start.5 = (bf16[3072,3,256]{2,0,1:T(8,128)(2,1)S(1)}, bf16[3072,3,256]{2,0,1:T(8,128)(2,1)}, u32[]{:S(2)}) copy-start(bf16[3072,3,256]{2,0,1:T(8,128)(2,1)} %param.10) | copy-start | bytes 14155780
  50.1 4.1 %copy-start.10 = (s32[16,6,6]{0,2,1:T(8,128)S(1)}, s32[16,6,6]{0,2,1:T(8,128)}, u32[]{:S(2)}) copy-start(s32[16,6,6]{0,2,1:T(8,128)} %param.9) | copy-start | bytes 6916
  53.7 12.6 %copy-start.1 = (bf16[256,3072]{1,0:T(8,128)(2,1)S(1)}, bf16[256,3072]{1,0:T(8,128)(2,1)}, u32[]{:S(2)}) copy-start(bf16[256,3072]{1,0:T(8,128)(2,1)} %weight_ref.4) | copy-start | bytes 4718596
  53.7 1.9 %collective-permute-start = (bf16[2,384,256]{2,1,0:T(8,128)(2,1)}, bf16[2,384,256]{2,1,0:T(8,128)(2,1)S(1)}, u32[]{:S(2)}, u32[]{:S(2)}) collective-permute-start(bf16[2,384,256]{2,1,0:T(8,128)(2,1)} %get-tuple-element.19.own_ref), channel_id=1, source_target_pairs={{0,8},{8,0},{16,24},{24,16},{32,40},{40,32},{48,56},{56,48},{64,72... | collective-permute-start | bytes 1179656 | tf_op jit(solution)/shard_map/ppermute | solution.py:369
  53.7 7.8 %collective-permute-start.3 = (bf16[4,128,384]{2,1,0:T(8,128)(2,1)S(1)}, bf16[4,128,384]{2,1,0:T(8,128)(2,1)S(1)}, u32[]{:S(2)}, u32[]{:S(2)}) collective-permute-start(bf16[4,128,384]{2,1,0:T(8,128)(2,1)S(1)} %collective-permute-done.2.half_ref), channel_id=1, source_target_pairs={{0,8},{8,0},{16,24},{24,16},{32,40},{40,32},{48,56},{56,48},{64,72... | collective-permute-start | bytes 1179656 | tf_op jit(solution)/shard_map/ppermute | solution.py:369
  57.8 8.5 %collective-permute-start.1 = (bf16[384,256]{1,0:T(8,128)(2,1)S(1)}, bf16[384,256]{1,0:T(8,128)(2,1)S(1)}, u32[]{:S(2)}, u32[]{:S(2)}) collective-permute-start(bf16[384,256]{1,0:T(8,128)(2,1)S(1)} %space_attend.1.own_ref), channel_id=1, source_target_pairs={{0,1},{1,0},{2,3},{3,2},{4,5},{5,4},{6,7},{7,6},{8,9},{9,8},{10,11... | collective-permute-start | bytes 589832 | tf_op jit(solution)/shard_map/ppermute | solution.py:372
  59.5 1.4 copy-start.2
  61.5 25.2 %copy-start.7 = (f32[1,384,384]{2,1,0:T(8,128)S(1)}, f32[1,384,384]{2,1,0:T(8,128)}, u32[]{:S(2)}) copy-start(f32[1,384,384]{2,1,0:T(8,128)} %param.8) | copy-start | bytes 1769476
  88.1 18.3 %all-to-all-start.2 = ((bf16[16,24,384]{2,1,0:T(8,128)(2,1)}), bf16[16,24,384]{2,1,0:T(8,128)(2,1)S(1)}, u32[]{:S(2)}, u32[]{:S(2)}) async-start(bf16[16,24,384]{2,1,0:T(8,128)(2,1)} %bitcast.5), calls=%async_computation.2 | async-start | bytes 589824 | tf_op jit(solution)/shard_map/all_to_all | solution.py:357
  96.8 13.1 %collective-permute-start.4 = (bf16[4,128,384]{2,1,0:T(8,128)(2,1)S(1)}, bf16[4,128,384]{2,1,0:T(8,128)(2,1)S(1)}, u32[]{:S(2)}, u32[]{:S(2)}) collective-permute-start(bf16[4,128,384]{2,1,0:T(8,128)(2,1)S(1)} %lend.3), channel_id=1, source_target_pairs={{0,1},{1,0},{2,3},{3,2},{4,5},{5,4},{6,7},{7,6},{8,9},{9,8},{10,11... | collective-permute-start | bytes 1179656 | tf_op jit(solution)/shard_map/ppermute | solution.py:372
  110.2 34.0 %copy-start.9 = (f32[3,3072]{1,0:T(4,128)S(1)}, f32[3,3072]{1,0:T(4,128)}, u32[]{:S(2)}) copy-start(f32[3,3072]{1,0:T(4,128)} %mod_ref.7) | copy-start | bytes 110596
  144.2 2.3 %copy-start.4 = (bf16[3072,3,256]{2,0,1:T(8,128)(2,1)S(1)}, bf16[3072,3,256]{2,0,1:T(8,128)(2,1)}, u32[]{:S(2)}) copy-start(bf16[3072,3,256]{2,0,1:T(8,128)(2,1)} %param.13) | copy-start | bytes 14155780
  146.5 27.5 %copy-start.3 = (bf16[256,3072]{1,0:T(8,128)(2,1)S(1)}, bf16[256,3072]{1,0:T(8,128)(2,1)}, u32[]{:S(2)}) copy-start(bf16[256,3072]{1,0:T(8,128)(2,1)} %weight_ref.6) | copy-start | bytes 4718596
  150.4 16.5 %all-to-all-start.4 = ((bf16[16,24,256]{2,1,0:T(8,128)(2,1)}), bf16[16,24,256]{2,1,0:T(8,128)(2,1)S(1)}, u32[]{:S(2)}, u32[]{:S(2)}) async-start(bf16[16,24,256]{2,1,0:T(8,128)(2,1)} %bitcast.8), calls=%async_computation.4 | async-start | bytes 393216 | tf_op jit(solution)/shard_map/all_to_all | solution.py:357
  158.2 9.9 %collective-permute-start.6 = (bf16[4,128,384]{2,1,0:T(8,128)(2,1)S(1)}, bf16[4,128,384]{2,1,0:T(8,128)(2,1)S(1)}, u32[]{:S(2)}, u32[]{:S(2)}) collective-permute-start(bf16[4,128,384]{2,1,0:T(8,128)(2,1)S(1)} %collective-permute-done.4.half_ref), channel_id=1, source_target_pairs={{0,8},{8,0},{16,24},{24,16},{32,40},{40,32},{48,56},{56,48},{64,72... | collective-permute-start | bytes 1179656 | tf_op jit(solution)/shard_map/ppermute | solution.py:369
  166.9 7.2 %collective-permute-start.5 = (bf16[384,256]{1,0:T(8,128)(2,1)S(1)}, bf16[384,256]{1,0:T(8,128)(2,1)S(1)}, u32[]{:S(2)}, u32[]{:S(2)}) collective-permute-start(bf16[384,256]{1,0:T(8,128)(2,1)S(1)} %bitcast.16), channel_id=1, source_target_pairs={{0,1},{1,0},{2,3},{3,2},{4,5},{5,4},{6,7},{7,6},{8,9},{9,8},{10,11... | collective-permute-start | bytes 589832 | tf_op jit(solution)/shard_map/ppermute | solution.py:372

commit v8 on v7

--- a/solution.py
+++ b/solution.py
@@ -12,7 +12,7 @@
 BLOCK = 128
 EPS = 1e-06
 SCALE = 1.0 / math.sqrt(HD)
-VMEM_LIMIT = 24 * 1024 * 1024
+VMEM_LIMIT = 48 * 1024 * 1024
 ROW_TILE = 192
 F32 = jnp.float32
 BF16 = jnp.bfloat16
@@ -108,20 +108,37 @@
             ).astype(BF16)
 
 
-def qkv_rows(normed_ref, weight_ref):
+def qkv_rows(parts_ref, mod_ref, weight_ref, normed_ref, held_ref, done):
+    copies = [
+        pltpu.make_async_copy(weight_ref.at[which], held_ref.at[which], done.at[which])
+        for which in range(3)
+    ]
+    for copy in copies:
+        copy.start()
+    modulate(parts_ref, mod_ref, normed_ref)
     rows = normed_ref.shape[0]
     tile = ROW_TILE if rows % ROW_TILE == 0 else rows
     for which in range(3):
+        copies[which].wait()
         for start in range(0, rows, tile):
             span = slice(start, start + tile)
             yield which, span, jnp.dot(
-                normed_ref[span, :], weight_ref[which], preferred_element_type=F32
+                normed_ref[span, :], held_ref[which], preferred_element_type=F32
             )
 
 
-def space_in_kernel(parts_ref, mod_ref, weight_ref, q_ref, kv_ref, normed_ref):
-    modulate(parts_ref, mod_ref, normed_ref)
-    for which, span, values in qkv_rows(normed_ref, weight_ref):
+def qkv_operands(rows, weight):
+    specs = vmem(2) + [pl.BlockSpec(memory_space=pl.ANY)]
+    scratch = [
+        pltpu.VMEM((rows, weight.shape[1]), BF16),
+        pltpu.VMEM(weight.shape, BF16),
+        pltpu.SemaphoreType.DMA((3,)),
+    ]
+    return specs, scratch
+
+
+def space_in_kernel(parts_ref, mod_ref, weight_ref, q_ref, kv_ref, *scratch):
+    for which, span, values in qkv_rows(parts_ref, mod_ref, weight_ref, *scratch):
         if which == 0:
             q_ref[span, :] = values.astype(BF16)
         else:
@@ -129,16 +146,17 @@
 
 
 def space_in(parts, mod, weight, rows):
-    model_width, heads_width = weight.shape[1:]
+    heads_width = weight.shape[2]
+    specs, scratch = qkv_operands(rows, weight)
     return pl.pallas_call(
         space_in_kernel,
-        in_specs=vmem(3),
+        in_specs=specs,
         out_specs=vmem(2),
         out_shape=[
             jax.ShapeDtypeStruct((rows, heads_width), BF16),
             jax.ShapeDtypeStruct((2, rows, heads_width), BF16),
         ],
-        scratch_shapes=[pltpu.VMEM((rows, model_width), BF16)],
+        scratch_shapes=scratch,
         compiler_params=params(),
         cost_estimate=pl.CostEstimate(
             flops=2 * rows * weight.size,
@@ -215,26 +233,43 @@
     )(where, mask, queries, own, other)
 
 
-def lend_kernel(where_ref, weight_ref, out_ref):
-    groups, count, width = out_ref.shape
-    lines = pl.ds(pl.multiple_of(where_ref[1] * count, 128), count)
-    other_side = 1 - where_ref[2] % 2
-    for group in range(groups):
-        first = pl.multiple_of((2 * group + other_side) * width, 128)
-        out_ref[group] = weight_ref[lines, pl.ds(first, width)]
-
-
-def lend(where, weight, width):
-    heads_width, model_width = weight.shape
+def lend_kernel(where_ref, *refs):
+    layers = (len(refs) - 1) // 2
+    done = refs[-1]
+    copies = []
+    for weight_ref, out_ref in zip(refs[:layers], refs[layers : 2 * layers]):
+        groups, count, width = out_ref.shape
+        lines = pl.ds(pl.multiple_of(where_ref[1] * count, 128), count)
+        other_side = 1 - where_ref[2] % 2
+        for group in range(groups):
+            first = pl.multiple_of((2 * group + other_side) * width, 128)
+            copies.append(
+                pltpu.make_async_copy(
+                    weight_ref.at[lines, pl.ds(first, width)], out_ref.at[group], done.at[len(copies)]
+                )
+            )
+    for copy in copies:
+        copy.start()
+    for copy in copies:
+        copy.wait()
+
+
+def lend(where, weights, width):
+    heads_width, model_width = weights[0].shape
+    groups = model_width // (2 * width)
+    shape = jax.ShapeDtypeStruct((groups, heads_width // 2, width), BF16)
     return pl.pallas_call(
         lend_kernel,
-        in_specs=smem(1) + vmem(1),
-        out_specs=vmem(1)[0],
-        out_shape=jax.ShapeDtypeStruct((model_width // (2 * width), heads_width // 2, width), BF16),
-        compiler_params=params(),
-        cost_estimate=pl.CostEstimate(flops=0, bytes_accessed=2 * weight.size, transcendentals=0),
+        in_specs=smem(1) + [pl.BlockSpec(memory_space=pl.ANY)] * len(weights),
+        out_specs=vmem(len(weights)),
+        out_shape=[shape] * len(weights),
+        scratch_shapes=[pltpu.SemaphoreType.DMA((groups * len(weights),))],
+        compiler_params=params(),
+        cost_estimate=pl.CostEstimate(
+            flops=0, bytes_accessed=2 * len(weights) * weights[0].size, transcendentals=0
+        ),
         name="lend",
-    )(where, weight)
+    )(where, *weights)
 
 
 def project_kernel(where_ref, own_ref, partner_ref, weight_ref, half_ref, other_half_ref, out_ref, lent_ref):
@@ -295,10 +330,9 @@
     )(where, parts, tokens, mod)
 
 
-def time_kernel(parts_ref, mod_ref, weight_ref, out_ref, normed_ref, packed_ref, att_ref):
-    modulate(parts_ref, mod_ref, normed_ref)
+def time_kernel(parts_ref, mod_ref, weight_ref, out_ref, packed_ref, att_ref, *scratch):
     frames, places, heads_width = att_ref.shape
-    for which, span, values in qkv_rows(normed_ref, weight_ref):
+    for which, span, values in qkv_rows(parts_ref, mod_ref, weight_ref, *scratch):
         first = span.start // places
         count = values.shape[0] // places
         packed_ref[which, first : first + count] = values.reshape(count, places, heads_width)
@@ -323,17 +357,18 @@
 
 
 def time_layer(parts, mod, weight, rows, frames):
-    model_width, heads_width = weight.shape[1:]
+    heads_width = weight.shape[2]
+    specs, scratch = qkv_operands(rows, weight)
     return pl.pallas_call(
         time_kernel,
-        in_specs=vmem(3),
+        in_specs=specs,
         out_specs=vmem(1)[0],
         out_shape=jax.ShapeDtypeStruct((rows, heads_width), BF16),
         scratch_shapes=[
-            pltpu.VMEM((rows, model_width), BF16),
             pltpu.VMEM((3, frames, rows // frames, heads_width), F32),
             pltpu.VMEM((frames, rows // frames, heads_width), F32),
-        ],
+        ]
+        + scratch,
         compiler_params=params(),
         cost_estimate=pl.CostEstimate(
             flops=2 * rows * weight.size,
@@ -383,17 +418,17 @@
         )
 
     local = tokens.reshape(rows, width)
-    packed, lent = lax.optimization_barrier((pack(local), lend(where, space_out, width)))
-    half = from_other_side(lent)
-    queries, own = space_in(gathered(packed), space_mod, jnp.swapaxes(space_qkv, 0, 1), rows)
+    space_lent, time_lent = lend(where, (space_out, time_out), width)
+    half = from_other_side(space_lent)
+    queries, own = space_in(gathered(pack(local)), space_mod, jnp.swapaxes(space_qkv, 0, 1), rows)
     attended = space_attend(where, block_mask.reshape(-1), queries, own, from_other_core(own))
-    attended, time_weight = lax.optimization_barrier((attended, time_out))
-    lent = lend(where, time_weight, width)
-    partial, lent = lax.optimization_barrier((projected(attended, space_out, half), lent))
-    half = from_other_side(lent)
+    partial = projected(attended, space_out, half)
+    partial, time_lent = lax.optimization_barrier((partial, time_lent))
+    half = from_other_side(time_lent)
     stream, sent = join(where, across_x(partial), local, space_mod, (F32, BF16))
-    packed, half = lax.optimization_barrier((pack(across_frames(sent)), half))
-    attended = time_layer(gathered(packed), time_mod, jnp.swapaxes(time_qkv, 0, 1), rows, frames)
+    sent, half = lax.optimization_barrier((sent, half))
+    wide = gathered(pack(across_frames(sent)))
+    attended = time_layer(wide, time_mod, jnp.swapaxes(time_qkv, 0, 1), rows, frames)
     arrived = across_x(projected(across_frames(attended), time_out, half))
     return join(where, arrived, stream, time_mod, (F32,))[0].reshape(tokens.shape)
 

time: 192 us -> 181 us (0.943)
  starting transfers between devices: 32.8 us -> 24.1 us
  local copies, waits for them, and re-layouts: 10.7 us -> 7.44 us
    all_to_all x2 -> x1, blocking collectives: 32.7 us -> 14 us  [across_x(): lax.all_to_all(values, 'fsdp', split_axis=0, concat_axis=0, tiled=True, a...]
    all_to_all x0 -> x1, blocking collectives: none -> 17.9 us  [across_frames(): lax.all_to_all(values.reshape(frames, rows // frames, -1), 'seq', split_a...]
    all_to_all x0 -> x1, waiting for transfers between devices: none -> 14.6 us  [across_x(): lax.all_to_all(values, 'fsdp', split_axis=0, concat_axis=0, tiled=True, a...]
    all_to_all x2 -> x1, starting transfers between devices: 16.6 us -> 4.82 us  [across_frames(): lax.all_to_all(values.reshape(frames, rows // frames, -1), 'seq', split_a...]
    all_to_all x2 -> x1, waiting for transfers between devices: 16 us -> 8.6 us  [across_frames(): lax.all_to_all(values.reshape(frames, rows // frames, -1), 'seq', split_a...]
    all_to_all x1, waiting for transfers between devices: 32.1 us -> 27.4 us  [across_parts(): lax.all_to_all(values, 'fsdp', split_axis=0, concat_axis=0, tiled=True)]
    all_to_all x0 -> x1, starting transfers between devices: none -> 3.53 us  [across_x(): lax.all_to_all(values, 'fsdp', split_axis=0, concat_axis=0, tiled=True, a...]
    unnamed x23 -> x19, local copies, waits for them, and re-layouts: 8.71 us -> 5.43 us
  transfers between devices with their start and end apart: 10 -> 10, of which waited for: 7 -> 6; matrix products, arithmetic and copies ran while one was open for 0% -> 0% of each run, Pallas kernels for 3% -> 4%
where the time goes in v8:
time: 181 us; the launch traced here: 180 us
  blocking collectives  64.8 us (36%)
  waiting for transfers between devices  64.3 us (36%)
  starting transfers between devices  24.1 us (13%)
  Pallas kernels  19.3 us (11%)
  local copies, waits for them, and re-layouts  7.44 us (4%)
    all_to_all x1, blocking collectives, across_parts(): lax.all_to_all(values, 'fsdp', split_axis=0, concat_axis=0, tiled=True)  32.8 us
    all_to_all x1, waiting for transfers between devices, across_parts(): lax.all_to_all(values, 'fsdp', split_axis=0, concat_axis=0, tiled=True)  27.4 us
    all_to_all x1, blocking collectives, across_frames(): lax.all_to_all(values.reshape(frames, rows // frames, -1), 'seq', split_a...  17.9 us
    all_to_all x1, waiting for transfers between devices, across_x(): lax.all_to_all(values, 'fsdp', split_axis=0, concat_axis=0, tiled=True, a...  14.6 us
    all_to_all x1, blocking collectives, across_x(): lax.all_to_all(values, 'fsdp', split_axis=0, concat_axis=0, tiled=True, a...  14 us
    ppermute x4, waiting for transfers between devices, from_other_side(): return lax.ppermute(values, 'fsdp', [(i, i ^ 1) for i in range(parts)])  12.7 us
    all_to_all x1, waiting for transfers between devices, across_frames(): lax.all_to_all(values.reshape(frames, rows // frames, -1), 'seq', split_a...  8.6 us
    ppermute x4, starting transfers between devices, from_other_side(): return lax.ppermute(values, 'fsdp', [(i, i ^ 1) for i in range(parts)])  8.21 us
  transfers between devices with their start and end apart: 10, of which 6 were waited for; matrix products, arithmetic and copies ran while one was open for 0% of the time, Pallas kernels for 4%

profile of v8, /device:TPU:32, one launch (start us, length us, event | category | flops | bytes accessed | tf_op | source)
XLA Modules:
  0.0 180.1 jit_solution(7059349509649994194)
XLA Ops:
  1.4 1.7 broadcast_in_dim.4
  3.0 6.9 %all-to-all-start = ((bf16[8,392,384]{2,1,0:T(8,128)(2,1)}), bf16[8,392,384]{2,1,0:T(8,128)(2,1)S(1)}, u32[]{:S(2)}, u32[]{:S(2)}) async-start(bf16[8,392,384]{2,1,0:T(8,128)(2,1)} %broadcast_in_dim.4), calls=%async_computation | async-start | bytes 4816896 | tf_op jit(solution)/shard_map/all_to_all | solution.py:398
  10.1 1.4 copy-done
  12.9 1.7 lend.1
  14.6 3.6 %collective-permute-start.2 = (bf16[4,128,384]{2,1,0:T(8,128)(2,1)}, bf16[4,128,384]{2,1,0:T(8,128)(2,1)S(1)}, u32[]{:S(2)}, u32[]{:S(2)}) collective-permute-start(bf16[4,128,384]{2,1,0:T(8,128)(2,1)} %get-tuple-element.17), channel_id=1, source_target_pairs={{0,1},{1,0},{2,3},{3,2},{4,5},{5,4},{6,7},{7,6},{8,9},{9,8},{10,11... | collective-permute-start | bytes 1179656 | tf_op jit(solution)/shard_map/ppermute | solution.py:407
  18.1 27.4 %all-to-all-done.parts_ref = bf16[8,392,384]{2,1,0:T(8,128)(2,1)S(1)} async-done(((bf16[8,392,384]{2,1,0:T(8,128)(2,1)}), bf16[8,392,384]{2,1,0:T(8,128)(2,1)S(1)}, u32[]{:S(2)}, u32[]{:S(2)}) %all-to-all-start) | async-done | bytes 2408480 | tf_op jit(solution)/shard_map/all_to_all | solution.py:398
  45.6 3.8 %space_in.1 = (bf16[384,256]{1,0:T(8,128)(2,1)S(1)}, bf16[2,384,256]{2,1,0:T(8,128)(2,1)S(1)}) custom-call(bf16[8,392,384]{2,1,0:T(8,128)(2,1)S(1)} %all-to-all-done.parts_ref, f32[3,3072]{1,0:T(4,128)S(1)} %copy-done.6, bf16[3,3072,256]{2,1,0:T(8,128)(2,1)} %bitcast.18), custom_call_target="tpu_custom_call" | custom-call | flops 1811939328 | bytes 7127040 | tf_op jit(solution)/shard_map/space_in/pallas_call | solution.py:151
  51.2 1.8 %space_attend.1.own_ref = bf16[384,256]{1,0:T(8,128)(2,1)S(1)} custom-call(s32[3]{0:T(128)S(1)} %pad_add_fusion.where_ref, s32[576]{0:T(1024)S(1)} %reshape.23.mask_ref, bf16[384,256]{1,0:T(8,128)(2,1)S(1)} %get-tuple-element.15.q_ref, bf16[2,384,256]{2,1,0:T(8,128)(2,1)S(1)} %get-tuple-element.16.own_ref, ...), custom_call_target="tpu_custom_call" | custom-call | flops 301989888 | bytes 1179648 | tf_op jit(solution)/shard_map/space_attend/pallas_call | solution.py:221
  53.0 1.7 collective-permute-start.1
  54.7 6.9 %collective-permute-done.1.partner_ref = bf16[384,256]{1,0:T(8,128)(2,1)S(1)} collective-permute-done((bf16[384,256]{1,0:T(8,128)(2,1)S(1)}, bf16[384,256]{1,0:T(8,128)(2,1)S(1)}, u32[]{:S(2)}, u32[]{:S(2)}) %collective-permute-start.1) | collective-permute-done | bytes 196640 | tf_op jit(solution)/shard_map/ppermute | solution.py:407
  61.6 1.4 copy-done.1
  63.0 2.6 %project.2 = bf16[4,384,384]{2,1,0:T(8,128)(2,1)} custom-call(s32[3]{0:T(128)S(1)} %pad_add_fusion.where_ref, bf16[384,256]{1,0:T(8,128)(2,1)S(1)} %space_attend.1.own_ref, bf16[384,256]{1,0:T(8,128)(2,1)S(1)} %collective-permute-done.1.partner_ref, bf16[256,3072]{1,0:T(8,128)(2,1)S(1)} %copy-done.1, ...), custom_call_target="tpu_custom_call" | custom-call | flops 603979776 | bytes 2752512 | tf_op jit(solution)/shard_map/project/pallas_call | solution.py:291
  65.6 3.5 %all-to-all-start.1 = ((bf16[4,384,384]{2,1,0:T(8,128)(2,1)}), bf16[4,384,384]{2,1,0:T(8,128)(2,1)S(1)}, u32[]{:S(2)}, u32[]{:S(2)}) async-start(bf16[4,384,384]{2,1,0:T(8,128)(2,1)} %project.2), calls=%async_computation.1 | async-start | bytes 2359296 | tf_op jit(solution)/shard_map/all_to_all | solution.py:416
  69.2 1.7 collective-permute-start.4
  70.8 14.6 %all-to-all-done.1.parts_ref = bf16[4,384,384]{2,1,0:T(8,128)(2,1)S(1)} async-done(((bf16[4,384,384]{2,1,0:T(8,128)(2,1)}), bf16[4,384,384]{2,1,0:T(8,128)(2,1)S(1)}, u32[]{:S(2)}, u32[]{:S(2)}) %all-to-all-start.1) | async-done | bytes 1179680 | tf_op jit(solution)/shard_map/all_to_all | solution.py:416
  86.1 17.9 %all_to_all.30 = bf16[16,24,384]{2,1,0:T(8,128)(2,1)S(1)} all-to-all(bf16[16,24,384]{2,1,0:T(8,128)(2,1)S(1)} %bitcast.16), channel_id=1, replica_groups={{0,16,32,48,64,80,96,112,128,144,160,176,192,208,224,240},{8,24,40,56,7..., dimensions={0} | all-to-all | bytes 589824 | tf_op jit(solution)/shard_map/all_to_all | solution.py:392
  104.6 32.8 %all_to_all.31.parts_ref = bf16[8,392,384]{2,1,0:T(8,128)(2,1)S(1)} all-to-all(bf16[8,392,384]{2,1,0:T(8,128)(2,1)S(1)} %broadcast_in_dim.5), channel_id=1, replica_groups=mesh['seq'=32,'fsdp'=8] {'fsdp'}, dimensions={0} | all-to-all | bytes 4816896 | tf_op jit(solution)/shard_map/all_to_all | solution.py:398
  137.4 4.9 %time_layer.1 = bf16[384,256]{1,0:T(8,128)(2,1)} custom-call(bf16[8,392,384]{2,1,0:T(8,128)(2,1)S(1)} %all_to_all.31.parts_ref, f32[3,3072]{1,0:T(4,128)S(1)} %copy-done.7, bf16[3,3072,256]{2,1,0:T(8,128)(2,1)} %bitcast.17), custom_call_target="tpu_custom_call" | custom-call | flops 1811939328 | bytes 7127040 | tf_op jit(solution)/shard_map/time_layer/pallas_call | solution.py:362
  142.4 4.8 %all-to-all-start.4 = ((bf16[16,24,256]{2,1,0:T(8,128)(2,1)}), bf16[16,24,256]{2,1,0:T(8,128)(2,1)S(1)}, u32[]{:S(2)}, u32[]{:S(2)}) async-start(bf16[16,24,256]{2,1,0:T(8,128)(2,1)} %bitcast.8), calls=%async_computation.4 | async-start | bytes 393216 | tf_op jit(solution)/shard_map/all_to_all | solution.py:392
  147.2 8.6 %all-to-all-done.4 = bf16[16,24,256]{2,1,0:T(8,128)(2,1)S(1)} async-done(((bf16[16,24,256]{2,1,0:T(8,128)(2,1)}), bf16[16,24,256]{2,1,0:T(8,128)(2,1)S(1)}, u32[]{:S(2)}, u32[]{:S(2)}) %all-to-all-start.4) | async-done | bytes 196640 | tf_op jit(solution)/shard_map/all_to_all | solution.py:392
  157.1 5.9 %collective-permute-done.5.partner_ref = bf16[384,256]{1,0:T(8,128)(2,1)S(1)} collective-permute-done((bf16[384,256]{1,0:T(8,128)(2,1)S(1)}, bf16[384,256]{1,0:T(8,128)(2,1)S(1)}, u32[]{:S(2)}, u32[]{:S(2)}) %collective-permute-start.5) | collective-permute-done | bytes 196640 | tf_op jit(solution)/shard_map/ppermute | solution.py:407
  163.0 1.6 project.3
  164.6 14.0 %all_to_all.32.parts_ref = bf16[4,384,384]{2,1,0:T(8,128)(2,1)S(1)} all-to-all(bf16[4,384,384]{2,1,0:T(8,128)(2,1)S(1)} %project.3), channel_id=1, replica_groups={{0,2,4,6},{1,3,5,7},{8,10,12,14},{9,11,13,15},{16,18,20,22},{17,19,21,2..., dimensions={0} | all-to-all | bytes 2359296 | tf_op jit(solution)/shard_map/all_to_all | solution.py:416
  178.6 1.5 join.3
  (32 shorter events, 7.3 us)
Async XLA Ops:
  0.0 1.1 copy-start.4
  3.0 42.5 %all-to-all-start = ((bf16[8,392,384]{2,1,0:T(8,128)(2,1)}), bf16[8,392,384]{2,1,0:T(8,128)(2,1)S(1)}, u32[]{:S(2)}, u32[]{:S(2)}) async-start(bf16[8,392,384]{2,1,0:T(8,128)(2,1)} %broadcast_in_dim.4), calls=%async_computation | async-start | bytes 4816896 | tf_op jit(solution)/shard_map/all_to_all | solution.py:398
  10.0 35.6 %copy-start.6 = (f32[3,3072]{1,0:T(4,128)S(1)}, f32[3,3072]{1,0:T(4,128)}, u32[]{:S(2)}) copy-start(f32[3,3072]{1,0:T(4,128)} %mod_ref.5) | copy-start | bytes 110596
  10.1 1.4 copy-start
  11.5 1.4 copy-start.2
  14.6 35.0 %collective-permute-start.2 = (bf16[4,128,384]{2,1,0:T(8,128)(2,1)}, bf16[4,128,384]{2,1,0:T(8,128)(2,1)S(1)}, u32[]{:S(2)}, u32[]{:S(2)}) collective-permute-start(bf16[4,128,384]{2,1,0:T(8,128)(2,1)} %get-tuple-element.17), channel_id=1, source_target_pairs={{0,1},{1,0},{2,3},{3,2},{4,5},{5,4},{6,7},{7,6},{8,9},{9,8},{10,11... | collective-permute-start | bytes 1179656 | tf_op jit(solution)/shard_map/ppermute | solution.py:407
  45.6 4.4 %copy-start.8 = (s32[16,6,6]{0,2,1:T(8,128)S(1)}, s32[16,6,6]{0,2,1:T(8,128)}, u32[]{:S(2)}) copy-start(s32[16,6,6]{0,2,1:T(8,128)} %param.9) | copy-start | bytes 6916
  49.4 1.8 %collective-permute-start = (bf16[2,384,256]{2,1,0:T(8,128)(2,1)S(1)}, bf16[2,384,256]{2,1,0:T(8,128)(2,1)S(1)}, u32[]{:S(2)}, u32[]{:S(2)}) collective-permute-start(bf16[2,384,256]{2,1,0:T(8,128)(2,1)S(1)} %get-tuple-element.16.own_ref), channel_id=1, source_target_pairs={{0,8},{8,0},{16,24},{24,16},{32,40},{40,32},{48,56},{56,48},{64,72... | collective-permute-start | bytes 1179656 | tf_op jit(solution)/shard_map/ppermute | solution.py:404
  49.5 5.2 %collective-permute-start.3 = (bf16[4,128,384]{2,1,0:T(8,128)(2,1)S(1)}, bf16[4,128,384]{2,1,0:T(8,128)(2,1)S(1)}, u32[]{:S(2)}, u32[]{:S(2)}) collective-permute-start(bf16[4,128,384]{2,1,0:T(8,128)(2,1)S(1)} %collective-permute-done.2.half_ref), channel_id=1, source_target_pairs={{0,8},{8,0},{16,24},{24,16},{32,40},{40,32},{48,56},{56,48},{64,72... | collective-permute-start | bytes 1179656 | tf_op jit(solution)/shard_map/ppermute | solution.py:404
  51.2 34.1 %copy-start.5 = (f32[1,384,384]{2,1,0:T(8,128)S(1)}, f32[1,384,384]{2,1,0:T(8,128)}, u32[]{:S(2)}) copy-start(f32[1,384,384]{2,1,0:T(8,128)} %param.8) | copy-start | bytes 1769476
  53.0 8.5 %collective-permute-start.1 = (bf16[384,256]{1,0:T(8,128)(2,1)S(1)}, bf16[384,256]{1,0:T(8,128)(2,1)S(1)}, u32[]{:S(2)}, u32[]{:S(2)}) collective-permute-start(bf16[384,256]{1,0:T(8,128)(2,1)S(1)} %space_attend.1.own_ref), channel_id=1, source_target_pairs={{0,1},{1,0},{2,3},{3,2},{4,5},{5,4},{6,7},{7,6},{8,9},{9,8},{10,11... | collective-permute-start | bytes 589832 | tf_op jit(solution)/shard_map/ppermute | solution.py:407
  61.6 1.4 copy-start.1
  65.6 19.7 %all-to-all-start.1 = ((bf16[4,384,384]{2,1,0:T(8,128)(2,1)}), bf16[4,384,384]{2,1,0:T(8,128)(2,1)S(1)}, u32[]{:S(2)}, u32[]{:S(2)}) async-start(bf16[4,384,384]{2,1,0:T(8,128)(2,1)} %project.2), calls=%async_computation.1 | async-start | bytes 2359296 | tf_op jit(solution)/shard_map/all_to_all | solution.py:416
  69.2 17.0 %collective-permute-start.4 = (bf16[4,128,384]{2,1,0:T(8,128)(2,1)}, bf16[4,128,384]{2,1,0:T(8,128)(2,1)S(1)}, u32[]{:S(2)}, u32[]{:S(2)}) collective-permute-start(bf16[4,128,384]{2,1,0:T(8,128)(2,1)} %get-tuple-element.21), channel_id=1, source_target_pairs={{0,1},{1,0},{2,3},{3,2},{4,5},{5,4},{6,7},{7,6},{8,9},{9,8},{10,11... | collective-permute-start | bytes 1179656 | tf_op jit(solution)/shard_map/ppermute | solution.py:407
  104.6 32.9 %copy-start.7 = (f32[3,3072]{1,0:T(4,128)S(1)}, f32[3,3072]{1,0:T(4,128)}, u32[]{:S(2)}) copy-start(f32[3,3072]{1,0:T(4,128)} %mod_ref.7) | copy-start | bytes 110596
  137.4 25.5 %copy-start.3 = (bf16[256,3072]{1,0:T(8,128)(2,1)S(1)}, bf16[256,3072]{1,0:T(8,128)(2,1)}, u32[]{:S(2)}) copy-start(bf16[256,3072]{1,0:T(8,128)(2,1)} %weight_ref.3) | copy-start | bytes 4718596
  142.4 13.4 %all-to-all-start.4 = ((bf16[16,24,256]{2,1,0:T(8,128)(2,1)}), bf16[16,24,256]{2,1,0:T(8,128)(2,1)S(1)}, u32[]{:S(2)}, u32[]{:S(2)}) async-start(bf16[16,24,256]{2,1,0:T(8,128)(2,1)} %bitcast.8), calls=%async_computation.4 | async-start | bytes 393216 | tf_op jit(solution)/shard_map/all_to_all | solution.py:392
  147.2 9.9 %collective-permute-start.6 = (bf16[4,128,384]{2,1,0:T(8,128)(2,1)S(1)}, bf16[4,128,384]{2,1,0:T(8,128)(2,1)S(1)}, u32[]{:S(2)}, u32[]{:S(2)}) collective-permute-start(bf16[4,128,384]{2,1,0:T(8,128)(2,1)S(1)} %collective-permute-done.4.half_ref), channel_id=1, source_target_pairs={{0,8},{8,0},{16,24},{24,16},{32,40},{40,32},{48,56},{56,48},{64,72... | collective-permute-start | bytes 1179656 | tf_op jit(solution)/shard_map/ppermute | solution.py:404
  155.8 7.2 %collective-permute-start.5 = (bf16[384,256]{1,0:T(8,128)(2,1)S(1)}, bf16[384,256]{1,0:T(8,128)(2,1)S(1)}, u32[]{:S(2)}, u32[]{:S(2)}) collective-permute-start(bf16[384,256]{1,0:T(8,128)(2,1)S(1)} %bitcast.14), channel_id=1, source_target_pairs={{0,1},{1,0},{2,3},{3,2},{4,5},{5,4},{6,7},{7,6},{8,9},{9,8},{10,11... | collective-permute-start | bytes 589832 | tf_op jit(solution)/shard_map/ppermute | solution.py:407

commit v9 on v8

--- a/solution.py
+++ b/solution.py
@@ -12,7 +12,8 @@
 BLOCK = 128
 EPS = 1e-06
 SCALE = 1.0 / math.sqrt(HD)
-VMEM_LIMIT = 48 * 1024 * 1024
+VMEM_LIMIT = 24 * 1024 * 1024
+HELD_LIMIT = 52 * 1024 * 1024
 ROW_TILE = 192
 F32 = jnp.float32
 BF16 = jnp.bfloat16
@@ -27,8 +28,8 @@
     return [pl.BlockSpec(memory_space=pltpu.SMEM)] * count
 
 
-def params():
-    return pltpu.CompilerParams(vmem_limit_bytes=VMEM_LIMIT)
+def params(limit=None):
+    return pltpu.CompilerParams(vmem_limit_bytes=limit or VMEM_LIMIT)
 
 
 def spread_columns(columns, rows):
@@ -92,12 +93,14 @@
     return jnp.transpose(jnp.concatenate([offsets, scales], axis=0))
 
 
-def modulate(parts_ref, mod_ref, normed_ref):
+def modulate(parts_ref, mod_ref, normed_ref, copies):
     parts, total_rows, width = parts_ref.shape
     rows = normed_ref.shape[0]
     table = row_table(parts_ref.at[:, rows:total_rows, :], width)
     scale = jnp.broadcast_to(table[:, 127:128], (rows, 128))
     for part in range(parts):
+        if copies and part in (parts // 4, parts // 2):
+            copies[part // (parts // 4) - 1].start()
         offset = jnp.broadcast_to(table[:, part : part + 1], (rows, 128))
         for start in range(0, width, 128):
             columns = slice(part * width + start, part * width + start + 128)
@@ -108,33 +111,26 @@
             ).astype(BF16)
 
 
-def qkv_rows(parts_ref, mod_ref, weight_ref, normed_ref, held_ref, done):
-    copies = [
-        pltpu.make_async_copy(weight_ref.at[which], held_ref.at[which], done.at[which])
-        for which in range(3)
-    ]
-    for copy in copies:
-        copy.start()
-    modulate(parts_ref, mod_ref, normed_ref)
+def qkv_rows(parts_ref, mod_ref, weight_ref, normed_ref, held_ref=None, done=None):
+    copies = []
+    if held_ref is not None:
+        copies = [
+            pltpu.make_async_copy(weight_ref.at[which], held_ref.at[which], done.at[which])
+            for which in range(3)
+        ]
+        copies[0].start()
+        weight_ref = held_ref
+    modulate(parts_ref, mod_ref, normed_ref, copies[1:])
     rows = normed_ref.shape[0]
     tile = ROW_TILE if rows % ROW_TILE == 0 else rows
     for which in range(3):
-        copies[which].wait()
+        if copies:
+            copies[which].wait()
         for start in range(0, rows, tile):
             span = slice(start, start + tile)
             yield which, span, jnp.dot(
-                normed_ref[span, :], held_ref[which], preferred_element_type=F32
+                normed_ref[span, :], weight_ref[which], preferred_element_type=F32
             )
-
-
-def qkv_operands(rows, weight):
-    specs = vmem(2) + [pl.BlockSpec(memory_space=pl.ANY)]
-    scratch = [
-        pltpu.VMEM((rows, weight.shape[1]), BF16),
-        pltpu.VMEM(weight.shape, BF16),
-        pltpu.SemaphoreType.DMA((3,)),
-    ]
-    return specs, scratch
 
 
 def space_in_kernel(parts_ref, mod_ref, weight_ref, q_ref, kv_ref, *scratch):
@@ -147,17 +143,20 @@
 
 def space_in(parts, mod, weight, rows):
     heads_width = weight.shape[2]
-    specs, scratch = qkv_operands(rows, weight)
     return pl.pallas_call(
         space_in_kernel,
-        in_specs=specs,
+        in_specs=vmem(2) + [pl.BlockSpec(memory_space=pl.ANY)],
         out_specs=vmem(2),
         out_shape=[
             jax.ShapeDtypeStruct((rows, heads_width), BF16),
             jax.ShapeDtypeStruct((2, rows, heads_width), BF16),
         ],
-        scratch_shapes=scratch,
-        compiler_params=params(),
+        scratch_shapes=[
+            pltpu.VMEM((rows, weight.shape[1]), BF16),
+            pltpu.VMEM(weight.shape, BF16),
+            pltpu.SemaphoreType.DMA((3,)),
+        ],
+        compiler_params=params(HELD_LIMIT),
         cost_estimate=pl.CostEstimate(
             flops=2 * rows * weight.size,
             bytes_accessed=2 * (weight.size + parts.size),
@@ -234,20 +233,23 @@
 
 
 def lend_kernel(where_ref, *refs):
-    layers = (len(refs) - 1) // 2
+    layers = (len(refs) - 1) // 3
     done = refs[-1]
+    side = where_ref[2] % 2
     copies = []
-    for weight_ref, out_ref in zip(refs[:layers], refs[layers : 2 * layers]):
-        groups, count, width = out_ref.shape
+    for layer in range(layers):
+        weight_ref, lent_ref, kept_ref = refs[layer], refs[layers + layer], refs[2 * layers + layer]
+        groups, count, width = lent_ref.shape
         lines = pl.ds(pl.multiple_of(where_ref[1] * count, 128), count)
-        other_side = 1 - where_ref[2] % 2
         for group in range(groups):
-            first = pl.multiple_of((2 * group + other_side) * width, 128)
-            copies.append(
-                pltpu.make_async_copy(
-                    weight_ref.at[lines, pl.ds(first, width)], out_ref.at[group], done.at[len(copies)]
-                )
-            )
+            there = pl.ds(pl.multiple_of((2 * group + 1 - side) * width, 128), width)
+            here = pl.ds(pl.multiple_of((2 * group + side) * width, 128), width)
+            copies.append((weight_ref.at[lines, there], lent_ref.at[group]))
+            copies.append((weight_ref.at[:, here], kept_ref.at[group]))
+    copies = [
+        pltpu.make_async_copy(source, target, done.at[index])
+        for index, (source, target) in enumerate(copies)
+    ]
     for copy in copies:
         copy.start()
     for copy in copies:
@@ -255,32 +257,34 @@
 
 
 def lend(where, weights, width):
+    layers = len(weights)
     heads_width, model_width = weights[0].shape
     groups = model_width // (2 * width)
-    shape = jax.ShapeDtypeStruct((groups, heads_width // 2, width), BF16)
-    return pl.pallas_call(
+    lent = jax.ShapeDtypeStruct((groups, heads_width // 2, width), BF16)
+    kept = jax.ShapeDtypeStruct((groups, heads_width, width), BF16)
+    outs = pl.pallas_call(
         lend_kernel,
-        in_specs=smem(1) + [pl.BlockSpec(memory_space=pl.ANY)] * len(weights),
-        out_specs=vmem(len(weights)),
-        out_shape=[shape] * len(weights),
-        scratch_shapes=[pltpu.SemaphoreType.DMA((groups * len(weights),))],
+        in_specs=smem(1) + [pl.BlockSpec(memory_space=pl.ANY)] * layers,
+        out_specs=vmem(2 * layers),
+        out_shape=[lent] * layers + [kept] * layers,
+        scratch_shapes=[pltpu.SemaphoreType.DMA((2 * groups * layers,))],
         compiler_params=params(),
         cost_estimate=pl.CostEstimate(
-            flops=0, bytes_accessed=2 * len(weights) * weights[0].size, transcendentals=0
+            flops=0, bytes_accessed=3 * layers * weights[0].size, transcendentals=0
         ),
         name="lend",
     )(where, *weights)
+    return outs[:layers], outs[layers:]
 
 
 def project_kernel(where_ref, own_ref, partner_ref, weight_ref, half_ref, other_half_ref, out_ref, lent_ref):
-    groups, _, width = out_ref.shape
+    groups = out_ref.shape[0]
     count = half_ref.shape[1]
-    core, side = where_ref[1], where_ref[2] % 2
+    core = where_ref[1]
     lent_ref[:, pl.ds(pl.multiple_of(core * count, 128), count), :] = half_ref[...]
     lent_ref[:, pl.ds(pl.multiple_of((1 - core) * count, 128), count), :] = other_half_ref[...]
     for group in range(groups):
-        first = pl.multiple_of((2 * group + side) * width, 128)
-        product = jnp.dot(own_ref[...], weight_ref[:, pl.ds(first, width)], preferred_element_type=F32)
+        product = jnp.dot(own_ref[...], weight_ref[group], preferred_element_type=F32)
         product += jnp.dot(partner_ref[...], lent_ref[group], preferred_element_type=F32)
         out_ref[group] = product.astype(BF16)
 
@@ -358,17 +362,16 @@
 
 def time_layer(parts, mod, weight, rows, frames):
     heads_width = weight.shape[2]
-    specs, scratch = qkv_operands(rows, weight)
     return pl.pallas_call(
         time_kernel,
-        in_specs=specs,
+        in_specs=vmem(3),
         out_specs=vmem(1)[0],
         out_shape=jax.ShapeDtypeStruct((rows, heads_width), BF16),
         scratch_shapes=[
             pltpu.VMEM((3, frames, rows // frames, heads_width), F32),
             pltpu.VMEM((frames, rows // frames, heads_width), F32),
-        ]
-        + scratch,
+            pltpu.VMEM((rows, weight.shape[1]), BF16),
+        ],
         compiler_params=params(),
         cost_estimate=pl.CostEstimate(
             flops=2 * rows * weight.size,
@@ -418,18 +421,18 @@
         )
 
     local = tokens.reshape(rows, width)
-    space_lent, time_lent = lend(where, (space_out, time_out), width)
+    (space_lent, time_lent), (space_kept, time_kept) = lend(where, (space_out, time_out), width)
     half = from_other_side(space_lent)
     queries, own = space_in(gathered(pack(local)), space_mod, jnp.swapaxes(space_qkv, 0, 1), rows)
     attended = space_attend(where, block_mask.reshape(-1), queries, own, from_other_core(own))
-    partial = projected(attended, space_out, half)
+    partial = projected(attended, space_kept, half)
     partial, time_lent = lax.optimization_barrier((partial, time_lent))
     half = from_other_side(time_lent)
     stream, sent = join(where, across_x(partial), local, space_mod, (F32, BF16))
     sent, half = lax.optimization_barrier((sent, half))
     wide = gathered(pack(across_frames(sent)))
     attended = time_layer(wide, time_mod, jnp.swapaxes(time_qkv, 0, 1), rows, frames)
-    arrived = across_x(projected(across_frames(attended), time_out, half))
+    arrived = across_x(projected(across_frames(attended), time_kept, half))
     return join(where, arrived, stream, time_mod, (F32,))[0].reshape(tokens.shape)
 
 

time: 181 us -> 180 us (level)
    unnamed x19 -> x29, local copies, waits for them, and re-layouts: 5.43 us -> 3.78 us
  transfers between devices with their start and end apart: 10 -> 10, of which waited for: 6 -> 6; matrix products, arithmetic and copies ran while one was open for 0% -> 0% of each run, Pallas kernels for 4% -> 5%
where the time goes in v9:
time: 180 us
  blocking collectives  64.8 us (36%)
  waiting for transfers between devices  64.6 us (36%)
  starting transfers between devices  24.2 us (13%)
  Pallas kernels  20.1 us (11%)
  local copies, waits for them, and re-layouts  5.78 us (3%)
    all_to_all x1, blocking collectives, across_parts(): lax.all_to_all(values, 'fsdp', split_axis=0, concat_axis=0, tiled=True)  32.8 us
    all_to_all x1, waiting for transfers between devices, across_parts(): lax.all_to_all(values, 'fsdp', split_axis=0, concat_axis=0, tiled=True)  27.7 us
    all_to_all x1, blocking collectives, across_frames(): lax.all_to_all(values.reshape(frames, rows // frames, -1), 'seq', split_a...  17.9 us
    all_to_all x1, waiting for transfers between devices, across_x(): lax.all_to_all(values, 'fsdp', split_axis=0, concat_axis=0, tiled=True, a...  14.6 us
    all_to_all x1, blocking collectives, across_x(): lax.all_to_all(values, 'fsdp', split_axis=0, concat_axis=0, tiled=True, a...  14 us
    ppermute x4, waiting for transfers between devices, from_other_side(): return lax.ppermute(values, 'fsdp', [(i, i ^ 1) for i in range(parts)])  12.7 us
    all_to_all x1, waiting for transfers between devices, across_frames(): lax.all_to_all(values.reshape(frames, rows // frames, -1), 'seq', split_a...  8.6 us
    ppermute x4, starting transfers between devices, from_other_side(): return lax.ppermute(values, 'fsdp', [(i, i ^ 1) for i in range(parts)])  8.12 us
  transfers between devices with their start and end apart: 10, of which 6 were waited for; matrix products, arithmetic and copies ran while one was open for 0% of the time, Pallas kernels for 5%

profile of v9, /device:TPU:32, one launch (start us, length us, event | category | flops | bytes accessed | tf_op | source)
XLA Modules:
  0.0 179.7 jit_solution(4352623897506599197)
XLA Ops:
  0.0 1.1 copy-done
  1.4 1.7 broadcast_in_dim.4
  3.0 7.2 %all-to-all-start = ((bf16[8,392,384]{2,1,0:T(8,128)(2,1)}), bf16[8,392,384]{2,1,0:T(8,128)(2,1)}, u32[]{:S(2)}, u32[]{:S(2)}) async-start(bf16[8,392,384]{2,1,0:T(8,128)(2,1)} %broadcast_in_dim.4), calls=%async_computation | async-start | bytes 4816896 | tf_op jit(solution)/shard_map/all_to_all | solution.py:401
  10.3 1.8 %lend.1 = (bf16[4,128,384]{2,1,0:T(8,128)(2,1)}, bf16[4,128,384]{2,1,0:T(8,128)(2,1)S(1)}, bf16[4,256,384]{2,1,0:T(8,128)(2,1)S(1)}, bf16[4,256,384]{2,1,0:T(8,128)(2,1)S(1)}) custom-call(s32[3]{0:T(128)S(1)} %pad_add_fusion.where_ref, bf16[256,3072]{1,0:T(8,128)(2,1)S(1)} %copy-done.2, bf16[256,3072]{1,0:T(8,128)(2,1)S(1)} %copy-done.3), custom_call_target="tpu_custom_call" | custom-call | bytes 4718592 | tf_op jit(solution)/shard_map/lend/pallas_call | solution.py:265
  14.7 3.5 %collective-permute-start.2 = (bf16[4,128,384]{2,1,0:T(8,128)(2,1)}, bf16[4,128,384]{2,1,0:T(8,128)(2,1)S(1)}, u32[]{:S(2)}, u32[]{:S(2)}) collective-permute-start(bf16[4,128,384]{2,1,0:T(8,128)(2,1)} %get-tuple-element.20), channel_id=1, source_target_pairs={{0,1},{1,0},{2,3},{3,2},{4,5},{5,4},{6,7},{7,6},{8,9},{9,8},{10,11... | collective-permute-start | bytes 1179656 | tf_op jit(solution)/shard_map/ppermute | solution.py:410
  18.2 27.7 %all-to-all-done.parts_ref = bf16[8,392,384]{2,1,0:T(8,128)(2,1)} async-done(((bf16[8,392,384]{2,1,0:T(8,128)(2,1)}), bf16[8,392,384]{2,1,0:T(8,128)(2,1)}, u32[]{:S(2)}, u32[]{:S(2)}) %all-to-all-start) | async-done | bytes 2408480 | tf_op jit(solution)/shard_map/all_to_all | solution.py:401
  46.0 5.5 %space_in.1 = (bf16[384,256]{1,0:T(8,128)(2,1)S(1)}, bf16[2,384,256]{2,1,0:T(8,128)(2,1)S(1)}) custom-call(bf16[8,392,384]{2,1,0:T(8,128)(2,1)} %all-to-all-done.parts_ref, f32[3,3072]{1,0:T(4,128)S(1)} %copy-done.8, bf16[3,3072,256]{2,1,0:T(8,128)(2,1)} %bitcast.20), custom_call_target="tpu_custom_call" | custom-call | flops 1811939328 | bytes 7127040 | tf_op jit(solution)/shard_map/space_in/pallas_call | solution.py:146
  53.3 1.7 space_attend.1.own_ref
  55.1 1.7 collective-permute-start.1
  56.7 6.9 %collective-permute-done.1.partner_ref = bf16[384,256]{1,0:T(8,128)(2,1)S(1)} collective-permute-done((bf16[384,256]{1,0:T(8,128)(2,1)S(1)}, bf16[384,256]{1,0:T(8,128)(2,1)S(1)}, u32[]{:S(2)}, u32[]{:S(2)}) %collective-permute-start.1) | collective-permute-done | bytes 196640 | tf_op jit(solution)/shard_map/ppermute | solution.py:410
  63.6 2.6 %project.2 = bf16[4,384,384]{2,1,0:T(8,128)(2,1)} custom-call(s32[3]{0:T(128)S(1)} %pad_add_fusion.where_ref, bf16[384,256]{1,0:T(8,128)(2,1)S(1)} %space_attend.1.own_ref, bf16[384,256]{1,0:T(8,128)(2,1)S(1)} %collective-permute-done.1.partner_ref, bf16[4,256,384]{2,1,0:T(8,128)(2,1)S(1)} %copy-done.7, ...), custom_call_target="tpu_custom_call" | custom-call | flops 603979776 | bytes 2752512 | tf_op jit(solution)/shard_map/project/pallas_call | solution.py:295
  66.2 3.5 %all-to-all-start.1 = ((bf16[4,384,384]{2,1,0:T(8,128)(2,1)}), bf16[4,384,384]{2,1,0:T(8,128)(2,1)S(1)}, u32[]{:S(2)}, u32[]{:S(2)}) async-start(bf16[4,384,384]{2,1,0:T(8,128)(2,1)} %project.2), calls=%async_computation.1 | async-start | bytes 2359296 | tf_op jit(solution)/shard_map/all_to_all | solution.py:419
  69.8 1.7 collective-permute-start.4
  71.4 14.6 %all-to-all-done.1.parts_ref = bf16[4,384,384]{2,1,0:T(8,128)(2,1)S(1)} async-done(((bf16[4,384,384]{2,1,0:T(8,128)(2,1)}), bf16[4,384,384]{2,1,0:T(8,128)(2,1)S(1)}, u32[]{:S(2)}, u32[]{:S(2)}) %all-to-all-start.1) | async-done | bytes 1179680 | tf_op jit(solution)/shard_map/all_to_all | solution.py:419
  86.7 17.9 %all_to_all.30 = bf16[16,24,384]{2,1,0:T(8,128)(2,1)S(1)} all-to-all(bf16[16,24,384]{2,1,0:T(8,128)(2,1)S(1)} %bitcast.19), channel_id=1, replica_groups={{0,16,32,48,64,80,96,112,128,144,160,176,192,208,224,240},{8,24,40,56,7..., dimensions={0} | all-to-all | bytes 589824 | tf_op jit(solution)/shard_map/all_to_all | solution.py:395
  105.2 32.8 %all_to_all.31.parts_ref = bf16[8,392,384]{2,1,0:T(8,128)(2,1)S(1)} all-to-all(bf16[8,392,384]{2,1,0:T(8,128)(2,1)S(1)} %broadcast_in_dim.5), channel_id=1, replica_groups=mesh['seq'=32,'fsdp'=8] {'fsdp'}, dimensions={0} | all-to-all | bytes 4816896 | tf_op jit(solution)/shard_map/all_to_all | solution.py:401
  138.1 3.8 %time_layer.1 = bf16[384,256]{1,0:T(8,128)(2,1)} custom-call(bf16[8,392,384]{2,1,0:T(8,128)(2,1)S(1)} %all_to_all.31.parts_ref, f32[3,3072]{1,0:T(4,128)S(1)} %copy-done.9, bf16[3,3072,256]{2,1,0:T(8,128)(2,1)S(1)} %bitcast.13), custom_call_target="tpu_custom_call" | custom-call | flops 1811939328 | bytes 7127040 | tf_op jit(solution)/shard_map/time_layer/pallas_call | solution.py:365
  141.9 4.8 %all-to-all-start.4 = ((bf16[16,24,256]{2,1,0:T(8,128)(2,1)}), bf16[16,24,256]{2,1,0:T(8,128)(2,1)S(1)}, u32[]{:S(2)}, u32[]{:S(2)}) async-start(bf16[16,24,256]{2,1,0:T(8,128)(2,1)} %bitcast.8), calls=%async_computation.4 | async-start | bytes 393216 | tf_op jit(solution)/shard_map/all_to_all | solution.py:395
  146.7 8.6 %all-to-all-done.4 = bf16[16,24,256]{2,1,0:T(8,128)(2,1)S(1)} async-done(((bf16[16,24,256]{2,1,0:T(8,128)(2,1)}), bf16[16,24,256]{2,1,0:T(8,128)(2,1)S(1)}, u32[]{:S(2)}, u32[]{:S(2)}) %all-to-all-start.4) | async-done | bytes 196640 | tf_op jit(solution)/shard_map/all_to_all | solution.py:395
  155.3 1.3 collective-permute-start.5
  156.6 5.9 %collective-permute-done.5.partner_ref = bf16[384,256]{1,0:T(8,128)(2,1)S(1)} collective-permute-done((bf16[384,256]{1,0:T(8,128)(2,1)S(1)}, bf16[384,256]{1,0:T(8,128)(2,1)S(1)}, u32[]{:S(2)}, u32[]{:S(2)}) %collective-permute-start.5) | collective-permute-done | bytes 196640 | tf_op jit(solution)/shard_map/ppermute | solution.py:410
  162.5 1.6 project.3
  164.1 14.0 %all_to_all.32.parts_ref = bf16[4,384,384]{2,1,0:T(8,128)(2,1)S(1)} all-to-all(bf16[4,384,384]{2,1,0:T(8,128)(2,1)S(1)} %project.3), channel_id=1, replica_groups={{0,2,4,6},{1,3,5,7},{8,10,12,14},{9,11,13,15},{16,18,20,22},{17,19,21,2..., dimensions={0} | all-to-all | bytes 2359296 | tf_op jit(solution)/shard_map/all_to_all | solution.py:419
  178.1 1.5 join.3
  (43 shorter events, 6.1 us)
Async XLA Ops:
  0.0 1.1 copy-start
  3.0 7.3 %copy-start.2 = (bf16[256,3072]{1,0:T(8,128)(2,1)S(1)}, bf16[256,3072]{1,0:T(8,128)(2,1)}, u32[]{:S(2)}) copy-start(bf16[256,3072]{1,0:T(8,128)(2,1)} %refs_0_.1) | copy-start | bytes 4718596
  3.0 7.3 %copy-start.3 = (bf16[256,3072]{1,0:T(8,128)(2,1)S(1)}, bf16[256,3072]{1,0:T(8,128)(2,1)}, u32[]{:S(2)}) copy-start(bf16[256,3072]{1,0:T(8,128)(2,1)} %refs_1_.1) | copy-start | bytes 4718596
  3.0 42.9 %all-to-all-start = ((bf16[8,392,384]{2,1,0:T(8,128)(2,1)}), bf16[8,392,384]{2,1,0:T(8,128)(2,1)}, u32[]{:S(2)}, u32[]{:S(2)}) async-start(bf16[8,392,384]{2,1,0:T(8,128)(2,1)} %broadcast_in_dim.4), calls=%async_computation | async-start | bytes 4816896 | tf_op jit(solution)/shard_map/all_to_all | solution.py:401
  10.2 35.7 %copy-start.8 = (f32[3,3072]{1,0:T(4,128)S(1)}, f32[3,3072]{1,0:T(4,128)}, u32[]{:S(2)}) copy-start(f32[3,3072]{1,0:T(4,128)} %mod_ref.5) | copy-start | bytes 110596
  12.2 0.9 copy-start.4
  13.1 0.9 copy-start.6
  14.0 0.8 copy-start.10
  14.7 36.9 %collective-permute-start.2 = (bf16[4,128,384]{2,1,0:T(8,128)(2,1)}, bf16[4,128,384]{2,1,0:T(8,128)(2,1)S(1)}, u32[]{:S(2)}, u32[]{:S(2)}) collective-permute-start(bf16[4,128,384]{2,1,0:T(8,128)(2,1)} %get-tuple-element.20), channel_id=1, source_target_pairs={{0,1},{1,0},{2,3},{3,2},{4,5},{5,4},{6,7},{7,6},{8,9},{9,8},{10,11... | collective-permute-start | bytes 1179656 | tf_op jit(solution)/shard_map/ppermute | solution.py:410
  45.9 6.2 %copy-start.11 = (s32[16,6,6]{0,2,1:T(8,128)S(1)}, s32[16,6,6]{0,2,1:T(8,128)}, u32[]{:S(2)}) copy-start(s32[16,6,6]{0,2,1:T(8,128)} %param.9) | copy-start | bytes 6916
  46.0 17.6 %copy-start.7 = (bf16[4,256,384]{2,1,0:T(8,128)(2,1)S(1)}, bf16[4,256,384]{2,1,0:T(8,128)(2,1)}, u32[]{:S(2)}) copy-start(bf16[4,256,384]{2,1,0:T(8,128)(2,1)} %copy-done.6) | copy-start | bytes 2359300
  51.5 1.8 %collective-permute-start = (bf16[2,384,256]{2,1,0:T(8,128)(2,1)S(1)}, bf16[2,384,256]{2,1,0:T(8,128)(2,1)S(1)}, u32[]{:S(2)}, u32[]{:S(2)}) collective-permute-start(bf16[2,384,256]{2,1,0:T(8,128)(2,1)S(1)} %get-tuple-element.18.own_ref), channel_id=1, source_target_pairs={{0,8},{8,0},{16,24},{24,16},{32,40},{40,32},{48,56},{56,48},{64,72... | collective-permute-start | bytes 1179656 | tf_op jit(solution)/shard_map/ppermute | solution.py:407
  51.6 5.1 %collective-permute-start.3 = (bf16[4,128,384]{2,1,0:T(8,128)(2,1)S(1)}, bf16[4,128,384]{2,1,0:T(8,128)(2,1)S(1)}, u32[]{:S(2)}, u32[]{:S(2)}) collective-permute-start(bf16[4,128,384]{2,1,0:T(8,128)(2,1)S(1)} %collective-permute-done.2.half_ref), channel_id=1, source_target_pairs={{0,8},{8,0},{16,24},{24,16},{32,40},{40,32},{48,56},{56,48},{64,72... | collective-permute-start | bytes 1179656 | tf_op jit(solution)/shard_map/ppermute | solution.py:407
  55.1 8.5 %collective-permute-start.1 = (bf16[384,256]{1,0:T(8,128)(2,1)S(1)}, bf16[384,256]{1,0:T(8,128)(2,1)S(1)}, u32[]{:S(2)}, u32[]{:S(2)}) collective-permute-start(bf16[384,256]{1,0:T(8,128)(2,1)S(1)} %space_attend.1.own_ref), channel_id=1, source_target_pairs={{0,1},{1,0},{2,3},{3,2},{4,5},{5,4},{6,7},{7,6},{8,9},{9,8},{10,11... | collective-permute-start | bytes 589832 | tf_op jit(solution)/shard_map/ppermute | solution.py:410
  63.6 22.4 %copy-start.1 = (f32[1,384,384]{2,1,0:T(8,128)S(1)}, f32[1,384,384]{2,1,0:T(8,128)}, u32[]{:S(2)}) copy-start(f32[1,384,384]{2,1,0:T(8,128)} %param.8) | copy-start | bytes 1769476
  63.6 74.5 %slice-start = ((s8[4718592]{0:T(1024)(128)(4,1)}), s8[524288]{0:T(1024)(128)(4,1)S(1)}, s32[]{:S(2)}) async-start(s8[4718592]{0:T(1024)(128)(4,1)} %bitcast.11), calls=%async_computation.6 | async-start | bytes 1048576
  66.2 19.7 %all-to-all-start.1 = ((bf16[4,384,384]{2,1,0:T(8,128)(2,1)}), bf16[4,384,384]{2,1,0:T(8,128)(2,1)S(1)}, u32[]{:S(2)}, u32[]{:S(2)}) async-start(bf16[4,384,384]{2,1,0:T(8,128)(2,1)} %project.2), calls=%async_computation.1 | async-start | bytes 2359296 | tf_op jit(solution)/shard_map/all_to_all | solution.py:419
  69.8 17.0 %collective-permute-start.4 = (bf16[4,128,384]{2,1,0:T(8,128)(2,1)}, bf16[4,128,384]{2,1,0:T(8,128)(2,1)S(1)}, u32[]{:S(2)}, u32[]{:S(2)}) collective-permute-start(bf16[4,128,384]{2,1,0:T(8,128)(2,1)} %copy-done.10), channel_id=1, source_target_pairs={{0,1},{1,0},{2,3},{3,2},{4,5},{5,4},{6,7},{7,6},{8,9},{9,8},{10,11... | collective-permute-start | bytes 1179656 | tf_op jit(solution)/shard_map/ppermute | solution.py:410
  104.7 33.4 %slice-start.1 = ((s8[4718592]{0:T(1024)(128)(4,1)}), s8[4194304]{0:T(1024)(128)(4,1)S(1)}, s32[]{:S(2)}) async-start(s8[4718592]{0:T(1024)(128)(4,1)} %bitcast.11), calls=%async_computation.7 | async-start | bytes 8388608
  105.2 32.9 %copy-start.9 = (f32[3,3072]{1,0:T(4,128)S(1)}, f32[3,3072]{1,0:T(4,128)}, u32[]{:S(2)}) copy-start(f32[3,3072]{1,0:T(4,128)} %mod_ref.7) | copy-start | bytes 110596
  138.1 24.4 %copy-start.5 = (bf16[4,256,384]{2,1,0:T(8,128)(2,1)S(1)}, bf16[4,256,384]{2,1,0:T(8,128)(2,1)}, u32[]{:S(2)}) copy-start(bf16[4,256,384]{2,1,0:T(8,128)(2,1)} %copy-done.4) | copy-start | bytes 2359300
  141.9 13.4 %all-to-all-start.4 = ((bf16[16,24,256]{2,1,0:T(8,128)(2,1)}), bf16[16,24,256]{2,1,0:T(8,128)(2,1)S(1)}, u32[]{:S(2)}, u32[]{:S(2)}) async-start(bf16[16,24,256]{2,1,0:T(8,128)(2,1)} %bitcast.8), calls=%async_computation.4 | async-start | bytes 393216 | tf_op jit(solution)/shard_map/all_to_all | solution.py:395
  146.7 9.9 %collective-permute-start.6 = (bf16[4,128,384]{2,1,0:T(8,128)(2,1)S(1)}, bf16[4,128,384]{2,1,0:T(8,128)(2,1)S(1)}, u32[]{:S(2)}, u32[]{:S(2)}) collective-permute-start(bf16[4,128,384]{2,1,0:T(8,128)(2,1)S(1)} %collective-permute-done.4.half_ref), channel_id=1, source_target_pairs={{0,8},{8,0},{16,24},{24,16},{32,40},{40,32},{48,56},{56,48},{64,72... | collective-permute-start | bytes 1179656 | tf_op jit(solution)/shard_map/ppermute | solution.py:407
  155.3 7.2 %collective-permute-start.5 = (bf16[384,256]{1,0:T(8,128)(2,1)S(1)}, bf16[384,256]{1,0:T(8,128)(2,1)S(1)}, u32[]{:S(2)}, u32[]{:S(2)}) collective-permute-start(bf16[384,256]{1,0:T(8,128)(2,1)S(1)} %bitcast.17), channel_id=1, source_target_pairs={{0,1},{1,0},{2,3},{3,2},{4,5},{5,4},{6,7},{7,6},{8,9},{9,8},{10,11... | collective-permute-start | bytes 589832 | tf_op jit(solution)/shard_map/ppermute | solution.py:410

commit v10 on v9

--- a/solution.py
+++ b/solution.py
@@ -93,14 +93,12 @@
     return jnp.transpose(jnp.concatenate([offsets, scales], axis=0))
 
 
-def modulate(parts_ref, mod_ref, normed_ref, copies):
+def modulate(parts_ref, mod_ref, normed_ref):
     parts, total_rows, width = parts_ref.shape
     rows = normed_ref.shape[0]
     table = row_table(parts_ref.at[:, rows:total_rows, :], width)
     scale = jnp.broadcast_to(table[:, 127:128], (rows, 128))
     for part in range(parts):
-        if copies and part in (parts // 4, parts // 2):
-            copies[part // (parts // 4) - 1].start()
         offset = jnp.broadcast_to(table[:, part : part + 1], (rows, 128))
         for start in range(0, width, 128):
             columns = slice(part * width + start, part * width + start + 128)
@@ -118,9 +116,10 @@
             pltpu.make_async_copy(weight_ref.at[which], held_ref.at[which], done.at[which])
             for which in range(3)
         ]
-        copies[0].start()
+        for copy in copies:
+            copy.start()
         weight_ref = held_ref
-    modulate(parts_ref, mod_ref, normed_ref, copies[1:])
+    modulate(parts_ref, mod_ref, normed_ref)
     rows = normed_ref.shape[0]
     tile = ROW_TILE if rows % ROW_TILE == 0 else rows
     for which in range(3):

time: 180 us -> 180 us (level)
  no operation moved by 1% of the time
where the time goes in v10:
time: 180 us
  blocking collectives  64.8 us (36%)
  waiting for transfers between devices  64.6 us (36%)
  starting transfers between devices  24.2 us (13%)
  Pallas kernels  20.1 us (11%)
  local copies, waits for them, and re-layouts  5.78 us (3%)
    all_to_all x1, blocking collectives, across_parts(): lax.all_to_all(values, 'fsdp', split_axis=0, concat_axis=0, tiled=True)  32.8 us
    all_to_all x1, waiting for transfers between devices, across_parts(): lax.all_to_all(values, 'fsdp', split_axis=0, concat_axis=0, tiled=True)  27.7 us
    all_to_all x1, blocking collectives, across_frames(): lax.all_to_all(values.reshape(frames, rows // frames, -1), 'seq', split_a...  17.9 us
    all_to_all x1, waiting for transfers between devices, across_x(): lax.all_to_all(values, 'fsdp', split_axis=0, concat_axis=0, tiled=True, a...  14.6 us
    all_to_all x1, blocking collectives, across_x(): lax.all_to_all(values, 'fsdp', split_axis=0, concat_axis=0, tiled=True, a...  14 us
    ppermute x4, waiting for transfers between devices, from_other_side(): return lax.ppermute(values, 'fsdp', [(i, i ^ 1) for i in range(parts)])  12.7 us
    all_to_all x1, waiting for transfers between devices, across_frames(): lax.all_to_all(values.reshape(frames, rows // frames, -1), 'seq', split_a...  8.6 us
    ppermute x4, starting transfers between devices, from_other_side(): return lax.ppermute(values, 'fsdp', [(i, i ^ 1) for i in range(parts)])  8.12 us
  transfers between devices with their start and end apart: 10, of which 6 were waited for; matrix products, arithmetic and copies ran while one was open for 0% of the time, Pallas kernels for 5%

profile of v10, /device:TPU:32, one launch (start us, length us, event | category | flops | bytes accessed | tf_op | source)
XLA Modules:
  0.0 179.7 jit_solution(4352623897506599197)
XLA Ops:
  0.0 1.1 copy-done
  1.4 1.7 broadcast_in_dim.4
  3.0 7.2 %all-to-all-start = ((bf16[8,392,384]{2,1,0:T(8,128)(2,1)}), bf16[8,392,384]{2,1,0:T(8,128)(2,1)}, u32[]{:S(2)}, u32[]{:S(2)}) async-start(bf16[8,392,384]{2,1,0:T(8,128)(2,1)} %broadcast_in_dim.4), calls=%async_computation | async-start | bytes 4816896 | tf_op jit(solution)/shard_map/all_to_all | solution.py:400
  10.3 1.8 %lend.1 = (bf16[4,128,384]{2,1,0:T(8,128)(2,1)}, bf16[4,128,384]{2,1,0:T(8,128)(2,1)S(1)}, bf16[4,256,384]{2,1,0:T(8,128)(2,1)S(1)}, bf16[4,256,384]{2,1,0:T(8,128)(2,1)S(1)}) custom-call(s32[3]{0:T(128)S(1)} %pad_add_fusion.where_ref, bf16[256,3072]{1,0:T(8,128)(2,1)S(1)} %copy-done.2, bf16[256,3072]{1,0:T(8,128)(2,1)S(1)} %copy-done.3), custom_call_target="tpu_custom_call" | custom-call | bytes 4718592 | tf_op jit(solution)/shard_map/lend/pallas_call | solution.py:264
  14.7 3.5 %collective-permute-start.2 = (bf16[4,128,384]{2,1,0:T(8,128)(2,1)}, bf16[4,128,384]{2,1,0:T(8,128)(2,1)S(1)}, u32[]{:S(2)}, u32[]{:S(2)}) collective-permute-start(bf16[4,128,384]{2,1,0:T(8,128)(2,1)} %get-tuple-element.20), channel_id=1, source_target_pairs={{0,1},{1,0},{2,3},{3,2},{4,5},{5,4},{6,7},{7,6},{8,9},{9,8},{10,11... | collective-permute-start | bytes 1179656 | tf_op jit(solution)/shard_map/ppermute | solution.py:409
  18.2 27.7 %all-to-all-done.parts_ref = bf16[8,392,384]{2,1,0:T(8,128)(2,1)} async-done(((bf16[8,392,384]{2,1,0:T(8,128)(2,1)}), bf16[8,392,384]{2,1,0:T(8,128)(2,1)}, u32[]{:S(2)}, u32[]{:S(2)}) %all-to-all-start) | async-done | bytes 2408480 | tf_op jit(solution)/shard_map/all_to_all | solution.py:400
  46.0 5.5 %space_in.1 = (bf16[384,256]{1,0:T(8,128)(2,1)S(1)}, bf16[2,384,256]{2,1,0:T(8,128)(2,1)S(1)}) custom-call(bf16[8,392,384]{2,1,0:T(8,128)(2,1)} %all-to-all-done.parts_ref, f32[3,3072]{1,0:T(4,128)S(1)} %copy-done.8, bf16[3,3072,256]{2,1,0:T(8,128)(2,1)} %bitcast.20), custom_call_target="tpu_custom_call" | custom-call | flops 1811939328 | bytes 7127040 | tf_op jit(solution)/shard_map/space_in/pallas_call | solution.py:145
  53.3 1.7 space_attend.1.own_ref
  55.1 1.7 collective-permute-start.1
  56.7 6.9 %collective-permute-done.1.partner_ref = bf16[384,256]{1,0:T(8,128)(2,1)S(1)} collective-permute-done((bf16[384,256]{1,0:T(8,128)(2,1)S(1)}, bf16[384,256]{1,0:T(8,128)(2,1)S(1)}, u32[]{:S(2)}, u32[]{:S(2)}) %collective-permute-start.1) | collective-permute-done | bytes 196640 | tf_op jit(solution)/shard_map/ppermute | solution.py:409
  63.6 2.6 %project.2 = bf16[4,384,384]{2,1,0:T(8,128)(2,1)} custom-call(s32[3]{0:T(128)S(1)} %pad_add_fusion.where_ref, bf16[384,256]{1,0:T(8,128)(2,1)S(1)} %space_attend.1.own_ref, bf16[384,256]{1,0:T(8,128)(2,1)S(1)} %collective-permute-done.1.partner_ref, bf16[4,256,384]{2,1,0:T(8,128)(2,1)S(1)} %copy-done.7, ...), custom_call_target="tpu_custom_call" | custom-call | flops 603979776 | bytes 2752512 | tf_op jit(solution)/shard_map/project/pallas_call | solution.py:294
  66.2 3.5 %all-to-all-start.1 = ((bf16[4,384,384]{2,1,0:T(8,128)(2,1)}), bf16[4,384,384]{2,1,0:T(8,128)(2,1)S(1)}, u32[]{:S(2)}, u32[]{:S(2)}) async-start(bf16[4,384,384]{2,1,0:T(8,128)(2,1)} %project.2), calls=%async_computation.1 | async-start | bytes 2359296 | tf_op jit(solution)/shard_map/all_to_all | solution.py:418
  69.8 1.7 collective-permute-start.4
  71.4 14.6 %all-to-all-done.1.parts_ref = bf16[4,384,384]{2,1,0:T(8,128)(2,1)S(1)} async-done(((bf16[4,384,384]{2,1,0:T(8,128)(2,1)}), bf16[4,384,384]{2,1,0:T(8,128)(2,1)S(1)}, u32[]{:S(2)}, u32[]{:S(2)}) %all-to-all-start.1) | async-done | bytes 1179680 | tf_op jit(solution)/shard_map/all_to_all | solution.py:418
  86.7 17.9 %all_to_all.30 = bf16[16,24,384]{2,1,0:T(8,128)(2,1)S(1)} all-to-all(bf16[16,24,384]{2,1,0:T(8,128)(2,1)S(1)} %bitcast.19), channel_id=1, replica_groups={{0,16,32,48,64,80,96,112,128,144,160,176,192,208,224,240},{8,24,40,56,7..., dimensions={0} | all-to-all | bytes 589824 | tf_op jit(solution)/shard_map/all_to_all | solution.py:394
  105.2 32.8 %all_to_all.31.parts_ref = bf16[8,392,384]{2,1,0:T(8,128)(2,1)S(1)} all-to-all(bf16[8,392,384]{2,1,0:T(8,128)(2,1)S(1)} %broadcast_in_dim.5), channel_id=1, replica_groups=mesh['seq'=32,'fsdp'=8] {'fsdp'}, dimensions={0} | all-to-all | bytes 4816896 | tf_op jit(solution)/shard_map/all_to_all | solution.py:400
  138.1 3.8 %time_layer.1 = bf16[384,256]{1,0:T(8,128)(2,1)} custom-call(bf16[8,392,384]{2,1,0:T(8,128)(2,1)S(1)} %all_to_all.31.parts_ref, f32[3,3072]{1,0:T(4,128)S(1)} %copy-done.9, bf16[3,3072,256]{2,1,0:T(8,128)(2,1)S(1)} %bitcast.13), custom_call_target="tpu_custom_call" | custom-call | flops 1811939328 | bytes 7127040 | tf_op jit(solution)/shard_map/time_layer/pallas_call | solution.py:364
  141.9 4.8 %all-to-all-start.4 = ((bf16[16,24,256]{2,1,0:T(8,128)(2,1)}), bf16[16,24,256]{2,1,0:T(8,128)(2,1)S(1)}, u32[]{:S(2)}, u32[]{:S(2)}) async-start(bf16[16,24,256]{2,1,0:T(8,128)(2,1)} %bitcast.8), calls=%async_computation.4 | async-start | bytes 393216 | tf_op jit(solution)/shard_map/all_to_all | solution.py:394
  146.7 8.6 %all-to-all-done.4 = bf16[16,24,256]{2,1,0:T(8,128)(2,1)S(1)} async-done(((bf16[16,24,256]{2,1,0:T(8,128)(2,1)}), bf16[16,24,256]{2,1,0:T(8,128)(2,1)S(1)}, u32[]{:S(2)}, u32[]{:S(2)}) %all-to-all-start.4) | async-done | bytes 196640 | tf_op jit(solution)/shard_map/all_to_all | solution.py:394
  155.3 1.3 collective-permute-start.5
  156.6 5.9 %collective-permute-done.5.partner_ref = bf16[384,256]{1,0:T(8,128)(2,1)S(1)} collective-permute-done((bf16[384,256]{1,0:T(8,128)(2,1)S(1)}, bf16[384,256]{1,0:T(8,128)(2,1)S(1)}, u32[]{:S(2)}, u32[]{:S(2)}) %collective-permute-start.5) | collective-permute-done | bytes 196640 | tf_op jit(solution)/shard_map/ppermute | solution.py:409
  162.5 1.6 project.3
  164.1 14.0 %all_to_all.32.parts_ref = bf16[4,384,384]{2,1,0:T(8,128)(2,1)S(1)} all-to-all(bf16[4,384,384]{2,1,0:T(8,128)(2,1)S(1)} %project.3), channel_id=1, replica_groups={{0,2,4,6},{1,3,5,7},{8,10,12,14},{9,11,13,15},{16,18,20,22},{17,19,21,2..., dimensions={0} | all-to-all | bytes 2359296 | tf_op jit(solution)/shard_map/all_to_all | solution.py:418
  178.1 1.5 join.3
  (43 shorter events, 6.1 us)
Async XLA Ops:
  0.0 1.1 copy-start
  3.0 7.3 %copy-start.2 = (bf16[256,3072]{1,0:T(8,128)(2,1)S(1)}, bf16[256,3072]{1,0:T(8,128)(2,1)}, u32[]{:S(2)}) copy-start(bf16[256,3072]{1,0:T(8,128)(2,1)} %refs_0_.1) | copy-start | bytes 4718596
  3.0 7.3 %copy-start.3 = (bf16[256,3072]{1,0:T(8,128)(2,1)S(1)}, bf16[256,3072]{1,0:T(8,128)(2,1)}, u32[]{:S(2)}) copy-start(bf16[256,3072]{1,0:T(8,128)(2,1)} %refs_1_.1) | copy-start | bytes 4718596
  3.0 42.9 %all-to-all-start = ((bf16[8,392,384]{2,1,0:T(8,128)(2,1)}), bf16[8,392,384]{2,1,0:T(8,128)(2,1)}, u32[]{:S(2)}, u32[]{:S(2)}) async-start(bf16[8,392,384]{2,1,0:T(8,128)(2,1)} %broadcast_in_dim.4), calls=%async_computation | async-start | bytes 4816896 | tf_op jit(solution)/shard_map/all_to_all | solution.py:400
  10.2 35.7 %copy-start.8 = (f32[3,3072]{1,0:T(4,128)S(1)}, f32[3,3072]{1,0:T(4,128)}, u32[]{:S(2)}) copy-start(f32[3,3072]{1,0:T(4,128)} %mod_ref.5) | copy-start | bytes 110596
  12.2 0.9 copy-start.4
  13.1 0.9 copy-start.6
  14.0 0.8 copy-start.10
  14.7 36.9 %collective-permute-start.2 = (bf16[4,128,384]{2,1,0:T(8,128)(2,1)}, bf16[4,128,384]{2,1,0:T(8,128)(2,1)S(1)}, u32[]{:S(2)}, u32[]{:S(2)}) collective-permute-start(bf16[4,128,384]{2,1,0:T(8,128)(2,1)} %get-tuple-element.20), channel_id=1, source_target_pairs={{0,1},{1,0},{2,3},{3,2},{4,5},{5,4},{6,7},{7,6},{8,9},{9,8},{10,11... | collective-permute-start | bytes 1179656 | tf_op jit(solution)/shard_map/ppermute | solution.py:409
  45.9 6.2 %copy-start.11 = (s32[16,6,6]{0,2,1:T(8,128)S(1)}, s32[16,6,6]{0,2,1:T(8,128)}, u32[]{:S(2)}) copy-start(s32[16,6,6]{0,2,1:T(8,128)} %param.9) | copy-start | bytes 6916
  46.0 17.6 %copy-start.7 = (bf16[4,256,384]{2,1,0:T(8,128)(2,1)S(1)}, bf16[4,256,384]{2,1,0:T(8,128)(2,1)}, u32[]{:S(2)}) copy-start(bf16[4,256,384]{2,1,0:T(8,128)(2,1)} %copy-done.6) | copy-start | bytes 2359300
  51.5 1.8 %collective-permute-start = (bf16[2,384,256]{2,1,0:T(8,128)(2,1)S(1)}, bf16[2,384,256]{2,1,0:T(8,128)(2,1)S(1)}, u32[]{:S(2)}, u32[]{:S(2)}) collective-permute-start(bf16[2,384,256]{2,1,0:T(8,128)(2,1)S(1)} %get-tuple-element.18.own_ref), channel_id=1, source_target_pairs={{0,8},{8,0},{16,24},{24,16},{32,40},{40,32},{48,56},{56,48},{64,72... | collective-permute-start | bytes 1179656 | tf_op jit(solution)/shard_map/ppermute | solution.py:406
  51.6 5.1 %collective-permute-start.3 = (bf16[4,128,384]{2,1,0:T(8,128)(2,1)S(1)}, bf16[4,128,384]{2,1,0:T(8,128)(2,1)S(1)}, u32[]{:S(2)}, u32[]{:S(2)}) collective-permute-start(bf16[4,128,384]{2,1,0:T(8,128)(2,1)S(1)} %collective-permute-done.2.half_ref), channel_id=1, source_target_pairs={{0,8},{8,0},{16,24},{24,16},{32,40},{40,32},{48,56},{56,48},{64,72... | collective-permute-start | bytes 1179656 | tf_op jit(solution)/shard_map/ppermute | solution.py:406
  55.1 8.5 %collective-permute-start.1 = (bf16[384,256]{1,0:T(8,128)(2,1)S(1)}, bf16[384,256]{1,0:T(8,128)(2,1)S(1)}, u32[]{:S(2)}, u32[]{:S(2)}) collective-permute-start(bf16[384,256]{1,0:T(8,128)(2,1)S(1)} %space_attend.1.own_ref), channel_id=1, source_target_pairs={{0,1},{1,0},{2,3},{3,2},{4,5},{5,4},{6,7},{7,6},{8,9},{9,8},{10,11... | collective-permute-start | bytes 589832 | tf_op jit(solution)/shard_map/ppermute | solution.py:409
  63.6 22.4 %copy-start.1 = (f32[1,384,384]{2,1,0:T(8,128)S(1)}, f32[1,384,384]{2,1,0:T(8,128)}, u32[]{:S(2)}) copy-start(f32[1,384,384]{2,1,0:T(8,128)} %param.8) | copy-start | bytes 1769476
  63.6 74.5 %slice-start = ((s8[4718592]{0:T(1024)(128)(4,1)}), s8[524288]{0:T(1024)(128)(4,1)S(1)}, s32[]{:S(2)}) async-start(s8[4718592]{0:T(1024)(128)(4,1)} %bitcast.11), calls=%async_computation.6 | async-start | bytes 1048576
  66.2 19.7 %all-to-all-start.1 = ((bf16[4,384,384]{2,1,0:T(8,128)(2,1)}), bf16[4,384,384]{2,1,0:T(8,128)(2,1)S(1)}, u32[]{:S(2)}, u32[]{:S(2)}) async-start(bf16[4,384,384]{2,1,0:T(8,128)(2,1)} %project.2), calls=%async_computation.1 | async-start | bytes 2359296 | tf_op jit(solution)/shard_map/all_to_all | solution.py:418
  69.8 17.0 %collective-permute-start.4 = (bf16[4,128,384]{2,1,0:T(8,128)(2,1)}, bf16[4,128,384]{2,1,0:T(8,128)(2,1)S(1)}, u32[]{:S(2)}, u32[]{:S(2)}) collective-permute-start(bf16[4,128,384]{2,1,0:T(8,128)(2,1)} %copy-done.10), channel_id=1, source_target_pairs={{0,1},{1,0},{2,3},{3,2},{4,5},{5,4},{6,7},{7,6},{8,9},{9,8},{10,11... | collective-permute-start | bytes 1179656 | tf_op jit(solution)/shard_map/ppermute | solution.py:409
  104.7 33.4 %slice-start.1 = ((s8[4718592]{0:T(1024)(128)(4,1)}), s8[4194304]{0:T(1024)(128)(4,1)S(1)}, s32[]{:S(2)}) async-start(s8[4718592]{0:T(1024)(128)(4,1)} %bitcast.11), calls=%async_computation.7 | async-start | bytes 8388608
  105.2 32.9 %copy-start.9 = (f32[3,3072]{1,0:T(4,128)S(1)}, f32[3,3072]{1,0:T(4,128)}, u32[]{:S(2)}) copy-start(f32[3,3072]{1,0:T(4,128)} %mod_ref.7) | copy-start | bytes 110596
  138.1 24.4 %copy-start.5 = (bf16[4,256,384]{2,1,0:T(8,128)(2,1)S(1)}, bf16[4,256,384]{2,1,0:T(8,128)(2,1)}, u32[]{:S(2)}) copy-start(bf16[4,256,384]{2,1,0:T(8,128)(2,1)} %copy-done.4) | copy-start | bytes 2359300
  141.9 13.4 %all-to-all-start.4 = ((bf16[16,24,256]{2,1,0:T(8,128)(2,1)}), bf16[16,24,256]{2,1,0:T(8,128)(2,1)S(1)}, u32[]{:S(2)}, u32[]{:S(2)}) async-start(bf16[16,24,256]{2,1,0:T(8,128)(2,1)} %bitcast.8), calls=%async_computation.4 | async-start | bytes 393216 | tf_op jit(solution)/shard_map/all_to_all | solution.py:394
  146.7 9.9 %collective-permute-start.6 = (bf16[4,128,384]{2,1,0:T(8,128)(2,1)S(1)}, bf16[4,128,384]{2,1,0:T(8,128)(2,1)S(1)}, u32[]{:S(2)}, u32[]{:S(2)}) collective-permute-start(bf16[4,128,384]{2,1,0:T(8,128)(2,1)S(1)} %collective-permute-done.4.half_ref), channel_id=1, source_target_pairs={{0,8},{8,0},{16,24},{24,16},{32,40},{40,32},{48,56},{56,48},{64,72... | collective-permute-start | bytes 1179656 | tf_op jit(solution)/shard_map/ppermute | solution.py:406
  155.3 7.2 %collective-permute-start.5 = (bf16[384,256]{1,0:T(8,128)(2,1)S(1)}, bf16[384,256]{1,0:T(8,128)(2,1)S(1)}, u32[]{:S(2)}, u32[]{:S(2)}) collective-permute-start(bf16[384,256]{1,0:T(8,128)(2,1)S(1)} %bitcast.17), channel_id=1, source_target_pairs={{0,1},{1,0},{2,3},{3,2},{4,5},{5,4},{6,7},{7,6},{8,9},{9,8},{10,11... | collective-permute-start | bytes 589832 | tf_op jit(solution)/shard_map/ppermute | solution.py:409

commit v11 on v10

--- a/solution.py
+++ b/solution.py
@@ -13,7 +13,7 @@
 EPS = 1e-06
 SCALE = 1.0 / math.sqrt(HD)
 VMEM_LIMIT = 24 * 1024 * 1024
-HELD_LIMIT = 52 * 1024 * 1024
+HELD_LIMIT = 50 * 1024 * 1024
 ROW_TILE = 192
 F32 = jnp.float32
 BF16 = jnp.bfloat16

time: 180 us -> 183 us (1.017)
  local copies, waits for them, and re-layouts: 5.78 us -> 9.6 us
    unnamed x29, local copies, waits for them, and re-layouts: 3.78 us -> 7.6 us
    all_to_all x1, waiting for transfers between devices: 27.7 us -> 25.7 us  [across_parts(): lax.all_to_all(values, 'fsdp', split_axis=0, concat_axis=0, tiled=True)]
where the time goes in v11:
time: 183 us; the launch traced here: 182 us
  blocking collectives  64.8 us (35%)
  waiting for transfers between devices  62.8 us (34%)
  starting transfers between devices  24 us (13%)
  Pallas kernels  20.6 us (11%)
  local copies, waits for them, and re-layouts  9.6 us (5%)
    all_to_all x1, blocking collectives, across_parts(): lax.all_to_all(values, 'fsdp', split_axis=0, concat_axis=0, tiled=True)  32.8 us
    all_to_all x1, waiting for transfers between devices, across_parts(): lax.all_to_all(values, 'fsdp', split_axis=0, concat_axis=0, tiled=True)  25.7 us
    all_to_all x1, blocking collectives, across_frames(): lax.all_to_all(values.reshape(frames, rows // frames, -1), 'seq', split_a...  18 us
    all_to_all x1, waiting for transfers between devices, across_x(): lax.all_to_all(values, 'fsdp', split_axis=0, concat_axis=0, tiled=True, a...  14.5 us
    all_to_all x1, blocking collectives, across_x(): lax.all_to_all(values, 'fsdp', split_axis=0, concat_axis=0, tiled=True, a...  14 us
    ppermute x4, waiting for transfers between devices, from_other_side(): return lax.ppermute(values, 'fsdp', [(i, i ^ 1) for i in range(parts)])  12.8 us
    all_to_all x1, waiting for transfers between devices, across_frames(): lax.all_to_all(values.reshape(frames, rows // frames, -1), 'seq', split_a...  8.6 us
    ppermute x4, starting transfers between devices, from_other_side(): return lax.ppermute(values, 'fsdp', [(i, i ^ 1) for i in range(parts)])  8.08 us
  transfers between devices with their start and end apart: 10, of which 6 were waited for; matrix products, arithmetic and copies ran while one was open for 0% of the time, Pallas kernels for 5%

profile of v11, /device:TPU:32, one launch (start us, length us, event | category | flops | bytes accessed | tf_op | source)
XLA Modules:
  0.0 182.0 jit_solution(17552549605864827600)
XLA Ops:
  1.4 1.7 broadcast_in_dim.4
  3.0 6.9 %all-to-all-start = ((bf16[8,392,384]{2,1,0:T(8,128)(2,1)}), bf16[8,392,384]{2,1,0:T(8,128)(2,1)S(1)}, u32[]{:S(2)}, u32[]{:S(2)}) async-start(bf16[8,392,384]{2,1,0:T(8,128)(2,1)} %broadcast_in_dim.4), calls=%async_computation | async-start | bytes 4816896 | tf_op jit(solution)/shard_map/all_to_all | solution.py:400
  10.1 1.4 copy-done.2
  11.5 1.4 copy-done.3
  12.9 1.8 lend.1
  16.3 3.5 %collective-permute-start.2 = (bf16[4,128,384]{2,1,0:T(8,128)(2,1)}, bf16[4,128,384]{2,1,0:T(8,128)(2,1)}, u32[]{:S(2)}, u32[]{:S(2)}) collective-permute-start(bf16[4,128,384]{2,1,0:T(8,128)(2,1)} %get-tuple-element.20), channel_id=1, source_target_pairs={{0,1},{1,0},{2,3},{3,2},{4,5},{5,4},{6,7},{7,6},{8,9},{9,8},{10,11... | collective-permute-start | bytes 1179656 | tf_op jit(solution)/shard_map/ppermute | solution.py:409
  19.8 25.7 %all-to-all-done.parts_ref = bf16[8,392,384]{2,1,0:T(8,128)(2,1)S(1)} async-done(((bf16[8,392,384]{2,1,0:T(8,128)(2,1)}), bf16[8,392,384]{2,1,0:T(8,128)(2,1)S(1)}, u32[]{:S(2)}, u32[]{:S(2)}) %all-to-all-start) | async-done | bytes 2408480 | tf_op jit(solution)/shard_map/all_to_all | solution.py:400
  45.6 4.5 %space_in.1 = (bf16[384,256]{1,0:T(8,128)(2,1)S(1)}, bf16[2,384,256]{2,1,0:T(8,128)(2,1)}) custom-call(bf16[8,392,384]{2,1,0:T(8,128)(2,1)S(1)} %all-to-all-done.parts_ref, f32[3,3072]{1,0:T(4,128)S(1)} %copy-done.8, bf16[3,3072,256]{2,1,0:T(8,128)(2,1)} %bitcast.20), custom_call_target="tpu_custom_call" | custom-call | flops 1811939328 | bytes 7127040 | tf_op jit(solution)/shard_map/space_in/pallas_call | solution.py:145
  52.1 2.2 %space_attend.1.own_ref = bf16[384,256]{1,0:T(8,128)(2,1)S(1)} custom-call(s32[3]{0:T(128)S(1)} %pad_add_fusion.where_ref, s32[576]{0:T(1024)S(1)} %reshape.23.mask_ref, bf16[384,256]{1,0:T(8,128)(2,1)S(1)} %get-tuple-element.17.q_ref, bf16[2,384,256]{2,1,0:T(8,128)(2,1)} %get-tuple-element.18.own_ref, bf16[2,384,256]{2,1,0:T(8,128)(2,1)S(1)} %collective-permute-done.other_ref), custom_call_target="tpu_custom_call" | custom-call | flops 301989888 | bytes 1179648 | tf_op jit(solution)/shard_map/space_attend/pallas_call | solution.py:219
  54.3 1.7 collective-permute-start.1
  56.0 6.9 %collective-permute-done.1.partner_ref = bf16[384,256]{1,0:T(8,128)(2,1)S(1)} collective-permute-done((bf16[384,256]{1,0:T(8,128)(2,1)S(1)}, bf16[384,256]{1,0:T(8,128)(2,1)S(1)}, u32[]{:S(2)}, u32[]{:S(2)}) %collective-permute-start.1) | collective-permute-done | bytes 196640 | tf_op jit(solution)/shard_map/ppermute | solution.py:409
  64.0 3.2 %project.2 = bf16[4,384,384]{2,1,0:T(8,128)(2,1)} custom-call(s32[3]{0:T(128)S(1)} %pad_add_fusion.where_ref, bf16[384,256]{1,0:T(8,128)(2,1)S(1)} %space_attend.1.own_ref, bf16[384,256]{1,0:T(8,128)(2,1)S(1)} %collective-permute-done.1.partner_ref, bf16[4,256,384]{2,1,0:T(8,128)(2,1)S(1)} %copy-done.5, ...), custom_call_target="tpu_custom_call" | custom-call | flops 603979776 | bytes 2752512 | tf_op jit(solution)/shard_map/project/pallas_call | solution.py:294
  67.2 3.5 %all-to-all-start.1 = ((bf16[4,384,384]{2,1,0:T(8,128)(2,1)}), bf16[4,384,384]{2,1,0:T(8,128)(2,1)S(1)}, u32[]{:S(2)}, u32[]{:S(2)}) async-start(bf16[4,384,384]{2,1,0:T(8,128)(2,1)} %project.2), calls=%async_computation.1 | async-start | bytes 2359296 | tf_op jit(solution)/shard_map/all_to_all | solution.py:418
  70.7 1.7 collective-permute-start.4
  72.4 14.5 %all-to-all-done.1.parts_ref = bf16[4,384,384]{2,1,0:T(8,128)(2,1)S(1)} async-done(((bf16[4,384,384]{2,1,0:T(8,128)(2,1)}), bf16[4,384,384]{2,1,0:T(8,128)(2,1)S(1)}, u32[]{:S(2)}, u32[]{:S(2)}) %all-to-all-start.1) | async-done | bytes 1179680 | tf_op jit(solution)/shard_map/all_to_all | solution.py:418
  88.5 18.0 %all_to_all.30 = bf16[16,24,384]{2,1,0:T(8,128)(2,1)S(1)} all-to-all(bf16[16,24,384]{2,1,0:T(8,128)(2,1)S(1)} %bitcast.19), channel_id=1, replica_groups={{0,16,32,48,64,80,96,112,128,144,160,176,192,208,224,240},{8,24,40,56,7..., dimensions={0} | all-to-all | bytes 589824 | tf_op jit(solution)/shard_map/all_to_all | solution.py:394
  107.0 32.8 %all_to_all.31.parts_ref = bf16[8,392,384]{2,1,0:T(8,128)(2,1)S(1)} all-to-all(bf16[8,392,384]{2,1,0:T(8,128)(2,1)S(1)} %broadcast_in_dim.5), channel_id=1, replica_groups=mesh['seq'=32,'fsdp'=8] {'fsdp'}, dimensions={0} | all-to-all | bytes 4816896 | tf_op jit(solution)/shard_map/all_to_all | solution.py:400
  139.9 3.8 %time_layer.1 = bf16[384,256]{1,0:T(8,128)(2,1)} custom-call(bf16[8,392,384]{2,1,0:T(8,128)(2,1)S(1)} %all_to_all.31.parts_ref, f32[3,3072]{1,0:T(4,128)S(1)} %copy-done.9, bf16[3,3072,256]{2,1,0:T(8,128)(2,1)S(1)} %bitcast.13), custom_call_target="tpu_custom_call" | custom-call | flops 1811939328 | bytes 7127040 | tf_op jit(solution)/shard_map/time_layer/pallas_call | solution.py:364
  143.7 4.9 %all-to-all-start.4 = ((bf16[16,24,256]{2,1,0:T(8,128)(2,1)}), bf16[16,24,256]{2,1,0:T(8,128)(2,1)S(1)}, u32[]{:S(2)}, u32[]{:S(2)}) async-start(bf16[16,24,256]{2,1,0:T(8,128)(2,1)} %bitcast.8), calls=%async_computation.4 | async-start | bytes 393216 | tf_op jit(solution)/shard_map/all_to_all | solution.py:394
  148.6 8.6 %all-to-all-done.4 = bf16[16,24,256]{2,1,0:T(8,128)(2,1)S(1)} async-done(((bf16[16,24,256]{2,1,0:T(8,128)(2,1)}), bf16[16,24,256]{2,1,0:T(8,128)(2,1)S(1)}, u32[]{:S(2)}, u32[]{:S(2)}) %all-to-all-start.4) | async-done | bytes 196640 | tf_op jit(solution)/shard_map/all_to_all | solution.py:394
  158.4 5.9 %collective-permute-done.5.partner_ref = bf16[384,256]{1,0:T(8,128)(2,1)S(1)} collective-permute-done((bf16[384,256]{1,0:T(8,128)(2,1)S(1)}, bf16[384,256]{1,0:T(8,128)(2,1)S(1)}, u32[]{:S(2)}, u32[]{:S(2)}) %collective-permute-start.5) | collective-permute-done | bytes 196640 | tf_op jit(solution)/shard_map/ppermute | solution.py:409
  164.4 2.1 %project.3 = bf16[4,384,384]{2,1,0:T(8,128)(2,1)S(1)} custom-call(s32[3]{0:T(128)S(1)} %pad_add_fusion.where_ref, bf16[384,256]{1,0:T(8,128)(2,1)S(1)} %bitcast.18, bf16[384,256]{1,0:T(8,128)(2,1)S(1)} %collective-permute-done.5.partner_ref, bf16[4,256,384]{2,1,0:T(8,128)(2,1)S(1)} %get-tuple-element.26.weight_ref, ...), custom_call_target="tpu_custom_call" | custom-call | flops 603979776 | bytes 2752512 | tf_op jit(solution)/shard_map/project/pallas_call | solution.py:294
  166.5 14.0 %all_to_all.32.parts_ref = bf16[4,384,384]{2,1,0:T(8,128)(2,1)S(1)} all-to-all(bf16[4,384,384]{2,1,0:T(8,128)(2,1)S(1)} %project.3), channel_id=1, replica_groups={{0,2,4,6},{1,3,5,7},{8,10,12,14},{9,11,13,15},{16,18,20,22},{17,19,21,2..., dimensions={0} | all-to-all | bytes 2359296 | tf_op jit(solution)/shard_map/all_to_all | solution.py:418
  180.5 1.5 join.3
  (43 shorter events, 9.6 us)
Async XLA Ops:
  0.0 1.1 copy-start
  3.0 42.5 %all-to-all-start = ((bf16[8,392,384]{2,1,0:T(8,128)(2,1)}), bf16[8,392,384]{2,1,0:T(8,128)(2,1)S(1)}, u32[]{:S(2)}, u32[]{:S(2)}) async-start(bf16[8,392,384]{2,1,0:T(8,128)(2,1)} %broadcast_in_dim.4), calls=%async_computation | async-start | bytes 4816896 | tf_op jit(solution)/shard_map/all_to_all | solution.py:400
  10.0 35.6 %copy-start.8 = (f32[3,3072]{1,0:T(4,128)S(1)}, f32[3,3072]{1,0:T(4,128)}, u32[]{:S(2)}) copy-start(f32[3,3072]{1,0:T(4,128)} %mod_ref.5) | copy-start | bytes 110596
  10.1 1.4 copy-start.2
  11.5 1.4 copy-start.3
  14.7 0.9 copy-start.4
  15.6 0.8 copy-start.10
  16.3 33.9 %collective-permute-start.2 = (bf16[4,128,384]{2,1,0:T(8,128)(2,1)}, bf16[4,128,384]{2,1,0:T(8,128)(2,1)}, u32[]{:S(2)}, u32[]{:S(2)}) collective-permute-start(bf16[4,128,384]{2,1,0:T(8,128)(2,1)} %get-tuple-element.20), channel_id=1, source_target_pairs={{0,1},{1,0},{2,3},{3,2},{4,5},{5,4},{6,7},{7,6},{8,9},{9,8},{10,11... | collective-permute-start | bytes 1179656 | tf_op jit(solution)/shard_map/ppermute | solution.py:409
  45.6 5.2 %copy-start.11 = (s32[16,6,6]{0,2,1:T(8,128)S(1)}, s32[16,6,6]{0,2,1:T(8,128)}, u32[]{:S(2)}) copy-start(s32[16,6,6]{0,2,1:T(8,128)} %param.9) | copy-start | bytes 6916
  50.1 2.0 %collective-permute-start = (bf16[2,384,256]{2,1,0:T(8,128)(2,1)}, bf16[2,384,256]{2,1,0:T(8,128)(2,1)S(1)}, u32[]{:S(2)}, u32[]{:S(2)}) collective-permute-start(bf16[2,384,256]{2,1,0:T(8,128)(2,1)} %get-tuple-element.18.own_ref), channel_id=1, source_target_pairs={{0,8},{8,0},{16,24},{24,16},{32,40},{40,32},{48,56},{56,48},{64,72... | collective-permute-start | bytes 1179656 | tf_op jit(solution)/shard_map/ppermute | solution.py:406
  50.2 5.8 %collective-permute-start.3 = (bf16[4,128,384]{2,1,0:T(8,128)(2,1)}, bf16[4,128,384]{2,1,0:T(8,128)(2,1)S(1)}, u32[]{:S(2)}, u32[]{:S(2)}) collective-permute-start(bf16[4,128,384]{2,1,0:T(8,128)(2,1)} %collective-permute-done.2.half_ref), channel_id=1, source_target_pairs={{0,8},{8,0},{16,24},{24,16},{32,40},{40,32},{48,56},{56,48},{64,72... | collective-permute-start | bytes 1179656 | tf_op jit(solution)/shard_map/ppermute | solution.py:406
  54.3 8.5 %collective-permute-start.1 = (bf16[384,256]{1,0:T(8,128)(2,1)S(1)}, bf16[384,256]{1,0:T(8,128)(2,1)S(1)}, u32[]{:S(2)}, u32[]{:S(2)}) collective-permute-start(bf16[384,256]{1,0:T(8,128)(2,1)S(1)} %space_attend.1.own_ref), channel_id=1, source_target_pairs={{0,1},{1,0},{2,3},{3,2},{4,5},{5,4},{6,7},{7,6},{8,9},{9,8},{10,11... | collective-permute-start | bytes 589832 | tf_op jit(solution)/shard_map/ppermute | solution.py:409
  62.9 1.1 copy-start.5
  64.0 22.9 %copy-start.1 = (f32[1,384,384]{2,1,0:T(8,128)S(1)}, f32[1,384,384]{2,1,0:T(8,128)}, u32[]{:S(2)}) copy-start(f32[1,384,384]{2,1,0:T(8,128)} %param.8) | copy-start | bytes 1769476
  64.0 75.8 %slice-start = ((s8[4718592]{0:T(1024)(128)(4,1)}), s8[524288]{0:T(1024)(128)(4,1)S(1)}, s32[]{:S(2)}) async-start(s8[4718592]{0:T(1024)(128)(4,1)} %bitcast.11), calls=%async_computation.6 | async-start | bytes 1048576
  67.2 19.7 %all-to-all-start.1 = ((bf16[4,384,384]{2,1,0:T(8,128)(2,1)}), bf16[4,384,384]{2,1,0:T(8,128)(2,1)S(1)}, u32[]{:S(2)}, u32[]{:S(2)}) async-start(bf16[4,384,384]{2,1,0:T(8,128)(2,1)} %project.2), calls=%async_computation.1 | async-start | bytes 2359296 | tf_op jit(solution)/shard_map/all_to_all | solution.py:418
  70.7 17.8 %collective-permute-start.4 = (bf16[4,128,384]{2,1,0:T(8,128)(2,1)}, bf16[4,128,384]{2,1,0:T(8,128)(2,1)}, u32[]{:S(2)}, u32[]{:S(2)}) collective-permute-start(bf16[4,128,384]{2,1,0:T(8,128)(2,1)} %copy-done.10), channel_id=1, source_target_pairs={{0,1},{1,0},{2,3},{3,2},{4,5},{5,4},{6,7},{7,6},{8,9},{9,8},{10,11... | collective-permute-start | bytes 1179656 | tf_op jit(solution)/shard_map/ppermute | solution.py:409
  87.7 0.8 copy-start.6
  106.4 33.4 %slice-start.1 = ((s8[4718592]{0:T(1024)(128)(4,1)}), s8[4194304]{0:T(1024)(128)(4,1)S(1)}, s32[]{:S(2)}) async-start(s8[4718592]{0:T(1024)(128)(4,1)} %bitcast.11), calls=%async_computation.7 | async-start | bytes 8388608
  107.0 32.8 %copy-start.9 = (f32[3,3072]{1,0:T(4,128)S(1)}, f32[3,3072]{1,0:T(4,128)}, u32[]{:S(2)}) copy-start(f32[3,3072]{1,0:T(4,128)} %mod_ref.7) | copy-start | bytes 110596
  143.7 13.5 %all-to-all-start.4 = ((bf16[16,24,256]{2,1,0:T(8,128)(2,1)}), bf16[16,24,256]{2,1,0:T(8,128)(2,1)S(1)}, u32[]{:S(2)}, u32[]{:S(2)}) async-start(bf16[16,24,256]{2,1,0:T(8,128)(2,1)} %bitcast.8), calls=%async_computation.4 | async-start | bytes 393216 | tf_op jit(solution)/shard_map/all_to_all | solution.py:394
  148.6 9.8 %collective-permute-start.6 = (bf16[4,128,384]{2,1,0:T(8,128)(2,1)}, bf16[4,128,384]{2,1,0:T(8,128)(2,1)S(1)}, u32[]{:S(2)}, u32[]{:S(2)}) collective-permute-start(bf16[4,128,384]{2,1,0:T(8,128)(2,1)} %collective-permute-done.4.half_ref), channel_id=1, source_target_pairs={{0,8},{8,0},{16,24},{24,16},{32,40},{40,32},{48,56},{56,48},{64,72... | collective-permute-start | bytes 1179656 | tf_op jit(solution)/shard_map/ppermute | solution.py:406
  157.2 7.2 %collective-permute-start.5 = (bf16[384,256]{1,0:T(8,128)(2,1)S(1)}, bf16[384,256]{1,0:T(8,128)(2,1)S(1)}, u32[]{:S(2)}, u32[]{:S(2)}) collective-permute-start(bf16[384,256]{1,0:T(8,128)(2,1)S(1)} %bitcast.17), channel_id=1, source_target_pairs={{0,1},{1,0},{2,3},{3,2},{4,5},{5,4},{6,7},{7,6},{8,9},{9,8},{10,11... | collective-permute-start | bytes 589832 | tf_op jit(solution)/shard_map/ppermute | solution.py:409
  164.4 16.2 %copy-start.7 = (f32[384,384]{1,0:T(8,128)S(1)}, f32[384,384]{1,0:T(8,128)}, u32[]{:S(2)}) copy-start(f32[384,384]{1,0:T(8,128)} %copy-done.6) | copy-start | bytes 1769476
